TPU v7x, 128 devices: a whole 4x4x4 slice. The times are simulated.
128 devices in a mesh: rows: 16 (over z, x_hi, core), cols: 8 (over y, x_lo).
Axes of the slice: x: 4 (x_hi: 2, x_lo: 2; x = x_hi * 2 + x_lo), y: 4, z: 4, core: 2. Of those that a mesh axis runs over, the one named last changes fastest.
Arguments:
- gradient: float32 [12288, 28672], P('rows', 'cols'), may hold values from -6 to 6
- basis: float32 [16, 28672, 128], P('rows', 'cols'), may hold values from -0.03125 to 0.03125
- panel_index: int32 [4], replicated, may hold values from 0 to 15, as said below
- input_eigen: float32 [8192], replicated, may hold values from 0.1 to 3
- output_eigen: float32 [28672], replicated, may hold values from 0.1 to 3
- input_pick: int32 [4, 128], replicated, may hold values from 0 to 8191
- output_pick: int32 [4, 128], replicated, may hold values from 0 to 28671
Outputs:
- preconditioned: float32 [12288, 28672], P('rows', 'cols')
Inputs may be any that keep to these rules, and one draw needn't show every extreme that they name: `panel_index`: the 4 entries are distinct.
All inputs are finite; a program needn't handle non-finite values.
Results may differ from a plain program's by a relative error of at most 0.0001.
Values sent between devices are 32-bit elements; how exact they have to be, the bound alone decides.
No kernel may reach another device: no remote copies, remote signals or barrier semaphores. Data moves between devices by JAX's collectives and lax.ppermute only.
A program may use at most 128 MiB of HBM per device.

v0:
```python
import jax
import jax.numpy as jnp
from jax import lax
from jax.experimental import pallas as pl
from jax.experimental.pallas import tpu as pltpu
from jax.sharding import PartitionSpec as P


NSEL = 4
PANEL = 128
PAIR = 2 * PANEL
PLANES = 4
COLS = 8
F32 = jnp.float32


CORE = [(r, r ^ 1) for r in range(16)]
XPAIR = [(r, r ^ 2) for r in range(16)]
RING = [(r, ((r // 4 + (1 if r % 2 == 0 else 3)) % 4) * 4 + r % 4) for r in range(16)]

VM = pl.BlockSpec()
SM = pl.BlockSpec(memory_space=pltpu.SMEM)
HBM = pl.BlockSpec(memory_space=pltpu.HBM)


def stay(value):
    return pltpu.with_memory_space_constraint(value, pltpu.HBM)


def ordered(first, mine, other):
    low = jnp.where(first, mine, other)
    high = jnp.where(first, other, mine)
    return jnp.concatenate([low, high], axis=0)


def rotate_body(at_ref, *refs):
    for i in range(PLANES):
        refs[PLANES + i][...] = refs[i][...]


def rotate(at, gradient, tile=96):
    rows, width = gradient.shape
    quarter = width // PLANES
    spec = lambda i: pl.BlockSpec((tile, quarter), lambda r, at_ref: (r, at_ref[i]))
    return pl.pallas_call(
        rotate_body,
        grid_spec=pltpu.PrefetchScalarGridSpec(
            num_scalar_prefetch=1,
            grid=(rows // tile,),
            in_specs=[spec(i) for i in range(PLANES)],
            out_specs=[pl.BlockSpec((tile, quarter), lambda r, at_ref: (r, 0))] * PLANES,
        ),
        out_shape=[jax.ShapeDtypeStruct((rows, quarter), F32)] * PLANES,
        compiler_params=pltpu.CompilerParams(vmem_limit_bytes=16 << 20),
        cost_estimate=pl.CostEstimate(flops=1, bytes_accessed=rows * width * 8, transcendentals=0),
        name="rotate",
    )(at, *[stay(gradient)] * PLANES)


def pick_body(at_ref, pieces_ref, a_ref, b_ref, give_ref):
    core = at_ref[NSEL]
    a_ref[...] = pieces_ref[at_ref[2 * core]]
    b_ref[...] = pieces_ref[at_ref[2 * core + 1]]
    give_ref[0] = pieces_ref[at_ref[2 - 2 * core]]
    give_ref[1] = pieces_ref[at_ref[3 - 2 * core]]


def pick(at, pieces):
    one = jax.ShapeDtypeStruct(pieces.shape[1:], F32)
    two = jax.ShapeDtypeStruct((2, *pieces.shape[1:]), F32)
    return pl.pallas_call(
        pick_body,
        out_shape=[one, one, two],
        in_specs=[SM, VM],
        out_specs=[VM] * 3,
        compiler_params=pltpu.CompilerParams(vmem_limit_bytes=8 << 20),
        cost_estimate=pl.CostEstimate(flops=1, bytes_accessed=pieces.size, transcendentals=0),
        name="pick",
    )(at, pieces)


def place_body(at_ref, *refs):
    v_ref, sems = refs[-2:]
    quarter = refs[0].shape[0]
    moves = []
    for side in range(2):
        for step in range(PLANES):
            rows = pl.ds(pl.multiple_of(at_ref[side * PLANES + step] * quarter, 128), quarter)
            lanes = pl.ds(side * PAIR, PAIR)
            moves.append(pltpu.make_async_copy(refs[side * PLANES + step], v_ref.at[rows, lanes], sems.at[side, step]))
    for move in moves:
        move.start()
    for move in moves:
        move.wait()


def place(at, own, oth):
    quarter = own[0].shape[0]
    return pl.pallas_call(
        place_body,
        out_shape=pltpu.HBM((PLANES * quarter, 2 * PAIR), F32),
        in_specs=[SM] + [VM] * (2 * PLANES),
        out_specs=HBM,
        scratch_shapes=[pltpu.SemaphoreType.DMA((2, PLANES))],
        compiler_params=pltpu.CompilerParams(vmem_limit_bytes=8 << 20),
        cost_estimate=pl.CostEstimate(flops=1, bytes_accessed=quarter * PAIR * 64, transcendentals=0),
        name="place",
    )(at, *own, *oth)


def dot(a, b):
    return jnp.dot(a, b, precision=lax.Precision.HIGH, preferred_element_type=F32)


def shards(gradient, basis, panel_index, input_eigen, output_eigen, input_pick, output_pick):
    rows, _ = gradient.shape
    me = lax.axis_index("rows")
    z, x, core = me // 4, (me // 2) % 2, me % 2
    even = core == 0
    way = jnp.where(even, 1, -1)

    damped = (input_eigen[input_pick] * output_eigen[output_pick] + 0.05).reshape(-1)
    damped = jnp.where(even, damped, jnp.roll(damped, PAIR))

    pieces = lax.all_to_all(basis.reshape(16, -1, PANEL), "rows", 0, 0)
    at = jnp.arange(PLANES, dtype=jnp.int32) * way.astype(jnp.int32)
    at = jnp.concatenate([(z - at + 4) % 4, (z + at + 4) % 4])
    pieces, *g = lax.optimization_barrier((pieces, *rotate(at, gradient)))
    mine_a, mine_b, give = pick(jnp.append(panel_index, core).astype(jnp.int32), pieces)
    got = lax.ppermute(give, "rows", CORE)
    halves = [ordered(even, mine_a, got[0]), ordered(even, mine_b, got[1])]
    own = [[], []]
    for c, half in enumerate(halves):
        own[c].append(ordered(x == 0, half, lax.ppermute(half, "rows", XPAIR)))

    v_own, v_oth, total, waiting = [], [], None, None

    def product(step, own, oth, total):
        mine, other = jnp.concatenate(own, axis=1), jnp.concatenate(oth, axis=1)
        v_own.append(mine)
        v_oth.append(other)
        mine, other = dot(g[step], mine), dot(g[-step % PLANES], other)
        return (mine, other) if total is None else (total[0] + mine, total[1] + other)

    for step in range(PLANES):
        oth = [None, None]
        for c in range(2):
            held = own[c][step]
            if c == 0 and waiting is not None:
                last_oth = waiting[2]
                if total is not None:
                    held, last_oth[0], *total = lax.optimization_barrier((held, last_oth[0], *total))
                else:
                    held, last_oth[0] = lax.optimization_barrier((held, last_oth[0]))
            if step < PLANES - 1:
                own[c].append(lax.ppermute(held, "rows", RING))
            oth[c] = lax.ppermute(held, "rows", CORE)
        if waiting is not None:
            total = product(*waiting, total)
        waiting = (step, [own[0][step], own[1][step]], oth)
    total = product(*waiting, total)
    p = jnp.concatenate(total, axis=1)
    v = place(at, v_own, v_oth)

    blocks = lax.all_to_all(p.reshape(COLS, rows // COLS, NSEL * PANEL), "cols", 0, 0)
    scaled = jnp.sum(blocks, axis=0) / damped[None, :]
    scaled = jnp.broadcast_to(scaled[None], (COLS,) + scaled.shape)
    scaled = lax.all_to_all(scaled, "cols", 0, 0).reshape(rows, NSEL * PANEL)
    return lax.dot_general(
        scaled, v, (((1,), (1,)), ((), ())), precision=lax.Precision.HIGH, preferred_element_type=F32
    )


def solution(mesh):
    in_specs = (P("rows", "cols"), P("rows", "cols", None), P(), P(), P(), P(), P())
    out_specs = P("rows", "cols")

    return jax.shard_map(shards, mesh=mesh, in_specs=in_specs, out_specs=out_specs, check_vma=False)
```

profile of v0, /device:TPU:0, one launch (start us, length us, event | category | flops | bytes accessed | tf_op | source)
XLA Modules:
  0.0 158.4 jit_solution(8970405999221245396)
XLA Ops:
  0.0 8.2 %all-to-all-start = ((f32[16,224,128]{2,1,0:T(8,128)}), f32[16,224,128]{2,1,0:T(8,128)}, u32[]{:S(2)}, u32[]{:S(2)}) async-start(f32[16,224,128]{2,1,0:T(8,128)} %bitcast.38), calls=%async_computation | async-start | bytes 3670016 | tf_op jit(solution)/shard_map/all_to_all | solution.py:125
  8.3 6.9 %rotate.1 = (f32[768,896]{1,0:T(8,128)S(1)}, f32[768,896]{1,0:T(8,128)S(1)}, f32[768,896]{1,0:T(8,128)S(1)}, f32[768,896]{1,0:T(8,128)S(1)}) custom-call(s32[8]{0:T(128)S(1)} %pad_add_fusion.1.at_ref, f32[768,3584]{1,0:T(8,128)} %refs_3_.1, f32[768,3584]{1,0:T(8,128)} %refs_3_.1, f32[768,3584]{1,0:T(8,128)} %refs_3_.1, f32[768,3584]{1,0:T(8,128)} %refs_3_.1), custom_call_target="tpu_custom_call" | custom-call | flops 1 | bytes 22020096 | tf_op jit(solution)/shard_map/rotate/pallas_call | solution.py:45
  15.2 1.5 copy-done.1
  16.7 1.5 copy-done.3
  18.3 1.5 copy-done.5
  19.9 14.8 %all-to-all-done.pieces_ref = f32[16,224,128]{2,1,0:T(8,128)} async-done(((f32[16,224,128]{2,1,0:T(8,128)}), f32[16,224,128]{2,1,0:T(8,128)}, u32[]{:S(2)}, u32[]{:S(2)}) %all-to-all-start) | async-done | bytes 1835040 | tf_op jit(solution)/shard_map/all_to_all | solution.py:125
  34.7 1.5 pick.1
  36.3 0.1 collective-permute-start
  36.3 1.5 collective-permute-done
  37.9 0.8 pad_maximum_fusion.3
  38.7 0.8 collective-permute-start.1
  39.4 2.8 %collective-permute-start.6 = (f32[448,128]{1,0:T(8,128)S(1)}, f32[448,128]{1,0:T(8,128)S(1)}, u32[]{:S(2)}, u32[]{:S(2)}) collective-permute-start(f32[448,128]{1,0:T(8,128)S(1)} %pad_maximum_fusion.4), channel_id=1, source_target_pairs={{0,16},{8,24},{16,0},{24,8},{32,48},{40,56},{48,32},{56,40},{64,80... | collective-permute-start | bytes 688136 | tf_op jit(solution)/shard_map/ppermute | solution.py:134
  42.3 6.7 %collective-permute-done.1 = f32[448,128]{1,0:T(8,128)} collective-permute-done((f32[448,128]{1,0:T(8,128)}, f32[448,128]{1,0:T(8,128)}, u32[]{:S(2)}, u32[]{:S(2)}) %collective-permute-start.1) | collective-permute-done | bytes 229408 | tf_op jit(solution)/shard_map/ppermute | solution.py:134
  49.0 1.1 broadcast_select_fusion.3
  50.1 0.1 collective-permute-start.3
  50.3 2.7 %collective-permute-done.6 = f32[448,128]{1,0:T(8,128)S(1)} collective-permute-done((f32[448,128]{1,0:T(8,128)S(1)}, f32[448,128]{1,0:T(8,128)S(1)}, u32[]{:S(2)}, u32[]{:S(2)}) %collective-permute-start.6) | collective-permute-done | bytes 229408 | tf_op jit(solution)/shard_map/ppermute | solution.py:134
  52.9 0.9 broadcast_select_fusion.1
  54.1 1.4 fusion.8
  55.6 4.4 %collective-permute-done.2 = f32[896,128]{1,0:T(8,128)S(1)} collective-permute-done((f32[896,128]{1,0:T(8,128)S(1)}, f32[896,128]{1,0:T(8,128)S(1)}, u32[]{:S(2)}, u32[]{:S(2)}) %collective-permute-start.2) | collective-permute-done | bytes 458784 | tf_op jit(solution)/shard_map/ppermute | solution.py:156
  60.1 1.4 fusion.10
  61.6 3.3 %collective-permute-done.10 = f32[896,128]{1,0:T(8,128)S(1)} collective-permute-done((f32[896,128]{1,0:T(8,128)S(1)}, f32[896,128]{1,0:T(8,128)S(1)}, u32[]{:S(2)}, u32[]{:S(2)}) %collective-permute-start.10) | collective-permute-done | bytes 458784 | tf_op jit(solution)/shard_map/ppermute | solution.py:156
  65.0 1.4 fusion.11
  66.4 3.4 %collective-permute-done.4 = f32[896,128]{1,0:T(8,128)S(1)} collective-permute-done((f32[896,128]{1,0:T(8,128)S(1)}, f32[896,128]{1,0:T(8,128)S(1)}, u32[]{:S(2)}, u32[]{:S(2)}) %collective-permute-start.4) | collective-permute-done | bytes 458784 | tf_op jit(solution)/shard_map/ppermute | solution.py:156
  69.8 0.1 add.80
  69.9 4.8 %collective-permute-done.12 = f32[896,128]{1,0:T(8,128)S(1)} collective-permute-done((f32[896,128]{1,0:T(8,128)S(1)}, f32[896,128]{1,0:T(8,128)S(1)}, u32[]{:S(2)}, u32[]{:S(2)}) %collective-permute-start.12) | collective-permute-done | bytes 458784 | tf_op jit(solution)/shard_map/ppermute | solution.py:156
  74.9 1.4 convolution_add_fusion.4
  76.3 3.3 %collective-permute-done.8 = f32[896,128]{1,0:T(8,128)S(1)} collective-permute-done((f32[896,128]{1,0:T(8,128)S(1)}, f32[896,128]{1,0:T(8,128)S(1)}, u32[]{:S(2)}, u32[]{:S(2)}) %collective-permute-start.8) | collective-permute-done | bytes 458784 | tf_op jit(solution)/shard_map/ppermute | solution.py:156
  79.7 1.4 convolution_add_fusion.3
  81.1 3.4 %collective-permute-done.13 = f32[896,128]{1,0:T(8,128)S(1)} collective-permute-done((f32[896,128]{1,0:T(8,128)S(1)}, f32[896,128]{1,0:T(8,128)S(1)}, u32[]{:S(2)}, u32[]{:S(2)}) %collective-permute-start.13) | collective-permute-done | bytes 458784 | tf_op jit(solution)/shard_map/ppermute | solution.py:156
  84.6 1.4 convolution_add_fusion.2
  86.1 1.4 convolution_add_fusion.1
  87.6 1.4 convolution_add_fusion
  89.0 1.3 pad_maximum_fusion
  90.4 4.7 %all-to-all-start.1 = ((f32[8,96,512]{2,1,0:T(8,128)}), f32[8,96,512]{2,1,0:T(8,128)S(1)}, u32[]{:S(2)}, u32[]{:S(2)}) async-start(f32[8,96,512]{2,1,0:T(8,128)} %bitcast.37), calls=%async_computation.1 | async-start | bytes 3145728 | tf_op jit(solution)/shard_map/all_to_all | solution.py:165
  95.1 3.1 %gather_fusion.1 = f32[512]{0:T(512)S(1)} fusion(f32[28672]{0:T(1024)S(1)} %copy-done, s32[1024]{0:T(1024)S(1)} %get-tuple-element.61), kind=kCustom, calls=%fused_computation.1 | custom fusion | bytes 6144 | tf_op jit(solution)/shard_map/gather | solution.py:122
  98.3 3.1 %gather_fusion = f32[512]{0:T(512)S(1)} fusion(f32[8192]{0:T(1024)S(1)} %copy-done.21, s32[1024]{0:T(1024)S(1)} %get-tuple-element.62), kind=kCustom, calls=%fused_computation | custom fusion | bytes 6144 | tf_op jit(solution)/shard_map/gather | solution.py:122
  101.5 15.6 %all-to-all-done.1 = f32[8,96,512]{2,1,0:T(8,128)S(1)} async-done(((f32[8,96,512]{2,1,0:T(8,128)}), f32[8,96,512]{2,1,0:T(8,128)S(1)}, u32[]{:S(2)}, u32[]{:S(2)}) %all-to-all-start.1) | async-done | bytes 1572896 | tf_op jit(solution)/shard_map/all_to_all | solution.py:165
  117.1 0.1 reduce_sum.9
  117.3 1.3 broadcast_in_dim.15
  118.6 4.8 %all-to-all-start.2 = ((f32[8,96,512]{2,1,0:T(8,128)}), f32[8,96,512]{2,1,0:T(8,128)}, u32[]{:S(2)}, u32[]{:S(2)}) async-start(f32[8,96,512]{2,1,0:T(8,128)} %broadcast_in_dim.15), calls=%async_computation.2 | async-start | bytes 3145728 | tf_op jit(solution)/shard_map/all_to_all | solution.py:168
  123.4 1.1 maximum_maximum_fusion.refs_0_
  124.5 1.2 copy-done.14
  125.7 1.2 copy-done.16
  126.9 1.2 copy-done.18
  128.1 1.2 copy-done.20
  129.3 3.7 %place.1 = f32[3584,512]{1,0:T(8,128)} custom-call(s32[8]{0:T(128)S(1)} %pad_add_fusion.1.at_ref, f32[896,256]{1,0:T(8,128)S(1)} %maximum_maximum_fusion.refs_0_, f32[896,256]{1,0:T(8,128)S(1)} %copy-done.20, f32[896,256]{1,0:T(8,128)S(1)} %copy-done.16, f32[896,256]{1,0:T(8,128)S(1)} %copy-done.12, f32[896,256]{1,0:T(8,128)S(1)} %copy-done.18, ...), custom_call_target="tpu_custom_call" | custom-call | flops 1 | bytes 14680064 | tf_op jit(solution)/shard_map/place/pallas_call | solution.py:99
  132.9 11.4 %all-to-all-done.2 = f32[8,96,512]{2,1,0:T(8,128)} async-done(((f32[8,96,512]{2,1,0:T(8,128)}), f32[8,96,512]{2,1,0:T(8,128)}, u32[]{:S(2)}, u32[]{:S(2)}) %all-to-all-start.2) | async-done | bytes 1572896 | tf_op jit(solution)/shard_map/all_to_all | solution.py:168
  144.4 14.1 %fusion.12 = f32[768,3584]{1,0:T(8,128)} fusion(f32[768,512]{1,0:T(8,128)} %bitcast.7, f32[3584,512]{1,0:T(8,128)} %place.1), kind=kOutput, calls=%fused_computation.61 | convolution fusion | flops 8455716864 | bytes 19922944 | tf_op jit(solution)/shard_map/dot_general | solution.py:169
  (102 shorter events, 1.2 us)
Async XLA Ops:
  0.0 95.1 %copy-start = (f32[28672]{0:T(1024)S(1)}, f32[28672]{0:T(1024)}, u32[]{:S(2)}) copy-start(f32[28672]{0:T(1024)} %param.11) | copy-start | bytes 344068
  0.0 34.7 %all-to-all-start = ((f32[16,224,128]{2,1,0:T(8,128)}), f32[16,224,128]{2,1,0:T(8,128)}, u32[]{:S(2)}, u32[]{:S(2)}) async-start(f32[16,224,128]{2,1,0:T(8,128)} %bitcast.38), calls=%async_computation | async-start | bytes 3670016 | tf_op jit(solution)/shard_map/all_to_all | solution.py:125
  8.3 11.5 %copy-start.29 = (s32[4]{0:T(128)S(1)}, s32[4]{0:T(128)}, u32[]{:S(2)}) copy-start(s32[4]{0:T(128)} %param.9) | copy-start | bytes 52
  15.2 1.5 copy-start.1
  16.7 1.5 copy-start.3
  18.3 1.5 copy-start.5
  36.3 1.6 collective-permute-start
  37.9 4.4 %copy-start.24 = (f32[224,128]{1,0:T(8,128)}, f32[224,128]{1,0:T(8,128)S(1)}, u32[]{:S(2)}) copy-start(f32[224,128]{1,0:T(8,128)S(1)} %get-tuple-element.54) | copy-start | bytes 344068
  37.9 4.4 %copy-start.25 = (f32[224,128]{1,0:T(8,128)}, f32[224,128]{1,0:T(8,128)S(1)}, u32[]{:S(2)}) copy-start(f32[224,128]{1,0:T(8,128)S(1)} %get-tuple-element.57) | copy-start | bytes 344068
  37.9 4.4 %copy-start.26 = (f32[224,128]{1,0:T(8,128)}, f32[224,128]{1,0:T(8,128)S(1)}, u32[]{:S(2)}) copy-start(f32[224,128]{1,0:T(8,128)S(1)} %get-tuple-element.58) | copy-start | bytes 344068
  38.7 10.3 %collective-permute-start.1 = (f32[448,128]{1,0:T(8,128)}, f32[448,128]{1,0:T(8,128)}, u32[]{:S(2)}, u32[]{:S(2)}) collective-permute-start(f32[448,128]{1,0:T(8,128)} %pad_maximum_fusion.3), channel_id=1, source_target_pairs={{0,16},{8,24},{16,0},{24,8},{32,48},{40,56},{48,32},{56,40},{64,80... | collective-permute-start | bytes 688136 | tf_op jit(solution)/shard_map/ppermute | solution.py:134
  39.4 14.7 %copy-start.6 = (f32[768,896]{1,0:T(8,128)S(1)}, f32[768,896]{1,0:T(8,128)}, u32[]{:S(2)}) copy-start(f32[768,896]{1,0:T(8,128)} %copy-done.5) | copy-start | bytes 8257540
  39.4 13.5 %collective-permute-start.6 = (f32[448,128]{1,0:T(8,128)S(1)}, f32[448,128]{1,0:T(8,128)S(1)}, u32[]{:S(2)}, u32[]{:S(2)}) collective-permute-start(f32[448,128]{1,0:T(8,128)S(1)} %pad_maximum_fusion.4), channel_id=1, source_target_pairs={{0,16},{8,24},{16,0},{24,8},{32,48},{40,56},{48,32},{56,40},{64,80... | collective-permute-start | bytes 688136 | tf_op jit(solution)/shard_map/ppermute | solution.py:134
  50.1 5.4 %collective-permute-start.3 = (f32[896,128]{1,0:T(8,128)S(1)}, f32[896,128]{1,0:T(8,128)S(1)}, u32[]{:S(2)}, u32[]{:S(2)}) collective-permute-start(f32[896,128]{1,0:T(8,128)S(1)} %pad_maximum_fusion.1), channel_id=1, source_target_pairs={{0,8},{8,0},{16,24},{24,16},{32,40},{40,32},{48,56},{56,48},{64,72... | collective-permute-start | bytes 1376264 | tf_op jit(solution)/shard_map/ppermute | solution.py:157
  50.2 9.8 %collective-permute-start.2 = (f32[896,128]{1,0:T(8,128)S(1)}, f32[896,128]{1,0:T(8,128)S(1)}, u32[]{:S(2)}, u32[]{:S(2)}) collective-permute-start(f32[896,128]{1,0:T(8,128)S(1)} %pad_maximum_fusion.1), channel_id=1, source_target_pairs={{0,32},{8,104},{16,48},{24,120},{32,64},{40,8},{48,80},{56,24},{64... | collective-permute-start | bytes 1376264 | tf_op jit(solution)/shard_map/ppermute | solution.py:156
  53.9 6.1 %copy-start.22 = (f32[448,128]{1,0:T(8,128)}, f32[448,128]{1,0:T(8,128)S(1)}, u32[]{:S(2)}) copy-start(f32[448,128]{1,0:T(8,128)S(1)} %get-tuple-element.49) | copy-start | bytes 688132
  53.9 6.1 %copy-start.23 = (f32[448,128]{1,0:T(8,128)}, f32[448,128]{1,0:T(8,128)S(1)}, u32[]{:S(2)}) copy-start(f32[448,128]{1,0:T(8,128)S(1)} %get-tuple-element.50) | copy-start | bytes 688132
  53.9 6.2 %collective-permute-start.7 = (f32[896,128]{1,0:T(8,128)S(1)}, f32[896,128]{1,0:T(8,128)S(1)}, u32[]{:S(2)}, u32[]{:S(2)}) collective-permute-start(f32[896,128]{1,0:T(8,128)S(1)} %pad_maximum_fusion.2), channel_id=1, source_target_pairs={{0,8},{8,0},{16,24},{24,16},{32,40},{40,32},{48,56},{56,48},{64,72... | collective-permute-start | bytes 1376264 | tf_op jit(solution)/shard_map/ppermute | solution.py:157
  54.0 10.8 %collective-permute-start.10 = (f32[896,128]{1,0:T(8,128)S(1)}, f32[896,128]{1,0:T(8,128)S(1)}, u32[]{:S(2)}, u32[]{:S(2)}) collective-permute-start(f32[896,128]{1,0:T(8,128)S(1)} %pad_maximum_fusion.2), channel_id=1, source_target_pairs={{0,32},{8,104},{16,48},{24,120},{32,64},{40,8},{48,80},{56,24},{64... | collective-permute-start | bytes 1376264 | tf_op jit(solution)/shard_map/ppermute | solution.py:156
  60.0 6.5 %collective-permute-start.5 = (f32[896,128]{1,0:T(8,128)S(1)}, f32[896,128]{1,0:T(8,128)S(1)}, u32[]{:S(2)}, u32[]{:S(2)}) collective-permute-start(f32[896,128]{1,0:T(8,128)S(1)} %collective-permute-done.2), channel_id=1, source_target_pairs={{0,8},{8,0},{16,24},{24,16},{32,40},{40,32},{48,56},{56,48},{64,72... | collective-permute-start | bytes 1376264 | tf_op jit(solution)/shard_map/ppermute | solution.py:157
  60.0 9.8 %collective-permute-start.4 = (f32[896,128]{1,0:T(8,128)S(1)}, f32[896,128]{1,0:T(8,128)S(1)}, u32[]{:S(2)}, u32[]{:S(2)}) collective-permute-start(f32[896,128]{1,0:T(8,128)S(1)} %collective-permute-done.2), channel_id=1, source_target_pairs={{0,32},{8,104},{16,48},{24,120},{32,64},{40,8},{48,80},{56,24},{64... | collective-permute-start | bytes 1376264 | tf_op jit(solution)/shard_map/ppermute | solution.py:156
  60.1 4.8 %copy-start.17 = (f32[896,256]{1,0:T(8,128)}, f32[896,256]{1,0:T(8,128)S(1)}, u32[]{:S(2)}) copy-start(f32[896,256]{1,0:T(8,128)S(1)} %constant_dynamic-update-slice_fusion.refs_4_) | copy-start | bytes 2752516
  64.9 9.8 %collective-permute-start.12 = (f32[896,128]{1,0:T(8,128)S(1)}, f32[896,128]{1,0:T(8,128)S(1)}, u32[]{:S(2)}, u32[]{:S(2)}) collective-permute-start(f32[896,128]{1,0:T(8,128)S(1)} %collective-permute-done.10), channel_id=1, source_target_pairs={{0,32},{8,104},{16,48},{24,120},{32,64},{40,8},{48,80},{56,24},{64... | collective-permute-start | bytes 1376264 | tf_op jit(solution)/shard_map/ppermute | solution.py:156
  64.9 10.0 %collective-permute-start.11 = (f32[896,128]{1,0:T(8,128)S(1)}, f32[896,128]{1,0:T(8,128)S(1)}, u32[]{:S(2)}, u32[]{:S(2)}) collective-permute-start(f32[896,128]{1,0:T(8,128)S(1)} %collective-permute-done.10), channel_id=1, source_target_pairs={{0,8},{8,0},{16,24},{24,16},{32,40},{40,32},{48,56},{56,48},{64,72... | collective-permute-start | bytes 1376264 | tf_op jit(solution)/shard_map/ppermute | solution.py:157
  65.0 4.9 %copy-start.19 = (f32[896,256]{1,0:T(8,128)}, f32[896,256]{1,0:T(8,128)S(1)}, u32[]{:S(2)}) copy-start(f32[896,256]{1,0:T(8,128)S(1)} %constant_dynamic-update-slice_fusion.2.refs_1_) | copy-start | bytes 2752516
  66.4 8.5 %copy-start.4 = (f32[768,896]{1,0:T(8,128)S(1)}, f32[768,896]{1,0:T(8,128)}, u32[]{:S(2)}) copy-start(f32[768,896]{1,0:T(8,128)} %copy-done.3) | copy-start | bytes 8257540
  69.8 6.5 %collective-permute-start.9 = (f32[896,128]{1,0:T(8,128)S(1)}, f32[896,128]{1,0:T(8,128)S(1)}, u32[]{:S(2)}, u32[]{:S(2)}) collective-permute-start(f32[896,128]{1,0:T(8,128)S(1)} %collective-permute-done.4), channel_id=1, source_target_pairs={{0,8},{8,0},{16,24},{24,16},{32,40},{40,32},{48,56},{56,48},{64,72... | collective-permute-start | bytes 1376264 | tf_op jit(solution)/shard_map/ppermute | solution.py:157
  69.8 9.8 %collective-permute-start.8 = (f32[896,128]{1,0:T(8,128)S(1)}, f32[896,128]{1,0:T(8,128)S(1)}, u32[]{:S(2)}, u32[]{:S(2)}) collective-permute-start(f32[896,128]{1,0:T(8,128)S(1)} %collective-permute-done.4), channel_id=1, source_target_pairs={{0,32},{8,104},{16,48},{24,120},{32,64},{40,8},{48,80},{56,24},{64... | collective-permute-start | bytes 1376264 | tf_op jit(solution)/shard_map/ppermute | solution.py:156
  74.7 11.3 %collective-permute-start.14 = (f32[896,128]{1,0:T(8,128)S(1)}, f32[896,128]{1,0:T(8,128)S(1)}, u32[]{:S(2)}, u32[]{:S(2)}) collective-permute-start(f32[896,128]{1,0:T(8,128)S(1)} %collective-permute-done.12), channel_id=1, source_target_pairs={{0,8},{8,0},{16,24},{24,16},{32,40},{40,32},{48,56},{56,48},{64,72... | collective-permute-start | bytes 1376264 | tf_op jit(solution)/shard_map/ppermute | solution.py:157
  74.7 9.8 %collective-permute-start.13 = (f32[896,128]{1,0:T(8,128)S(1)}, f32[896,128]{1,0:T(8,128)S(1)}, u32[]{:S(2)}, u32[]{:S(2)}) collective-permute-start(f32[896,128]{1,0:T(8,128)S(1)} %collective-permute-done.12), channel_id=1, source_target_pairs={{0,32},{8,104},{16,48},{24,120},{32,64},{40,8},{48,80},{56,24},{64... | collective-permute-start | bytes 1376264 | tf_op jit(solution)/shard_map/ppermute | solution.py:156
  74.8 4.9 %copy-start.15 = (f32[896,256]{1,0:T(8,128)}, f32[896,256]{1,0:T(8,128)S(1)}, u32[]{:S(2)}) copy-start(f32[896,256]{1,0:T(8,128)S(1)} %constant_dynamic-update-slice_fusion.6.refs_2_) | copy-start | bytes 2752516
  74.9 4.7 %copy-start.9 = (f32[896,256]{1,0:T(8,128)}, f32[896,256]{1,0:T(8,128)S(1)}, u32[]{:S(2)}) copy-start(f32[896,256]{1,0:T(8,128)S(1)} %constant_dynamic-update-slice_fusion.4.refs_5_) | copy-start | bytes 2752516
  74.9 4.8 %copy-start.2 = (f32[768,896]{1,0:T(8,128)S(1)}, f32[768,896]{1,0:T(8,128)}, u32[]{:S(2)}) copy-start(f32[768,896]{1,0:T(8,128)} %copy-done.1) | copy-start | bytes 8257540
  79.6 7.9 %collective-permute-start.15 = (f32[896,128]{1,0:T(8,128)S(1)}, f32[896,128]{1,0:T(8,128)S(1)}, u32[]{:S(2)}, u32[]{:S(2)}) collective-permute-start(f32[896,128]{1,0:T(8,128)S(1)} %collective-permute-done.8), channel_id=1, source_target_pairs={{0,8},{8,0},{16,24},{24,16},{32,40},{40,32},{48,56},{56,48},{64,72... | collective-permute-start | bytes 1376264 | tf_op jit(solution)/shard_map/ppermute | solution.py:157
  84.5 3.0 %collective-permute-start.16 = (f32[896,128]{1,0:T(8,128)S(1)}, f32[896,128]{1,0:T(8,128)S(1)}, u32[]{:S(2)}, u32[]{:S(2)}) collective-permute-start(f32[896,128]{1,0:T(8,128)S(1)} %collective-permute-done.13), channel_id=1, source_target_pairs={{0,8},{8,0},{16,24},{24,16},{32,40},{40,32},{48,56},{56,48},{64,72... | collective-permute-start | bytes 1376264 | tf_op jit(solution)/shard_map/ppermute | solution.py:157
  84.6 1.5 copy-start.11
  86.0 1.5 copy-start.7
  87.6 2.8 %copy-start.13 = (f32[896,256]{1,0:T(8,128)}, f32[896,256]{1,0:T(8,128)S(1)}, u32[]{:S(2)}) copy-start(f32[896,256]{1,0:T(8,128)S(1)} %constant_dynamic-update-slice_fusion.12.refs_7_) | copy-start | bytes 2752516
  89.0 6.0 %copy-start.27 = (s32[4,128]{1,0:T(4,128)S(1)}, s32[4,128]{1,0:T(4,128)}, u32[]{:S(2)}) copy-start(s32[4,128]{1,0:T(4,128)} %param.12) | copy-start | bytes 6148
  89.0 6.0 %copy-start.28 = (s32[4,128]{1,0:T(4,128)S(1)}, s32[4,128]{1,0:T(4,128)}, u32[]{:S(2)}) copy-start(s32[4,128]{1,0:T(4,128)} %param.13) | copy-start | bytes 6148
  90.4 7.9 %copy-start.21 = (f32[8192]{0:T(1024)S(1)}, f32[8192]{0:T(1024)}, u32[]{:S(2)}) copy-start(f32[8192]{0:T(1024)} %param.10) | copy-start | bytes 98308
  90.4 26.7 %all-to-all-start.1 = ((f32[8,96,512]{2,1,0:T(8,128)}), f32[8,96,512]{2,1,0:T(8,128)S(1)}, u32[]{:S(2)}, u32[]{:S(2)}) async-start(f32[8,96,512]{2,1,0:T(8,128)} %bitcast.37), calls=%async_computation.1 | async-start | bytes 3145728 | tf_op jit(solution)/shard_map/all_to_all | solution.py:165
  118.6 5.9 %copy-start.8 = (f32[896,256]{1,0:T(8,128)S(1)}, f32[896,256]{1,0:T(8,128)}, u32[]{:S(2)}) copy-start(f32[896,256]{1,0:T(8,128)} %copy-done.7) | copy-start | bytes 2752516
  118.6 5.9 %copy-start.10 = (f32[896,256]{1,0:T(8,128)S(1)}, f32[896,256]{1,0:T(8,128)}, u32[]{:S(2)}) copy-start(f32[896,256]{1,0:T(8,128)} %copy-done.9) | copy-start | bytes 2752516
  118.6 5.9 %copy-start.12 = (f32[896,256]{1,0:T(8,128)S(1)}, f32[896,256]{1,0:T(8,128)}, u32[]{:S(2)}) copy-start(f32[896,256]{1,0:T(8,128)} %copy-done.11) | copy-start | bytes 2752516
  118.6 25.8 %all-to-all-start.2 = ((f32[8,96,512]{2,1,0:T(8,128)}), f32[8,96,512]{2,1,0:T(8,128)}, u32[]{:S(2)}, u32[]{:S(2)}) async-start(f32[8,96,512]{2,1,0:T(8,128)} %broadcast_in_dim.15), calls=%async_computation.2 | async-start | bytes 3145728 | tf_op jit(solution)/shard_map/all_to_all | solution.py:168
  124.5 1.2 copy-start.14
  126.9 1.2 copy-start.18
  (2 other events, 2.4 us)
where the time goes:
time: 159 us; the launch traced here: 158 us
  waiting for transfers between devices  75.2 us (47%)
  matrix products  25.3 us (16%)
  starting transfers between devices  21.7 us (14%)
  local copies, waits for them, and re-layouts  17.5 us (11%)
  Pallas kernels  12.1 us (8%)
  other arithmetic  5.82 us (4%)
    ppermute x6, waiting for transfers between devices, shards(): own[c].append(lax.ppermute(held, 'rows', RING))  22.5 us
    all_to_all x1, waiting for transfers between devices, shards(): lax.all_to_all(p.reshape(COLS, rows // COLS, NSEL * PANEL), 'cols', 0, 0)  15.6 us
    all_to_all x1, waiting for transfers between devices, shards(): pieces = lax.all_to_all(basis.reshape(16, -1, PANEL), 'rows', 0, 0)  14.8 us
    dot_general x1, matrix products, shards(): lax.dot_general(scaled, v, (((1,), (1,)), ((), ())), precision=lax.Precis...  14.1 us
    all_to_all x1, waiting for transfers between devices, shards(): scaled = lax.all_to_all(scaled, 'cols', 0, 0).reshape(rows, NSEL * PANEL)  11.4 us
    dot_general x8, matrix products, dot(): jnp.dot(a, b, precision=lax.Precision.HIGH, preferred_element_type=F32)  11.3 us
    unnamed x67, local copies, waits for them, and re-layouts  9.6 us
    ppermute x2, waiting for transfers between devices, shards(): own[c].append(ordered(x == 0, half, lax.ppermute(half, 'rows', XPAIR)))  9.32 us
  transfers between devices with their start and end apart: 20, of which 12 were waited for; matrix products, arithmetic and copies ran while one was open for 13% of the time, Pallas kernels for 7%

commit v1 on v0

--- a/solution.py
+++ b/solution.py
@@ -15,6 +15,7 @@
 
 
 CORE = [(r, r ^ 1) for r in range(16)]
+CHIPS = [[r for r in range(16) if r % 2 == core] for core in range(2)]
 XPAIR = [(r, r ^ 2) for r in range(16)]
 RING = [(r, ((r // 4 + (1 if r % 2 == 0 else 3)) % 4) * 4 + r % 4) for r in range(16)]
 
@@ -57,26 +58,51 @@
     )(at, *[stay(gradient)] * PLANES)
 
 
-def pick_body(at_ref, pieces_ref, a_ref, b_ref, give_ref):
+def pick_body(at_ref, pieces_ref, mine_ref, give_ref):
     core = at_ref[NSEL]
-    a_ref[...] = pieces_ref[at_ref[2 * core]]
-    b_ref[...] = pieces_ref[at_ref[2 * core + 1]]
-    give_ref[0] = pieces_ref[at_ref[2 - 2 * core]]
-    give_ref[1] = pieces_ref[at_ref[3 - 2 * core]]
+    for i in range(2):
+        mine_ref[i] = pieces_ref[at_ref[2 * core + i] // 2]
+        give_ref[i] = pieces_ref[at_ref[2 - 2 * core + i] // 2]
 
 
 def pick(at, pieces):
-    one = jax.ShapeDtypeStruct(pieces.shape[1:], F32)
     two = jax.ShapeDtypeStruct((2, *pieces.shape[1:]), F32)
     return pl.pallas_call(
         pick_body,
-        out_shape=[one, one, two],
+        out_shape=[two, two],
         in_specs=[SM, VM],
-        out_specs=[VM] * 3,
+        out_specs=[VM] * 2,
         compiler_params=pltpu.CompilerParams(vmem_limit_bytes=8 << 20),
         cost_estimate=pl.CostEstimate(flops=1, bytes_accessed=pieces.size, transcendentals=0),
         name="pick",
     )(at, pieces)
+
+
+def settle_body(at_ref, mine_ref, got_ref, *outs):
+    core = at_ref[NSEL]
+    for i, out in enumerate(outs):
+        here = at_ref[2 * core + i] % 2 == core
+
+        @pl.when(here)
+        def _():
+            out[...] = mine_ref[i]
+
+        @pl.when(jnp.logical_not(here))
+        def _():
+            out[...] = got_ref[i]
+
+
+def settle(at, mine, got):
+    one = jax.ShapeDtypeStruct(mine.shape[1:], F32)
+    return pl.pallas_call(
+        settle_body,
+        out_shape=[one, one],
+        in_specs=[SM, VM, VM],
+        out_specs=[VM] * 2,
+        compiler_params=pltpu.CompilerParams(vmem_limit_bytes=8 << 20),
+        cost_estimate=pl.CostEstimate(flops=1, bytes_accessed=mine.size * 8, transcendentals=0),
+        name="settle",
+    )(at, mine, got)
 
 
 def place_body(at_ref, *refs):
@@ -98,9 +124,9 @@
     quarter = own[0].shape[0]
     return pl.pallas_call(
         place_body,
-        out_shape=pltpu.HBM((PLANES * quarter, 2 * PAIR), F32),
+        out_shape=pltpu.VMEM((PLANES * quarter, 2 * PAIR), F32),
         in_specs=[SM] + [VM] * (2 * PLANES),
-        out_specs=HBM,
+        out_specs=VM,
         scratch_shapes=[pltpu.SemaphoreType.DMA((2, PLANES))],
         compiler_params=pltpu.CompilerParams(vmem_limit_bytes=8 << 20),
         cost_estimate=pl.CostEstimate(flops=1, bytes_accessed=quarter * PAIR * 64, transcendentals=0),
@@ -122,16 +148,21 @@
     damped = (input_eigen[input_pick] * output_eigen[output_pick] + 0.05).reshape(-1)
     damped = jnp.where(even, damped, jnp.roll(damped, PAIR))
 
-    pieces = lax.all_to_all(basis.reshape(16, -1, PANEL), "rows", 0, 0)
+    pieces = lax.all_to_all(basis.reshape(8, -1, PANEL), "rows", 0, 0, axis_index_groups=CHIPS)
     at = jnp.arange(PLANES, dtype=jnp.int32) * way.astype(jnp.int32)
     at = jnp.concatenate([(z - at + 4) % 4, (z + at + 4) % 4])
     pieces, *g = lax.optimization_barrier((pieces, *rotate(at, gradient)))
-    mine_a, mine_b, give = pick(jnp.append(panel_index, core).astype(jnp.int32), pieces)
-    got = lax.ppermute(give, "rows", CORE)
-    halves = [ordered(even, mine_a, got[0]), ordered(even, mine_b, got[1])]
-    own = [[], []]
-    for c, half in enumerate(halves):
-        own[c].append(ordered(x == 0, half, lax.ppermute(half, "rows", XPAIR)))
+    chosen = jnp.append(panel_index, core).astype(jnp.int32)
+    mine, give = pick(chosen, pieces)
+    half_a, half_b = settle(chosen, mine, lax.ppermute(give, "rows", CORE))
+
+    def other_x(half):
+        return ordered(x == 0, half, lax.ppermute(half, "rows", XPAIR))
+
+    own, halves = [[other_x(half_a)], []], [half_b]
+    for step in range(PLANES - 1):
+        halves.append(lax.ppermute(halves[step], "rows", RING))
+    own[1] = [other_x(half) for half in halves]
 
     v_own, v_oth, total, waiting = [], [], None, None
 
@@ -152,7 +183,7 @@
                     held, last_oth[0], *total = lax.optimization_barrier((held, last_oth[0], *total))
                 else:
                     held, last_oth[0] = lax.optimization_barrier((held, last_oth[0]))
-            if step < PLANES - 1:
+            if c == 0 and step < PLANES - 1:
                 own[c].append(lax.ppermute(held, "rows", RING))
             oth[c] = lax.ppermute(held, "rows", CORE)
         if waiting is not None:

time: 159 us -> 162 us (1.019)
  starting transfers between devices: 21.7 us -> 29.1 us
  waiting for transfers between devices: 75.2 us -> 73.3 us
    ppermute x6 -> x3, waiting for transfers between devices: 22.5 us -> 4.81 us  [shards(): own[c].append(lax.ppermute(held, 'rows', RING))]
    ppermute x3 -> x9, waiting for transfers between devices: 10.8 us -> 25.3 us  [the longest x5 22 us: other_x(): return ordered(x == 0, half, lax.ppermute(half, 'rows', XPAIR))]
    ppermute x3 -> x9, starting transfers between devices: 3.69 us -> 10.4 us  [the longest x5 9.08 us: other_x(): return ordered(x == 0, half, lax.ppermute(half, 'rows', XPAIR))]
    all_to_all x1, waiting for transfers between devices: 11.4 us -> 13.5 us  [shards(): scaled = lax.all_to_all(scaled, 'cols', 0, 0).reshape(rows, NSEL * PANEL)]
    pallas_call x2 -> x3, Pallas kernels: 5.23 us -> 3.94 us  [the longest x1 1.76 us: place(): pl.pallas_call(place_body, out_shape=pltpu.VMEM((PLANES * quarter, 2 * PA...]
    unnamed x67 -> x86, local copies, waits for them, and re-layouts: 9.6 us -> 10.4 us
  transfers between devices with their start and end apart: 20 -> 23, of which waited for: 12 -> 11; matrix products, arithmetic and copies ran while one was open for 13% -> 12% of each run, Pallas kernels for 7% -> 5%
where the time goes in v1:
time: 162 us
  waiting for transfers between devices  73.3 us (45%)
  starting transfers between devices  29.1 us (18%)
  matrix products  24.8 us (15%)
  local copies, waits for them, and re-layouts  18.1 us (11%)
  Pallas kernels  10.8 us (7%)
  other arithmetic  4.58 us (3%)
    ppermute x5, waiting for transfers between devices, other_x(): return ordered(x == 0, half, lax.ppermute(half, 'rows', XPAIR))  22 us
    all_to_all x1, waiting for transfers between devices, shards(): lax.all_to_all(p.reshape(COLS, rows // COLS, NSEL * PANEL), 'cols', 0, 0)  15.6 us
    all_to_all x1, waiting for transfers between devices, shards(): lax.all_to_all(basis.reshape(8, -1, PANEL), 'rows', 0, 0, axis_index_grou...  14.1 us
    dot_general x1, matrix products, shards(): lax.dot_general(scaled, v, (((1,), (1,)), ((), ())), precision=lax.Precis...  13.6 us
    all_to_all x1, waiting for transfers between devices, shards(): scaled = lax.all_to_all(scaled, 'cols', 0, 0).reshape(rows, NSEL * PANEL)  13.5 us
    dot_general x8, matrix products, dot(): jnp.dot(a, b, precision=lax.Precision.HIGH, preferred_element_type=F32)  11.3 us
    unnamed x86, local copies, waits for them, and re-layouts  10.4 us
    ppermute x5, starting transfers between devices, other_x(): return ordered(x == 0, half, lax.ppermute(half, 'rows', XPAIR))  9.08 us
  transfers between devices with their start and end apart: 23, of which 11 were waited for; matrix products, arithmetic and copies ran while one was open for 12% of the time, Pallas kernels for 5%

profile of v1, /device:TPU:0, one launch (start us, length us, event | category | flops | bytes accessed | tf_op | source)
XLA Modules:
  0.0 161.8 jit_solution(8577883268584798343)
XLA Ops:
  0.0 8.0 %all-to-all-start = ((f32[8,448,128]{2,1,0:T(8,128)}), f32[8,448,128]{2,1,0:T(8,128)}, u32[]{:S(2)}, u32[]{:S(2)}) async-start(f32[8,448,128]{2,1,0:T(8,128)} %bitcast.23), calls=%async_computation | async-start | bytes 3670016 | tf_op jit(solution)/shard_map/all_to_all | solution.py:151
  8.1 6.9 %rotate.1 = (f32[768,896]{1,0:T(8,128)S(1)}, f32[768,896]{1,0:T(8,128)S(1)}, f32[768,896]{1,0:T(8,128)S(1)}, f32[768,896]{1,0:T(8,128)S(1)}) custom-call(s32[8]{0:T(128)S(1)} %pad_add_fusion.1.at_ref, f32[768,3584]{1,0:T(8,128)} %refs_3_.1, f32[768,3584]{1,0:T(8,128)} %refs_3_.1, f32[768,3584]{1,0:T(8,128)} %refs_3_.1, f32[768,3584]{1,0:T(8,128)} %refs_3_.1), custom_call_target="tpu_custom_call" | custom-call | flops 1 | bytes 22020096 | tf_op jit(solution)/shard_map/rotate/pallas_call | solution.py:46
  15.0 1.5 copy-done.2
  16.5 1.5 copy-done.4
  18.1 1.5 copy-done.6
  19.7 14.1 %all-to-all-done.pieces_ref = f32[8,448,128]{2,1,0:T(8,128)} async-done(((f32[8,448,128]{2,1,0:T(8,128)}), f32[8,448,128]{2,1,0:T(8,128)}, u32[]{:S(2)}, u32[]{:S(2)}) %all-to-all-start) | async-done | bytes 1835040 | tf_op jit(solution)/shard_map/all_to_all | solution.py:151
  33.8 1.6 pick.1
  35.5 1.8 %collective-permute-done.got_ref = f32[2,448,128]{2,1,0:T(8,128)S(1)} collective-permute-done((f32[2,448,128]{2,1,0:T(8,128)S(1)}, f32[2,448,128]{2,1,0:T(8,128)S(1)}, u32[]{:S(2)}, u32[]{:S(2)}) %collective-permute-start) | collective-permute-done | bytes 458784 | tf_op jit(solution)/shard_map/ppermute | solution.py:157
  37.3 0.6 settle.1
  37.9 0.9 collective-permute-start.1
  38.8 0.6 collective-permute-start.10
  39.4 2.2 %collective-permute-start.6 = (f32[448,128]{1,0:T(8,128)S(1)}, f32[448,128]{1,0:T(8,128)S(1)}, u32[]{:S(2)}, u32[]{:S(2)}) collective-permute-start(f32[448,128]{1,0:T(8,128)S(1)} %get-tuple-element.38), channel_id=1, source_target_pairs={{0,16},{8,24},{16,0},{24,8},{32,48},{40,56},{48,32},{56,40},{64,80... | collective-permute-start | bytes 688136 | tf_op jit(solution)/shard_map/ppermute | solution.py:160
  41.5 6.5 %collective-permute-done.1 = f32[448,128]{1,0:T(8,128)} collective-permute-done((f32[448,128]{1,0:T(8,128)S(1)}, f32[448,128]{1,0:T(8,128)}, u32[]{:S(2)}, u32[]{:S(2)}) %collective-permute-start.1) | collective-permute-done | bytes 229408 | tf_op jit(solution)/shard_map/ppermute | solution.py:160
  48.1 1.0 broadcast_select_fusion.9
  49.3 2.8 %collective-permute-done.6 = f32[448,128]{1,0:T(8,128)S(1)} collective-permute-done((f32[448,128]{1,0:T(8,128)S(1)}, f32[448,128]{1,0:T(8,128)S(1)}, u32[]{:S(2)}, u32[]{:S(2)}) %collective-permute-start.6) | collective-permute-done | bytes 229408 | tf_op jit(solution)/shard_map/ppermute | solution.py:160
  52.2 0.9 collective-permute-start.11
  53.1 1.4 fusion.7
  54.6 0.6 collective-permute-start.13
  55.2 6.5 %collective-permute-done.11 = f32[448,128]{1,0:T(8,128)S(1)} collective-permute-done((f32[448,128]{1,0:T(8,128)S(1)}, f32[448,128]{1,0:T(8,128)S(1)}, u32[]{:S(2)}, u32[]{:S(2)}) %collective-permute-start.11) | collective-permute-done | bytes 229408 | tf_op jit(solution)/shard_map/ppermute | solution.py:160
  62.0 2.6 %collective-permute-start.14 = (f32[448,128]{1,0:T(8,128)S(1)}, f32[448,128]{1,0:T(8,128)S(1)}, u32[]{:S(2)}, u32[]{:S(2)}) collective-permute-start(f32[448,128]{1,0:T(8,128)S(1)} %collective-permute-done.13), channel_id=1, source_target_pairs={{0,16},{8,24},{16,0},{24,8},{32,48},{40,56},{48,32},{56,40},{64,80... | collective-permute-start | bytes 688136 | tf_op jit(solution)/shard_map/ppermute | solution.py:160
  64.9 1.4 fusion.9
  66.3 1.4 fusion.6
  67.7 1.5 collective-permute-done.15
  69.2 2.6 %collective-permute-start.16 = (f32[448,128]{1,0:T(8,128)S(1)}, f32[448,128]{1,0:T(8,128)S(1)}, u32[]{:S(2)}, u32[]{:S(2)}) collective-permute-start(f32[448,128]{1,0:T(8,128)S(1)} %collective-permute-done.15), channel_id=1, source_target_pairs={{0,16},{8,24},{16,0},{24,8},{32,48},{40,56},{48,32},{56,40},{64,80... | collective-permute-start | bytes 688136 | tf_op jit(solution)/shard_map/ppermute | solution.py:160
  72.2 6.0 %collective-permute-done.16 = f32[448,128]{1,0:T(8,128)S(1)} collective-permute-done((f32[448,128]{1,0:T(8,128)S(1)}, f32[448,128]{1,0:T(8,128)S(1)}, u32[]{:S(2)}, u32[]{:S(2)}) %collective-permute-start.16) | collective-permute-done | bytes 229408 | tf_op jit(solution)/shard_map/ppermute | solution.py:160
  78.3 0.9 collective-permute-start.19
  79.3 0.4 collective-permute-start.8
  79.8 1.4 fusion.10
  81.5 1.5 copy-done.3
  83.0 1.4 fusion.5
  84.4 4.8 %collective-permute-done.8 = f32[896,128]{1,0:T(8,128)S(1)} collective-permute-done((f32[896,128]{1,0:T(8,128)S(1)}, f32[896,128]{1,0:T(8,128)S(1)}, u32[]{:S(2)}, u32[]{:S(2)}) %collective-permute-start.8) | collective-permute-done | bytes 458784 | tf_op jit(solution)/shard_map/ppermute | solution.py:187
  89.3 1.4 add_add_fusion.1
  90.8 1.4 fusion.11
  92.3 1.4 add_add_fusion
  93.8 1.3 pad_maximum_fusion
  95.1 4.6 %all-to-all-start.1 = ((f32[8,96,512]{2,1,0:T(8,128)}), f32[8,96,512]{2,1,0:T(8,128)S(1)}, u32[]{:S(2)}, u32[]{:S(2)}) async-start(f32[8,96,512]{2,1,0:T(8,128)} %bitcast.2), calls=%async_computation.1 | async-start | bytes 3145728 | tf_op jit(solution)/shard_map/all_to_all | solution.py:196
  99.8 3.1 %gather_fusion.1 = f32[512]{0:T(512)S(1)} fusion(f32[28672]{0:T(1024)S(1)} %copy-done, s32[1024]{0:T(1024)S(1)} %get-tuple-element.63), kind=kCustom, calls=%fused_computation.1 | custom fusion | bytes 6144 | tf_op jit(solution)/shard_map/gather | solution.py:148
  103.0 3.1 %gather_fusion = f32[512]{0:T(512)S(1)} fusion(f32[8192]{0:T(1024)S(1)} %copy-done.16, s32[1024]{0:T(1024)S(1)} %get-tuple-element.64), kind=kCustom, calls=%fused_computation | custom fusion | bytes 6144 | tf_op jit(solution)/shard_map/gather | solution.py:148
  106.2 15.6 %all-to-all-done.1 = f32[8,96,512]{2,1,0:T(8,128)S(1)} async-done(((f32[8,96,512]{2,1,0:T(8,128)}), f32[8,96,512]{2,1,0:T(8,128)S(1)}, u32[]{:S(2)}, u32[]{:S(2)}) %all-to-all-start.1) | async-done | bytes 1572896 | tf_op jit(solution)/shard_map/all_to_all | solution.py:196
  122.0 1.3 broadcast_in_dim.15
  123.4 3.9 %all-to-all-start.2 = ((f32[8,96,512]{2,1,0:T(8,128)}), f32[8,96,512]{2,1,0:T(8,128)S(1)}, u32[]{:S(2)}, u32[]{:S(2)}) async-start(f32[8,96,512]{2,1,0:T(8,128)} %broadcast_in_dim.15), calls=%async_computation.2 | async-start | bytes 3145728 | tf_op jit(solution)/shard_map/all_to_all | solution.py:199
  127.5 1.2 maximum_maximum_fusion.1.refs_1_
  129.2 0.3 copy-done.11
  129.8 0.3 copy-done.15
  130.0 1.8 %place.1 = f32[3584,512]{1,0:T(8,128)S(1)} custom-call(s32[8]{0:T(128)S(1)} %pad_add_fusion.1.at_ref, f32[896,256]{1,0:T(8,128)S(1)} %maximum_maximum_fusion.refs_0_, f32[896,256]{1,0:T(8,128)S(1)} %maximum_maximum_fusion.1.refs_1_, f32[896,256]{1,0:T(8,128)S(1)} %maximum_maximum_fusion.2.refs_2_, f32[896,256]{1,0:T(8,128)S(1)} %maximum_maximum_fusion.3.refs_3_, ...), custom_call_target="tpu_custom_call" | custom-call | flops 1 | bytes 14680064 | tf_op jit(solution)/shard_map/place/pallas_call | solution.py:125
  131.8 2.9 %copy-done.1 = f32[3584,512]{1,0:T(8,128)} copy-done((f32[3584,512]{1,0:T(8,128)}, f32[3584,512]{1,0:T(8,128)S(1)}, u32[]{:S(2)}) %copy-start.1) | copy-done | bytes 7340056
  134.7 13.5 %all-to-all-done.2 = f32[8,96,512]{2,1,0:T(8,128)S(1)} async-done(((f32[8,96,512]{2,1,0:T(8,128)}), f32[8,96,512]{2,1,0:T(8,128)S(1)}, u32[]{:S(2)}, u32[]{:S(2)}) %all-to-all-start.2) | async-done | bytes 1572896 | tf_op jit(solution)/shard_map/all_to_all | solution.py:199
  148.2 13.6 %fusion.12 = f32[768,3584]{1,0:T(8,128)} fusion(f32[768,512]{1,0:T(8,128)S(1)} %bitcast.22, f32[3584,512]{1,0:T(8,128)} %copy-done.1), kind=kOutput, calls=%fused_computation.60 | convolution fusion | flops 8455716864 | bytes 19922944 | tf_op jit(solution)/shard_map/dot_general | solution.py:200
  (132 shorter events, 3.2 us)
Async XLA Ops:
  0.0 99.8 %copy-start = (f32[28672]{0:T(1024)S(1)}, f32[28672]{0:T(1024)}, u32[]{:S(2)}) copy-start(f32[28672]{0:T(1024)} %param.11) | copy-start | bytes 344068
  0.0 33.8 %all-to-all-start = ((f32[8,448,128]{2,1,0:T(8,128)}), f32[8,448,128]{2,1,0:T(8,128)}, u32[]{:S(2)}, u32[]{:S(2)}) async-start(f32[8,448,128]{2,1,0:T(8,128)} %bitcast.23), calls=%async_computation | async-start | bytes 3670016 | tf_op jit(solution)/shard_map/all_to_all | solution.py:151
  8.1 11.5 %copy-start.40 = (s32[4]{0:T(128)S(1)}, s32[4]{0:T(128)}, u32[]{:S(2)}) copy-start(s32[4]{0:T(128)} %param.9) | copy-start | bytes 52
  35.4 1.9 %collective-permute-start = (f32[2,448,128]{2,1,0:T(8,128)S(1)}, f32[2,448,128]{2,1,0:T(8,128)S(1)}, u32[]{:S(2)}, u32[]{:S(2)}) collective-permute-start(f32[2,448,128]{2,1,0:T(8,128)S(1)} %get-tuple-element.34), channel_id=1, source_target_pairs={{0,8},{8,0},{16,24},{24,16},{32,40},{40,32},{48,56},{56,48},{64,72... | collective-permute-start | bytes 1376264 | tf_op jit(solution)/shard_map/ppermute | solution.py:157
  37.9 10.2 %collective-permute-start.1 = (f32[448,128]{1,0:T(8,128)S(1)}, f32[448,128]{1,0:T(8,128)}, u32[]{:S(2)}, u32[]{:S(2)}) collective-permute-start(f32[448,128]{1,0:T(8,128)S(1)} %get-tuple-element.35), channel_id=1, source_target_pairs={{0,16},{8,24},{16,0},{24,8},{32,48},{40,56},{48,32},{56,40},{64,80... | collective-permute-start | bytes 688136 | tf_op jit(solution)/shard_map/ppermute | solution.py:160
  38.8 14.3 %copy-start.7 = (f32[768,896]{1,0:T(8,128)S(1)}, f32[768,896]{1,0:T(8,128)}, u32[]{:S(2)}) copy-start(f32[768,896]{1,0:T(8,128)} %copy-done.6) | copy-start | bytes 8257540
  38.8 13.4 %collective-permute-start.10 = (f32[448,128]{1,0:T(8,128)S(1)}, f32[448,128]{1,0:T(8,128)S(1)}, u32[]{:S(2)}, u32[]{:S(2)}) collective-permute-start(f32[448,128]{1,0:T(8,128)S(1)} %get-tuple-element.38), channel_id=1, source_target_pairs={{0,32},{8,104},{16,48},{24,120},{32,64},{40,8},{48,80},{56,24},{64... | collective-permute-start | bytes 688136 | tf_op jit(solution)/shard_map/ppermute | solution.py:164
  39.4 12.7 %collective-permute-start.6 = (f32[448,128]{1,0:T(8,128)S(1)}, f32[448,128]{1,0:T(8,128)S(1)}, u32[]{:S(2)}, u32[]{:S(2)}) collective-permute-start(f32[448,128]{1,0:T(8,128)S(1)} %get-tuple-element.38), channel_id=1, source_target_pairs={{0,16},{8,24},{16,0},{24,8},{32,48},{40,56},{48,32},{56,40},{64,80... | collective-permute-start | bytes 688136 | tf_op jit(solution)/shard_map/ppermute | solution.py:160
  49.0 5.5 %copy-start.17 = (f32[448,128]{1,0:T(8,128)}, f32[448,128]{1,0:T(8,128)S(1)}, u32[]{:S(2)}) copy-start(f32[448,128]{1,0:T(8,128)S(1)} %get-tuple-element.59) | copy-start | bytes 688132
  49.0 5.5 %copy-start.19 = (f32[448,128]{1,0:T(8,128)}, f32[448,128]{1,0:T(8,128)S(1)}, u32[]{:S(2)}) copy-start(f32[448,128]{1,0:T(8,128)S(1)} %get-tuple-element.60) | copy-start | bytes 688132
  49.1 12.9 %collective-permute-start.3 = (f32[896,128]{1,0:T(8,128)S(1)}, f32[896,128]{1,0:T(8,128)S(1)}, u32[]{:S(2)}, u32[]{:S(2)}) collective-permute-start(f32[896,128]{1,0:T(8,128)S(1)} %pad_maximum_fusion.1), channel_id=1, source_target_pairs={{0,8},{8,0},{16,24},{24,16},{32,40},{40,32},{48,56},{56,48},{64,72... | collective-permute-start | bytes 1376264 | tf_op jit(solution)/shard_map/ppermute | solution.py:188
  49.2 15.4 %collective-permute-start.2 = (f32[896,128]{1,0:T(8,128)S(1)}, f32[896,128]{1,0:T(8,128)S(1)}, u32[]{:S(2)}, u32[]{:S(2)}) collective-permute-start(f32[896,128]{1,0:T(8,128)S(1)} %pad_maximum_fusion.1), channel_id=1, source_target_pairs={{0,32},{8,104},{16,48},{24,120},{32,64},{40,8},{48,80},{56,24},{64... | collective-permute-start | bytes 1376264 | tf_op jit(solution)/shard_map/ppermute | solution.py:187
  52.1 9.7 %copy-start.21 = (f32[448,128]{1,0:T(8,128)}, f32[448,128]{1,0:T(8,128)S(1)}, u32[]{:S(2)}) copy-start(f32[448,128]{1,0:T(8,128)S(1)} %get-tuple-element.58) | copy-start | bytes 688132
  52.1 12.5 %collective-permute-start.7 = (f32[896,128]{1,0:T(8,128)S(1)}, f32[896,128]{1,0:T(8,128)S(1)}, u32[]{:S(2)}, u32[]{:S(2)}) collective-permute-start(f32[896,128]{1,0:T(8,128)S(1)} %pad_maximum_fusion.2), channel_id=1, source_target_pairs={{0,8},{8,0},{16,24},{24,16},{32,40},{40,32},{48,56},{56,48},{64,72... | collective-permute-start | bytes 1376264 | tf_op jit(solution)/shard_map/ppermute | solution.py:188
  52.2 9.5 %collective-permute-start.11 = (f32[448,128]{1,0:T(8,128)S(1)}, f32[448,128]{1,0:T(8,128)S(1)}, u32[]{:S(2)}, u32[]{:S(2)}) collective-permute-start(f32[448,128]{1,0:T(8,128)S(1)} %collective-permute-done.10), channel_id=1, source_target_pairs={{0,16},{8,24},{16,0},{24,8},{32,48},{40,56},{48,32},{56,40},{64,80... | collective-permute-start | bytes 688136 | tf_op jit(solution)/shard_map/ppermute | solution.py:160
  54.6 7.4 %collective-permute-start.13 = (f32[448,128]{1,0:T(8,128)S(1)}, f32[448,128]{1,0:T(8,128)S(1)}, u32[]{:S(2)}, u32[]{:S(2)}) collective-permute-start(f32[448,128]{1,0:T(8,128)S(1)} %collective-permute-done.10), channel_id=1, source_target_pairs={{0,32},{8,104},{16,48},{24,120},{32,64},{40,8},{48,80},{56,24},{64... | collective-permute-start | bytes 688136 | tf_op jit(solution)/shard_map/ppermute | solution.py:164
  61.8 4.5 %copy-start.23 = (f32[448,128]{1,0:T(8,128)}, f32[448,128]{1,0:T(8,128)S(1)}, u32[]{:S(2)}) copy-start(f32[448,128]{1,0:T(8,128)S(1)} %get-tuple-element.56) | copy-start | bytes 688132
  61.8 17.9 %collective-permute-start.12 = (f32[896,128]{1,0:T(8,128)S(1)}, f32[896,128]{1,0:T(8,128)S(1)}, u32[]{:S(2)}, u32[]{:S(2)}) collective-permute-start(f32[896,128]{1,0:T(8,128)S(1)} %pad_maximum_fusion.3), channel_id=1, source_target_pairs={{0,8},{8,0},{16,24},{24,16},{32,40},{40,32},{48,56},{56,48},{64,72... | collective-permute-start | bytes 1376264 | tf_op jit(solution)/shard_map/ppermute | solution.py:188
  61.9 7.3 %collective-permute-start.15 = (f32[448,128]{1,0:T(8,128)S(1)}, f32[448,128]{1,0:T(8,128)S(1)}, u32[]{:S(2)}, u32[]{:S(2)}) collective-permute-start(f32[448,128]{1,0:T(8,128)S(1)} %collective-permute-done.13), channel_id=1, source_target_pairs={{0,32},{8,104},{16,48},{24,120},{32,64},{40,8},{48,80},{56,24},{64... | collective-permute-start | bytes 688136 | tf_op jit(solution)/shard_map/ppermute | solution.py:164
  62.0 9.9 %collective-permute-start.14 = (f32[448,128]{1,0:T(8,128)S(1)}, f32[448,128]{1,0:T(8,128)S(1)}, u32[]{:S(2)}, u32[]{:S(2)}) collective-permute-start(f32[448,128]{1,0:T(8,128)S(1)} %collective-permute-done.13), channel_id=1, source_target_pairs={{0,16},{8,24},{16,0},{24,8},{32,48},{40,56},{48,32},{56,40},{64,80... | collective-permute-start | bytes 688136 | tf_op jit(solution)/shard_map/ppermute | solution.py:160
  64.6 14.6 %collective-permute-start.5 = (f32[896,128]{1,0:T(8,128)S(1)}, f32[896,128]{1,0:T(8,128)S(1)}, u32[]{:S(2)}, u32[]{:S(2)}) collective-permute-start(f32[896,128]{1,0:T(8,128)S(1)} %collective-permute-done.2), channel_id=1, source_target_pairs={{0,8},{8,0},{16,24},{24,16},{32,40},{40,32},{48,56},{56,48},{64,72... | collective-permute-start | bytes 1376264 | tf_op jit(solution)/shard_map/ppermute | solution.py:188
  64.6 14.6 %collective-permute-start.4 = (f32[896,128]{1,0:T(8,128)S(1)}, f32[896,128]{1,0:T(8,128)S(1)}, u32[]{:S(2)}, u32[]{:S(2)}) collective-permute-start(f32[896,128]{1,0:T(8,128)S(1)} %collective-permute-done.2), channel_id=1, source_target_pairs={{0,32},{8,104},{16,48},{24,120},{32,64},{40,8},{48,80},{56,24},{64... | collective-permute-start | bytes 1376264 | tf_op jit(solution)/shard_map/ppermute | solution.py:187
  64.9 2.9 %copy-start.8 = (f32[896,256]{1,0:T(8,128)}, f32[896,256]{1,0:T(8,128)S(1)}, u32[]{:S(2)}) copy-start(f32[896,256]{1,0:T(8,128)S(1)} %constant_dynamic-update-slice_fusion.refs_4_) | copy-start | bytes 2752516
  67.7 12.1 %copy-start.5 = (f32[768,896]{1,0:T(8,128)S(1)}, f32[768,896]{1,0:T(8,128)}, u32[]{:S(2)}) copy-start(f32[768,896]{1,0:T(8,128)} %copy-done.4) | copy-start | bytes 8257540
  69.2 9.0 %collective-permute-start.16 = (f32[448,128]{1,0:T(8,128)S(1)}, f32[448,128]{1,0:T(8,128)S(1)}, u32[]{:S(2)}, u32[]{:S(2)}) collective-permute-start(f32[448,128]{1,0:T(8,128)S(1)} %collective-permute-done.15), channel_id=1, source_target_pairs={{0,16},{8,24},{16,0},{24,8},{32,48},{40,56},{48,32},{56,40},{64,80... | collective-permute-start | bytes 688136 | tf_op jit(solution)/shard_map/ppermute | solution.py:160
  72.0 9.5 %copy-start.25 = (f32[448,128]{1,0:T(8,128)}, f32[448,128]{1,0:T(8,128)S(1)}, u32[]{:S(2)}) copy-start(f32[448,128]{1,0:T(8,128)S(1)} %get-tuple-element.51) | copy-start | bytes 688132
  72.0 9.5 %copy-start.27 = (f32[448,128]{1,0:T(8,128)}, f32[448,128]{1,0:T(8,128)S(1)}, u32[]{:S(2)}) copy-start(f32[448,128]{1,0:T(8,128)S(1)} %get-tuple-element.52) | copy-start | bytes 688132
  72.1 18.7 %collective-permute-start.17 = (f32[896,128]{1,0:T(8,128)S(1)}, f32[896,128]{1,0:T(8,128)S(1)}, u32[]{:S(2)}, u32[]{:S(2)}) collective-permute-start(f32[896,128]{1,0:T(8,128)S(1)} %pad_maximum_fusion.4), channel_id=1, source_target_pairs={{0,8},{8,0},{16,24},{24,16},{32,40},{40,32},{48,56},{56,48},{64,72... | collective-permute-start | bytes 1376264 | tf_op jit(solution)/shard_map/ppermute | solution.py:188
  78.3 11.0 %copy-start.29 = (f32[448,128]{1,0:T(8,128)}, f32[448,128]{1,0:T(8,128)S(1)}, u32[]{:S(2)}) copy-start(f32[448,128]{1,0:T(8,128)S(1)} %get-tuple-element.53) | copy-start | bytes 688132
  78.3 11.0 %copy-start.31 = (f32[448,128]{1,0:T(8,128)}, f32[448,128]{1,0:T(8,128)S(1)}, u32[]{:S(2)}) copy-start(f32[448,128]{1,0:T(8,128)S(1)} %get-tuple-element.54) | copy-start | bytes 688132
  78.3 13.9 %collective-permute-start.19 = (f32[896,128]{1,0:T(8,128)S(1)}, f32[896,128]{1,0:T(8,128)S(1)}, u32[]{:S(2)}, u32[]{:S(2)}) collective-permute-start(f32[896,128]{1,0:T(8,128)S(1)} %pad_maximum_fusion.5), channel_id=1, source_target_pairs={{0,8},{8,0},{16,24},{24,16},{32,40},{40,32},{48,56},{56,48},{64,72... | collective-permute-start | bytes 1376264 | tf_op jit(solution)/shard_map/ppermute | solution.py:188
  79.2 2.3 %copy-start.34 = (f32[896,128]{1,0:T(8,128)}, f32[896,128]{1,0:T(8,128)S(1)}, u32[]{:S(2)}) copy-start(f32[896,128]{1,0:T(8,128)S(1)} %collective-permute-done.4) | copy-start | bytes 1376260
  79.2 5.2 %collective-permute-start.9 = (f32[896,128]{1,0:T(8,128)S(1)}, f32[896,128]{1,0:T(8,128)S(1)}, u32[]{:S(2)}, u32[]{:S(2)}) collective-permute-start(f32[896,128]{1,0:T(8,128)S(1)} %collective-permute-done.4), channel_id=1, source_target_pairs={{0,8},{8,0},{16,24},{24,16},{32,40},{40,32},{48,56},{56,48},{64,72... | collective-permute-start | bytes 1376264 | tf_op jit(solution)/shard_map/ppermute | solution.py:188
  79.3 9.9 %collective-permute-start.8 = (f32[896,128]{1,0:T(8,128)S(1)}, f32[896,128]{1,0:T(8,128)S(1)}, u32[]{:S(2)}, u32[]{:S(2)}) collective-permute-start(f32[896,128]{1,0:T(8,128)S(1)} %collective-permute-done.4), channel_id=1, source_target_pairs={{0,32},{8,104},{16,48},{24,120},{32,64},{40,8},{48,80},{56,24},{64... | collective-permute-start | bytes 1376264 | tf_op jit(solution)/shard_map/ppermute | solution.py:187
  89.3 3.0 %collective-permute-start.18 = (f32[896,128]{1,0:T(8,128)S(1)}, f32[896,128]{1,0:T(8,128)S(1)}, u32[]{:S(2)}, u32[]{:S(2)}) collective-permute-start(f32[896,128]{1,0:T(8,128)S(1)} %collective-permute-done.8), channel_id=1, source_target_pairs={{0,8},{8,0},{16,24},{24,16},{32,40},{40,32},{48,56},{56,48},{64,72... | collective-permute-start | bytes 1376264 | tf_op jit(solution)/shard_map/ppermute | solution.py:188
  93.8 6.0 %copy-start.38 = (s32[4,128]{1,0:T(4,128)S(1)}, s32[4,128]{1,0:T(4,128)}, u32[]{:S(2)}) copy-start(s32[4,128]{1,0:T(4,128)} %param.12) | copy-start | bytes 6148
  93.8 6.0 %copy-start.39 = (s32[4,128]{1,0:T(4,128)S(1)}, s32[4,128]{1,0:T(4,128)}, u32[]{:S(2)}) copy-start(s32[4,128]{1,0:T(4,128)} %param.13) | copy-start | bytes 6148
  95.1 7.9 %copy-start.16 = (f32[8192]{0:T(1024)S(1)}, f32[8192]{0:T(1024)}, u32[]{:S(2)}) copy-start(f32[8192]{0:T(1024)} %param.10) | copy-start | bytes 98308
  95.1 26.7 %all-to-all-start.1 = ((f32[8,96,512]{2,1,0:T(8,128)}), f32[8,96,512]{2,1,0:T(8,128)S(1)}, u32[]{:S(2)}, u32[]{:S(2)}) async-start(f32[8,96,512]{2,1,0:T(8,128)} %bitcast.2), calls=%async_computation.1 | async-start | bytes 3145728 | tf_op jit(solution)/shard_map/all_to_all | solution.py:196
  122.0 5.3 %copy-start.18 = (f32[448,128]{1,0:T(8,128)S(1)}, f32[448,128]{1,0:T(8,128)}, u32[]{:S(2)}) copy-start(f32[448,128]{1,0:T(8,128)} %copy-done.17) | copy-start | bytes 688132
  122.0 5.3 %copy-start.20 = (f32[448,128]{1,0:T(8,128)S(1)}, f32[448,128]{1,0:T(8,128)}, u32[]{:S(2)}) copy-start(f32[448,128]{1,0:T(8,128)} %copy-done.19) | copy-start | bytes 688132
  122.0 5.3 %copy-start.22 = (f32[448,128]{1,0:T(8,128)S(1)}, f32[448,128]{1,0:T(8,128)}, u32[]{:S(2)}) copy-start(f32[448,128]{1,0:T(8,128)} %copy-done.21) | copy-start | bytes 688132
  123.4 4.1 %copy-start.24 = (f32[448,128]{1,0:T(8,128)S(1)}, f32[448,128]{1,0:T(8,128)}, u32[]{:S(2)}) copy-start(f32[448,128]{1,0:T(8,128)} %copy-done.23) | copy-start | bytes 688132
  123.4 5.4 %copy-start.26 = (f32[448,128]{1,0:T(8,128)S(1)}, f32[448,128]{1,0:T(8,128)}, u32[]{:S(2)}) copy-start(f32[448,128]{1,0:T(8,128)} %copy-done.25) | copy-start | bytes 688132
  123.4 24.8 %all-to-all-start.2 = ((f32[8,96,512]{2,1,0:T(8,128)}), f32[8,96,512]{2,1,0:T(8,128)S(1)}, u32[]{:S(2)}, u32[]{:S(2)}) async-start(f32[8,96,512]{2,1,0:T(8,128)} %broadcast_in_dim.15), calls=%async_computation.2 | async-start | bytes 3145728 | tf_op jit(solution)/shard_map/all_to_all | solution.py:199
  127.5 2.3 %copy-start.13 = (f32[896,256]{1,0:T(8,128)S(1)}, f32[896,256]{1,0:T(8,128)}, u32[]{:S(2)}) copy-start(f32[896,256]{1,0:T(8,128)} %copy-done.12) | copy-start | bytes 2752516
  127.5 2.6 %copy-start.15 = (f32[896,256]{1,0:T(8,128)S(1)}, f32[896,256]{1,0:T(8,128)}, u32[]{:S(2)}) copy-start(f32[896,256]{1,0:T(8,128)} %copy-done.14) | copy-start | bytes 2752516
  131.8 2.9 %copy-start.1 = (f32[3584,512]{1,0:T(8,128)}, f32[3584,512]{1,0:T(8,128)S(1)}, u32[]{:S(2)}) copy-start(f32[3584,512]{1,0:T(8,128)S(1)} %place.1) | copy-start | bytes 22020100
  (16 other events, 25.1 us)

commit v2 on v1

--- a/solution.py
+++ b/solution.py
@@ -136,6 +136,10 @@
 
 def dot(a, b):
     return jnp.dot(a, b, precision=lax.Precision.HIGH, preferred_element_type=F32)
+
+
+def across(dy, dx):
+    return [(c, ((c // 2 + dy) % 4) * 2 + (c % 2 ^ dx)) for c in range(COLS)]
 
 
 def shards(gradient, basis, panel_index, input_eigen, output_eigen, input_pick, output_pick):
@@ -193,10 +197,20 @@
     p = jnp.concatenate(total, axis=1)
     v = place(at, v_own, v_oth)
 
-    blocks = lax.all_to_all(p.reshape(COLS, rows // COLS, NSEL * PANEL), "cols", 0, 0)
-    scaled = jnp.sum(blocks, axis=0) / damped[None, :]
-    scaled = jnp.broadcast_to(scaled[None], (COLS,) + scaled.shape)
-    scaled = lax.all_to_all(scaled, "cols", 0, 0).reshape(rows, NSEL * PANEL)
+    mine = lax.axis_index("cols")
+    block = rows // COLS
+    turns = [(dy, dx) for dy in (2, 1, 3, 0) for dx in (1, 0)]
+    there = [((mine // 2 + dy) % 4) * 2 + (mine % 2 ^ dx) for dy, dx in turns]
+    back = [((mine // 2 - dy) % 4) * 2 + (mine % 2 ^ dx) for dy, dx in turns]
+    sums = []
+    for at_rows, turn in zip(there, turns):
+        part = lax.dynamic_slice(p, (at_rows * block, 0), (block, NSEL * PANEL))
+        sums.append(part if turn == (0, 0) else lax.ppermute(part, "cols", across(*turn)))
+    scaled_block = sum(sums[1:], sums[0]) / damped[None, :]
+    scaled = jnp.zeros((rows, NSEL * PANEL), F32)
+    for at_rows, turn in zip(back, turns):
+        part = scaled_block if turn == (0, 0) else lax.ppermute(scaled_block, "cols", across(*turn))
+        scaled = lax.dynamic_update_slice(scaled, part, (at_rows * block, 0))
     return lax.dot_general(
         scaled, v, (((1,), (1,)), ((), ())), precision=lax.Precision.HIGH, preferred_element_type=F32
     )

time: 162 us -> 169 us (1.043)
  starting transfers between devices: 29.1 us -> 40.2 us
  waiting for transfers between devices: 73.3 us -> 65.7 us
  Pallas kernels: 10.8 us -> 12.8 us
    all_to_all x2 -> x0, waiting for transfers between devices: 29.1 us -> none  [the longest x1 15.6 us: shards(): lax.all_to_all(p.reshape(COLS, rows // COLS, NSEL * PANEL), 'cols', 0, 0)]
    ppermute x0 -> x14, starting transfers between devices: none -> 21.5 us  [the longest x7 11.4 us: shards(): lax.ppermute(scaled_block, 'cols', across(*turn))]
    ppermute x0 -> x14, waiting for transfers between devices: none -> 21.1 us  [the longest x7 14.6 us: shards(): lax.ppermute(part, 'cols', across(*turn))]
    all_to_all x2 -> x0, starting transfers between devices: 8.57 us -> none  [the longest x1 4.63 us: shards(): lax.all_to_all(p.reshape(COLS, rows // COLS, NSEL * PANEL), 'cols', 0, 0)]
    ppermute x3, waiting for transfers between devices: 1.49 us -> 4.93 us  [shards(): halves.append(lax.ppermute(halves[step], 'rows', RING))]
    unnamed x86 -> x64, local copies, waits for them, and re-layouts: 10.4 us -> 13 us
    concatenate x4, other arithmetic: 1.41 us -> 4.02 us  [product(): mine, other = (jnp.concatenate(own, axis=1), jnp.concatenate(oth, axis=1))]
    ppermute x1, waiting for transfers between devices: 1.8 us -> 0.01 us  [shards(): half_a, half_b = settle(chosen, mine, lax.ppermute(give, 'rows', CORE))]
  transfers between devices with their start and end apart: 23 -> 35, of which waited for: 11 -> 17; matrix products, arithmetic and copies ran while one was open for 12% -> 13% of each run, Pallas kernels for 5% -> 5%
where the time goes in v2:
time: 169 us
  waiting for transfers between devices  65.7 us (39%)
  starting transfers between devices  40.2 us (24%)
  matrix products  23.2 us (14%)
  local copies, waits for them, and re-layouts  19.7 us (12%)
  Pallas kernels  12.8 us (8%)
  other arithmetic  6.02 us (4%)
    ppermute x5, waiting for transfers between devices, other_x(): return ordered(x == 0, half, lax.ppermute(half, 'rows', XPAIR))  22.1 us
    ppermute x7, waiting for transfers between devices, shards(): lax.ppermute(part, 'cols', across(*turn))  14.6 us
    all_to_all x1, waiting for transfers between devices, shards(): lax.all_to_all(basis.reshape(8, -1, PANEL), 'rows', 0, 0, axis_index_grou...  14.1 us
    unnamed x64, local copies, waits for them, and re-layouts  13 us
    dot_general x1, matrix products, shards(): lax.dot_general(scaled, v, (((1,), (1,)), ((), ())), precision=lax.Precis...  11.8 us
    dot_general x8, matrix products, dot(): jnp.dot(a, b, precision=lax.Precision.HIGH, preferred_element_type=F32)  11.4 us
    ppermute x7, starting transfers between devices, shards(): lax.ppermute(scaled_block, 'cols', across(*turn))  11.4 us
    ppermute x7, starting transfers between devices, shards(): lax.ppermute(part, 'cols', across(*turn))  10.1 us
  transfers between devices with their start and end apart: 35, of which 17 were waited for; matrix products, arithmetic and copies ran while one was open for 13% of the time, Pallas kernels for 5%

profile of v2, /device:TPU:0, one launch (start us, length us, event | category | flops | bytes accessed | tf_op | source)
XLA Modules:
  0.0 168.5 jit_solution(15953248048548370199)
XLA Ops:
  0.0 8.0 %all-to-all-start = ((f32[8,448,128]{2,1,0:T(8,128)}), f32[8,448,128]{2,1,0:T(8,128)}, u32[]{:S(2)}, u32[]{:S(2)}) async-start(f32[8,448,128]{2,1,0:T(8,128)} %bitcast.20), calls=%async_computation | async-start | bytes 3670016 | tf_op jit(solution)/shard_map/all_to_all | solution.py:155
  8.1 6.9 %rotate.1 = (f32[768,896]{1,0:T(8,128)S(1)}, f32[768,896]{1,0:T(8,128)S(1)}, f32[768,896]{1,0:T(8,128)S(1)}, f32[768,896]{1,0:T(8,128)S(1)}) custom-call(s32[8]{0:T(128)S(1)} %pad_add_fusion.1.at_ref, f32[768,3584]{1,0:T(8,128)} %refs_3_.1, f32[768,3584]{1,0:T(8,128)} %refs_3_.1, f32[768,3584]{1,0:T(8,128)} %refs_3_.1, f32[768,3584]{1,0:T(8,128)} %refs_3_.1), custom_call_target="tpu_custom_call" | custom-call | flops 1 | bytes 22020096 | tf_op jit(solution)/shard_map/rotate/pallas_call | solution.py:46
  15.0 1.5 copy-done.2
  16.5 1.6 copy-done.4
  18.1 1.5 copy-done.6
  19.7 14.1 %all-to-all-done.pieces_ref = f32[8,448,128]{2,1,0:T(8,128)} async-done(((f32[8,448,128]{2,1,0:T(8,128)}), f32[8,448,128]{2,1,0:T(8,128)}, u32[]{:S(2)}, u32[]{:S(2)}) %all-to-all-start) | async-done | bytes 1835040 | tf_op jit(solution)/shard_map/all_to_all | solution.py:155
  33.8 2.4 %pick.1 = (f32[2,448,128]{2,1,0:T(8,128)S(1)}, f32[2,448,128]{2,1,0:T(8,128)}) custom-call(s32[5]{0:T(128)S(1)} %pad_add_fusion.at_ref, f32[8,448,128]{2,1,0:T(8,128)} %all-to-all-done.pieces_ref), custom_call_target="tpu_custom_call" | custom-call | flops 1 | bytes 458752 | tf_op jit(solution)/shard_map/pick/pallas_call | solution.py:70
  36.3 3.1 %gather_fusion = f32[512]{0:T(512)S(1)} fusion(f32[8192]{0:T(1024)S(1)} %copy-done.24, s32[1024]{0:T(1024)S(1)} %pad_clamp_fusion.1), kind=kCustom, calls=%fused_computation | custom fusion | bytes 6144 | tf_op jit(solution)/shard_map/gather | solution.py:152
  39.5 3.1 %gather_fusion.1 = f32[512]{0:T(512)S(1)} fusion(f32[28672]{0:T(1024)S(1)} %copy-done, s32[1024]{0:T(1024)S(1)} %pad_clamp_fusion), kind=kCustom, calls=%fused_computation.1 | custom fusion | bytes 6144 | tf_op jit(solution)/shard_map/gather | solution.py:152
  43.4 1.8 %settle.1 = (f32[448,128]{1,0:T(8,128)}, f32[448,128]{1,0:T(8,128)S(1)}) custom-call(s32[5]{0:T(128)S(1)} %copy-done.23, f32[2,448,128]{2,1,0:T(8,128)S(1)} %get-tuple-element.33.mine_ref, f32[2,448,128]{2,1,0:T(8,128)} %collective-permute-done.got_ref), custom_call_target="tpu_custom_call" | custom-call | flops 1 | bytes 917504 | tf_op jit(solution)/shard_map/settle/pallas_call | solution.py:97
  46.0 2.7 %collective-permute-start.6 = (f32[448,128]{1,0:T(8,128)S(1)}, f32[448,128]{1,0:T(8,128)S(1)}, u32[]{:S(2)}, u32[]{:S(2)}) collective-permute-start(f32[448,128]{1,0:T(8,128)S(1)} %get-tuple-element.38), channel_id=1, source_target_pairs={{0,16},{8,24},{16,0},{24,8},{32,48},{40,56},{48,32},{56,40},{64,80... | collective-permute-start | bytes 688136 | tf_op jit(solution)/shard_map/ppermute | solution.py:164
  48.7 6.6 %collective-permute-done.1 = f32[448,128]{1,0:T(8,128)S(1)} collective-permute-done((f32[448,128]{1,0:T(8,128)}, f32[448,128]{1,0:T(8,128)S(1)}, u32[]{:S(2)}, u32[]{:S(2)}) %collective-permute-start.1) | collective-permute-done | bytes 229408 | tf_op jit(solution)/shard_map/ppermute | solution.py:164
  56.6 3.3 %collective-permute-done.6 = f32[448,128]{1,0:T(8,128)S(1)} collective-permute-done((f32[448,128]{1,0:T(8,128)S(1)}, f32[448,128]{1,0:T(8,128)S(1)}, u32[]{:S(2)}, u32[]{:S(2)}) %collective-permute-start.6) | collective-permute-done | bytes 229408 | tf_op jit(solution)/shard_map/ppermute | solution.py:164
  60.8 1.4 fusion.17
  63.0 5.6 %collective-permute-done.11 = f32[448,128]{1,0:T(8,128)S(1)} collective-permute-done((f32[448,128]{1,0:T(8,128)S(1)}, f32[448,128]{1,0:T(8,128)S(1)}, u32[]{:S(2)}, u32[]{:S(2)}) %collective-permute-start.11) | collective-permute-done | bytes 229408 | tf_op jit(solution)/shard_map/ppermute | solution.py:164
  69.6 2.7 %collective-permute-start.14 = (f32[448,128]{1,0:T(8,128)S(1)}, f32[448,128]{1,0:T(8,128)S(1)}, u32[]{:S(2)}, u32[]{:S(2)}) collective-permute-start(f32[448,128]{1,0:T(8,128)S(1)} %collective-permute-done.13), channel_id=1, source_target_pairs={{0,16},{8,24},{16,0},{24,8},{32,48},{40,56},{48,32},{56,40},{64,80... | collective-permute-start | bytes 688136 | tf_op jit(solution)/shard_map/ppermute | solution.py:164
  72.6 1.4 fusion.19
  74.1 1.4 fusion.16
  75.5 4.1 %collective-permute-done.15 = f32[448,128]{1,0:T(8,128)S(1)} collective-permute-done((f32[448,128]{1,0:T(8,128)S(1)}, f32[448,128]{1,0:T(8,128)S(1)}, u32[]{:S(2)}, u32[]{:S(2)}) %collective-permute-start.15) | collective-permute-done | bytes 229408 | tf_op jit(solution)/shard_map/ppermute | solution.py:168
  80.6 6.5 %collective-permute-done.16 = f32[448,128]{1,0:T(8,128)S(1)} collective-permute-done((f32[448,128]{1,0:T(8,128)S(1)}, f32[448,128]{1,0:T(8,128)S(1)}, u32[]{:S(2)}, u32[]{:S(2)}) %collective-permute-start.16) | collective-permute-done | bytes 229408 | tf_op jit(solution)/shard_map/ppermute | solution.py:164
  87.4 1.3 collective-permute-start.9
  88.9 1.4 fusion.20
  90.6 1.5 copy-done.3
  92.1 1.4 fusion.15
  93.6 3.5 %collective-permute-done.8 = f32[896,128]{1,0:T(8,128)S(1)} collective-permute-done((f32[896,128]{1,0:T(8,128)S(1)}, f32[896,128]{1,0:T(8,128)S(1)}, u32[]{:S(2)}, u32[]{:S(2)}) %collective-permute-start.8) | collective-permute-done | bytes 458784 | tf_op jit(solution)/shard_map/ppermute | solution.py:191
  97.1 1.4 add_add_fusion.1
  98.6 1.4 fusion.21
  100.2 1.4 add_add_fusion
  102.5 3.1 %collective-permute-start.25 = (f32[96,512]{1,0:T(8,128)S(1)}, f32[96,512]{1,0:T(8,128)S(1)}, u32[]{:S(2)}, u32[]{:S(2)}) collective-permute-start(f32[96,512]{1,0:T(8,128)S(1)} %get-tuple-element.56), channel_id=1, source_target_pairs={{0,6},{1,7},{2,0},{3,1},{4,2},{5,3},{6,4},{7,5},{8,14},{9,15},{10,... | collective-permute-start | bytes 589832 | tf_op jit(solution)/shard_map/ppermute | solution.py:208
  105.6 1.7 collective-permute-start.24
  107.3 1.3 collective-permute-start.23
  109.5 3.3 %collective-permute-start.20 = (f32[96,512]{1,0:T(8,128)S(1)}, f32[96,512]{1,0:T(8,128)S(1)}, u32[]{:S(2)}, u32[]{:S(2)}) collective-permute-start(f32[96,512]{1,0:T(8,128)S(1)} %get-tuple-element.52), channel_id=1, source_target_pairs={{0,5},{1,4},{2,7},{3,6},{4,1},{5,0},{6,3},{7,2},{8,13},{9,12},{10,... | collective-permute-start | bytes 589832 | tf_op jit(solution)/shard_map/ppermute | solution.py:208
  112.9 1.5 collective-permute-done.25
  116.3 4.1 %collective-permute-done.22 = f32[96,512]{1,0:T(8,128)S(1)} collective-permute-done((f32[96,512]{1,0:T(8,128)S(1)}, f32[96,512]{1,0:T(8,128)S(1)}, u32[]{:S(2)}, u32[]{:S(2)}) %collective-permute-start.22) | collective-permute-done | bytes 196640 | tf_op jit(solution)/shard_map/ppermute | solution.py:208
  120.4 4.0 %collective-permute-done.20 = f32[96,512]{1,0:T(8,128)S(1)} collective-permute-done((f32[96,512]{1,0:T(8,128)S(1)}, f32[96,512]{1,0:T(8,128)S(1)}, u32[]{:S(2)}, u32[]{:S(2)}) %collective-permute-start.20) | collective-permute-done | bytes 196640 | tf_op jit(solution)/shard_map/ppermute | solution.py:208
  124.4 4.1 %collective-permute-done.21 = f32[96,512]{1,0:T(8,128)S(1)} collective-permute-done((f32[96,512]{1,0:T(8,128)S(1)}, f32[96,512]{1,0:T(8,128)S(1)}, u32[]{:S(2)}, u32[]{:S(2)}) %collective-permute-start.21) | collective-permute-done | bytes 196640 | tf_op jit(solution)/shard_map/ppermute | solution.py:208
  130.5 2.9 %collective-permute-start.28 = (f32[96,512]{1,0:T(8,128)S(1)}, f32[96,512]{1,0:T(8,128)S(1)}, u32[]{:S(2)}, u32[]{:S(2)}) collective-permute-start(f32[96,512]{1,0:T(8,128)S(1)} %fusion.2), channel_id=1, source_target_pairs={{0,4},{1,5},{2,6},{3,7},{4,0},{5,1},{6,2},{7,3},{8,12},{9,13},{10,... | collective-permute-start | bytes 589832 | tf_op jit(solution)/shard_map/ppermute | solution.py:212
  135.7 1.2 copy-done.16
  136.8 1.2 copy-done.17
  138.0 1.2 copy-done.18
  140.4 1.8 %place.1 = f32[3584,512]{1,0:T(8,128)S(1)} custom-call(s32[8]{0:T(128)S(1)} %copy-done.21, f32[896,256]{1,0:T(8,128)S(1)} %copy-done.16, f32[896,256]{1,0:T(8,128)S(1)} %copy-done.17, f32[896,256]{1,0:T(8,128)S(1)} %copy-done.18, f32[896,256]{1,0:T(8,128)S(1)} %copy-done.19, f32[896,256]{1,0:T(8,128)S(1)} %copy-done.9, f32[896,256]{1,0:T(8,128)S(1)} %copy-done.13, ...), custom_call_target="tpu_custom_call" | custom-call | flops 1 | bytes 14680064 | tf_op jit(solution)/shard_map/place/pallas_call | solution.py:125
  142.2 1.4 collective-permute-start.30
  143.6 3.0 %collective-permute-start.31 = (f32[96,512]{1,0:T(8,128)S(1)}, f32[96,512]{1,0:T(8,128)S(1)}, u32[]{:S(2)}, u32[]{:S(2)}) collective-permute-start(f32[96,512]{1,0:T(8,128)S(1)} %fusion.2), channel_id=1, source_target_pairs={{0,7},{1,6},{2,1},{3,0},{4,3},{5,2},{6,5},{7,4},{8,15},{9,14},{10,... | collective-permute-start | bytes 589832 | tf_op jit(solution)/shard_map/ppermute | solution.py:212
  146.6 1.8 %collective-permute-start.32 = (f32[96,512]{1,0:T(8,128)S(1)}, f32[96,512]{1,0:T(8,128)S(1)}, u32[]{:S(2)}, u32[]{:S(2)}) collective-permute-start(f32[96,512]{1,0:T(8,128)S(1)} %fusion.2), channel_id=1, source_target_pairs={{0,6},{1,7},{2,0},{3,1},{4,2},{5,3},{6,4},{7,5},{8,14},{9,15},{10,... | collective-permute-start | bytes 589832 | tf_op jit(solution)/shard_map/ppermute | solution.py:212
  148.6 1.5 collective-permute-start.33
  150.1 2.0 %collective-permute-done.29 = f32[96,512]{1,0:T(8,128)S(1)} collective-permute-done((f32[96,512]{1,0:T(8,128)S(1)}, f32[96,512]{1,0:T(8,128)S(1)}, u32[]{:S(2)}, u32[]{:S(2)}) %collective-permute-start.29) | collective-permute-done | bytes 196640 | tf_op jit(solution)/shard_map/ppermute | solution.py:212
  152.1 2.6 %collective-permute-done.30 = f32[96,512]{1,0:T(8,128)S(1)} collective-permute-done((f32[96,512]{1,0:T(8,128)S(1)}, f32[96,512]{1,0:T(8,128)S(1)}, u32[]{:S(2)}, u32[]{:S(2)}) %collective-permute-start.30) | collective-permute-done | bytes 196640 | tf_op jit(solution)/shard_map/ppermute | solution.py:212
  156.7 11.8 %fusion.22 = f32[768,3584]{1,0:T(8,128)} fusion(f32[768,512]{1,0:T(8,128)S(1)} %constant_dynamic-update-slice_fusion.8, f32[3584,512]{1,0:T(8,128)S(1)} %place.1), kind=kOutput, calls=%fused_computation.92 | convolution fusion | flops 8455716864 | bytes 19922944 | tf_op jit(solution)/shard_map/dot_general | solution.py:214
  (142 shorter events, 18.9 us)
Async XLA Ops:
  0.0 39.5 %copy-start = (f32[28672]{0:T(1024)S(1)}, f32[28672]{0:T(1024)}, u32[]{:S(2)}) copy-start(f32[28672]{0:T(1024)} %param.11) | copy-start | bytes 344068
  0.0 33.8 %all-to-all-start = ((f32[8,448,128]{2,1,0:T(8,128)}), f32[8,448,128]{2,1,0:T(8,128)}, u32[]{:S(2)}, u32[]{:S(2)}) async-start(f32[8,448,128]{2,1,0:T(8,128)} %bitcast.20), calls=%async_computation | async-start | bytes 3670016 | tf_op jit(solution)/shard_map/all_to_all | solution.py:155
  8.1 6.9 %copy-start.20 = (s32[8]{0:T(128)}, s32[8]{0:T(128)S(1)}, u32[]{:S(2)}) copy-start(s32[8]{0:T(128)S(1)} %pad_add_fusion.1.at_ref) | copy-start | bytes 100
  8.1 11.5 %copy-start.29 = (s32[4]{0:T(128)S(1)}, s32[4]{0:T(128)}, u32[]{:S(2)}) copy-start(s32[4]{0:T(128)} %param.9) | copy-start | bytes 52
  19.6 16.6 %copy-start.27 = (s32[4,128]{1,0:T(4,128)S(1)}, s32[4,128]{1,0:T(4,128)}, u32[]{:S(2)}) copy-start(s32[4,128]{1,0:T(4,128)} %param.12) | copy-start | bytes 6148
  19.6 16.6 %copy-start.28 = (s32[4,128]{1,0:T(4,128)S(1)}, s32[4,128]{1,0:T(4,128)}, u32[]{:S(2)}) copy-start(s32[4,128]{1,0:T(4,128)} %param.13) | copy-start | bytes 6148
  19.6 16.7 %copy-start.24 = (f32[8192]{0:T(1024)S(1)}, f32[8192]{0:T(1024)}, u32[]{:S(2)}) copy-start(f32[8192]{0:T(1024)} %param.10) | copy-start | bytes 98308
  19.7 19.8 %copy-start.22 = (s32[5]{0:T(128)}, s32[5]{0:T(128)S(1)}, u32[]{:S(2)}) copy-start(s32[5]{0:T(128)S(1)} %pad_add_fusion.at_ref) | copy-start | bytes 64
  36.2 6.5 %collective-permute-start = (f32[2,448,128]{2,1,0:T(8,128)}, f32[2,448,128]{2,1,0:T(8,128)}, u32[]{:S(2)}, u32[]{:S(2)}) collective-permute-start(f32[2,448,128]{2,1,0:T(8,128)} %get-tuple-element.34), channel_id=1, source_target_pairs={{0,8},{8,0},{16,24},{24,16},{32,40},{40,32},{48,56},{56,48},{64,72... | collective-permute-start | bytes 1376264 | tf_op jit(solution)/shard_map/ppermute | solution.py:161
  42.7 17.2 %copy-start.25 = (f32[512]{0:T(512)}, f32[512]{0:T(512)S(1)}, u32[]{:S(2)}) copy-start(f32[512]{0:T(512)S(1)} %multiply_add_fusion) | copy-start | bytes 6148
  45.2 10.2 %collective-permute-start.1 = (f32[448,128]{1,0:T(8,128)}, f32[448,128]{1,0:T(8,128)S(1)}, u32[]{:S(2)}, u32[]{:S(2)}) collective-permute-start(f32[448,128]{1,0:T(8,128)} %get-tuple-element.35), channel_id=1, source_target_pairs={{0,16},{8,24},{16,0},{24,8},{32,48},{40,56},{48,32},{56,40},{64,80... | collective-permute-start | bytes 688136 | tf_op jit(solution)/shard_map/ppermute | solution.py:164
  46.0 14.8 %copy-start.7 = (f32[768,896]{1,0:T(8,128)S(1)}, f32[768,896]{1,0:T(8,128)}, u32[]{:S(2)}) copy-start(f32[768,896]{1,0:T(8,128)} %copy-done.6) | copy-start | bytes 8257540
  46.0 13.8 %collective-permute-start.6 = (f32[448,128]{1,0:T(8,128)S(1)}, f32[448,128]{1,0:T(8,128)S(1)}, u32[]{:S(2)}, u32[]{:S(2)}) collective-permute-start(f32[448,128]{1,0:T(8,128)S(1)} %get-tuple-element.38), channel_id=1, source_target_pairs={{0,16},{8,24},{16,0},{24,8},{32,48},{40,56},{48,32},{56,40},{64,80... | collective-permute-start | bytes 688136 | tf_op jit(solution)/shard_map/ppermute | solution.py:164
  48.7 11.1 %collective-permute-start.10 = (f32[448,128]{1,0:T(8,128)S(1)}, f32[448,128]{1,0:T(8,128)S(1)}, u32[]{:S(2)}, u32[]{:S(2)}) collective-permute-start(f32[448,128]{1,0:T(8,128)S(1)} %get-tuple-element.38), channel_id=1, source_target_pairs={{0,32},{8,104},{16,48},{24,120},{32,64},{40,8},{48,80},{56,24},{64... | collective-permute-start | bytes 688136 | tf_op jit(solution)/shard_map/ppermute | solution.py:168
  56.4 16.0 %collective-permute-start.2 = (f32[896,128]{1,0:T(8,128)S(1)}, f32[896,128]{1,0:T(8,128)S(1)}, u32[]{:S(2)}, u32[]{:S(2)}) collective-permute-start(f32[896,128]{1,0:T(8,128)S(1)} %pad_maximum_fusion), channel_id=1, source_target_pairs={{0,32},{8,104},{16,48},{24,120},{32,64},{40,8},{48,80},{56,24},{64... | collective-permute-start | bytes 1376264 | tf_op jit(solution)/shard_map/ppermute | solution.py:191
  56.5 15.9 %collective-permute-start.3 = (f32[896,128]{1,0:T(8,128)S(1)}, f32[896,128]{1,0:T(8,128)S(1)}, u32[]{:S(2)}, u32[]{:S(2)}) collective-permute-start(f32[896,128]{1,0:T(8,128)S(1)} %pad_maximum_fusion), channel_id=1, source_target_pairs={{0,8},{8,0},{16,24},{24,16},{32,40},{40,32},{48,56},{56,48},{64,72... | collective-permute-start | bytes 1376264 | tf_op jit(solution)/shard_map/ppermute | solution.py:192
  59.9 8.7 %collective-permute-start.11 = (f32[448,128]{1,0:T(8,128)S(1)}, f32[448,128]{1,0:T(8,128)S(1)}, u32[]{:S(2)}, u32[]{:S(2)}) collective-permute-start(f32[448,128]{1,0:T(8,128)S(1)} %collective-permute-done.10), channel_id=1, source_target_pairs={{0,16},{8,24},{16,0},{24,8},{32,48},{40,56},{48,32},{56,40},{64,80... | collective-permute-start | bytes 688136 | tf_op jit(solution)/shard_map/ppermute | solution.py:164
  62.2 10.2 %collective-permute-start.7 = (f32[896,128]{1,0:T(8,128)S(1)}, f32[896,128]{1,0:T(8,128)S(1)}, u32[]{:S(2)}, u32[]{:S(2)}) collective-permute-start(f32[896,128]{1,0:T(8,128)S(1)} %pad_maximum_fusion.1), channel_id=1, source_target_pairs={{0,8},{8,0},{16,24},{24,16},{32,40},{40,32},{48,56},{56,48},{64,72... | collective-permute-start | bytes 1376264 | tf_op jit(solution)/shard_map/ppermute | solution.py:192
  62.3 7.3 %collective-permute-start.13 = (f32[448,128]{1,0:T(8,128)S(1)}, f32[448,128]{1,0:T(8,128)S(1)}, u32[]{:S(2)}, u32[]{:S(2)}) collective-permute-start(f32[448,128]{1,0:T(8,128)S(1)} %collective-permute-done.10), channel_id=1, source_target_pairs={{0,32},{8,104},{16,48},{24,120},{32,64},{40,8},{48,80},{56,24},{64... | collective-permute-start | bytes 688136 | tf_op jit(solution)/shard_map/ppermute | solution.py:168
  68.7 20.1 %collective-permute-start.12 = (f32[896,128]{1,0:T(8,128)S(1)}, f32[896,128]{1,0:T(8,128)S(1)}, u32[]{:S(2)}, u32[]{:S(2)}) collective-permute-start(f32[896,128]{1,0:T(8,128)S(1)} %pad_maximum_fusion.2), channel_id=1, source_target_pairs={{0,8},{8,0},{16,24},{24,16},{32,40},{40,32},{48,56},{56,48},{64,72... | collective-permute-start | bytes 1376264 | tf_op jit(solution)/shard_map/ppermute | solution.py:192
  69.6 10.8 %collective-permute-start.14 = (f32[448,128]{1,0:T(8,128)S(1)}, f32[448,128]{1,0:T(8,128)S(1)}, u32[]{:S(2)}, u32[]{:S(2)}) collective-permute-start(f32[448,128]{1,0:T(8,128)S(1)} %collective-permute-done.13), channel_id=1, source_target_pairs={{0,16},{8,24},{16,0},{24,8},{32,48},{40,56},{48,32},{56,40},{64,80... | collective-permute-start | bytes 688136 | tf_op jit(solution)/shard_map/ppermute | solution.py:164
  72.3 7.2 %collective-permute-start.15 = (f32[448,128]{1,0:T(8,128)S(1)}, f32[448,128]{1,0:T(8,128)S(1)}, u32[]{:S(2)}, u32[]{:S(2)}) collective-permute-start(f32[448,128]{1,0:T(8,128)S(1)} %collective-permute-done.13), channel_id=1, source_target_pairs={{0,32},{8,104},{16,48},{24,120},{32,64},{40,8},{48,80},{56,24},{64... | collective-permute-start | bytes 688136 | tf_op jit(solution)/shard_map/ppermute | solution.py:168
  72.4 14.9 %collective-permute-start.4 = (f32[896,128]{1,0:T(8,128)S(1)}, f32[896,128]{1,0:T(8,128)S(1)}, u32[]{:S(2)}, u32[]{:S(2)}) collective-permute-start(f32[896,128]{1,0:T(8,128)S(1)} %collective-permute-done.2), channel_id=1, source_target_pairs={{0,32},{8,104},{16,48},{24,120},{32,64},{40,8},{48,80},{56,24},{64... | collective-permute-start | bytes 1376264 | tf_op jit(solution)/shard_map/ppermute | solution.py:191
  72.5 14.8 %collective-permute-start.5 = (f32[896,128]{1,0:T(8,128)S(1)}, f32[896,128]{1,0:T(8,128)S(1)}, u32[]{:S(2)}, u32[]{:S(2)}) collective-permute-start(f32[896,128]{1,0:T(8,128)S(1)} %collective-permute-done.2), channel_id=1, source_target_pairs={{0,8},{8,0},{16,24},{24,16},{32,40},{40,32},{48,56},{56,48},{64,72... | collective-permute-start | bytes 1376264 | tf_op jit(solution)/shard_map/ppermute | solution.py:192
  79.6 7.5 %collective-permute-start.16 = (f32[448,128]{1,0:T(8,128)S(1)}, f32[448,128]{1,0:T(8,128)S(1)}, u32[]{:S(2)}, u32[]{:S(2)}) collective-permute-start(f32[448,128]{1,0:T(8,128)S(1)} %collective-permute-done.15), channel_id=1, source_target_pairs={{0,16},{8,24},{16,0},{24,8},{32,48},{40,56},{48,32},{56,40},{64,80... | collective-permute-start | bytes 688136 | tf_op jit(solution)/shard_map/ppermute | solution.py:164
  80.5 18.1 %collective-permute-start.17 = (f32[896,128]{1,0:T(8,128)S(1)}, f32[896,128]{1,0:T(8,128)S(1)}, u32[]{:S(2)}, u32[]{:S(2)}) collective-permute-start(f32[896,128]{1,0:T(8,128)S(1)} %pad_maximum_fusion.3), channel_id=1, source_target_pairs={{0,8},{8,0},{16,24},{24,16},{32,40},{40,32},{48,56},{56,48},{64,72... | collective-permute-start | bytes 1376264 | tf_op jit(solution)/shard_map/ppermute | solution.py:192
  87.2 12.9 %collective-permute-start.19 = (f32[896,128]{1,0:T(8,128)S(1)}, f32[896,128]{1,0:T(8,128)S(1)}, u32[]{:S(2)}, u32[]{:S(2)}) collective-permute-start(f32[896,128]{1,0:T(8,128)S(1)} %pad_maximum_fusion.4), channel_id=1, source_target_pairs={{0,8},{8,0},{16,24},{24,16},{32,40},{40,32},{48,56},{56,48},{64,72... | collective-permute-start | bytes 1376264 | tf_op jit(solution)/shard_map/ppermute | solution.py:192
  87.3 9.8 %collective-permute-start.8 = (f32[896,128]{1,0:T(8,128)S(1)}, f32[896,128]{1,0:T(8,128)S(1)}, u32[]{:S(2)}, u32[]{:S(2)}) collective-permute-start(f32[896,128]{1,0:T(8,128)S(1)} %collective-permute-done.4), channel_id=1, source_target_pairs={{0,32},{8,104},{16,48},{24,120},{32,64},{40,8},{48,80},{56,24},{64... | collective-permute-start | bytes 1376264 | tf_op jit(solution)/shard_map/ppermute | solution.py:191
  87.4 9.7 %collective-permute-start.9 = (f32[896,128]{1,0:T(8,128)S(1)}, f32[896,128]{1,0:T(8,128)S(1)}, u32[]{:S(2)}, u32[]{:S(2)}) collective-permute-start(f32[896,128]{1,0:T(8,128)S(1)} %collective-permute-done.4), channel_id=1, source_target_pairs={{0,8},{8,0},{16,24},{24,16},{32,40},{40,32},{48,56},{56,48},{64,72... | collective-permute-start | bytes 1376264 | tf_op jit(solution)/shard_map/ppermute | solution.py:192
  97.1 3.0 %collective-permute-start.18 = (f32[896,128]{1,0:T(8,128)S(1)}, f32[896,128]{1,0:T(8,128)S(1)}, u32[]{:S(2)}, u32[]{:S(2)}) collective-permute-start(f32[896,128]{1,0:T(8,128)S(1)} %collective-permute-done.8), channel_id=1, source_target_pairs={{0,8},{8,0},{16,24},{24,16},{32,40},{40,32},{48,56},{56,48},{64,72... | collective-permute-start | bytes 1376264 | tf_op jit(solution)/shard_map/ppermute | solution.py:192
  101.7 7.9 %collective-permute-start.26 = (f32[96,512]{1,0:T(8,128)S(1)}, f32[96,512]{1,0:T(8,128)S(1)}, u32[]{:S(2)}, u32[]{:S(2)}) collective-permute-start(f32[96,512]{1,0:T(8,128)S(1)} %fusion.9), channel_id=1, source_target_pairs={{0,1},{1,0},{2,3},{3,2},{4,5},{5,4},{6,7},{7,6},{8,9},{9,8},{10,11... | collective-permute-start | bytes 589832 | tf_op jit(solution)/shard_map/ppermute | solution.py:208
  102.5 11.9 %collective-permute-start.25 = (f32[96,512]{1,0:T(8,128)S(1)}, f32[96,512]{1,0:T(8,128)S(1)}, u32[]{:S(2)}, u32[]{:S(2)}) collective-permute-start(f32[96,512]{1,0:T(8,128)S(1)} %get-tuple-element.56), channel_id=1, source_target_pairs={{0,6},{1,7},{2,0},{3,1},{4,2},{5,3},{6,4},{7,5},{8,14},{9,15},{10,... | collective-permute-start | bytes 589832 | tf_op jit(solution)/shard_map/ppermute | solution.py:208
  105.6 10.7 %collective-permute-start.24 = (f32[96,512]{1,0:T(8,128)S(1)}, f32[96,512]{1,0:T(8,128)S(1)}, u32[]{:S(2)}, u32[]{:S(2)}) collective-permute-start(f32[96,512]{1,0:T(8,128)S(1)} %get-tuple-element.55), channel_id=1, source_target_pairs={{0,7},{1,6},{2,1},{3,0},{4,3},{5,2},{6,5},{7,4},{8,15},{9,14},{10,... | collective-permute-start | bytes 589832 | tf_op jit(solution)/shard_map/ppermute | solution.py:208
  107.3 9.1 %collective-permute-start.23 = (f32[96,512]{1,0:T(8,128)S(1)}, f32[96,512]{1,0:T(8,128)S(1)}, u32[]{:S(2)}, u32[]{:S(2)}) collective-permute-start(f32[96,512]{1,0:T(8,128)S(1)} %get-tuple-element.54), channel_id=1, source_target_pairs={{0,2},{1,3},{2,4},{3,5},{4,6},{5,7},{6,0},{7,1},{8,10},{9,11},{10,... | collective-permute-start | bytes 589832 | tf_op jit(solution)/shard_map/ppermute | solution.py:208
  108.5 11.9 %collective-permute-start.22 = (f32[96,512]{1,0:T(8,128)S(1)}, f32[96,512]{1,0:T(8,128)S(1)}, u32[]{:S(2)}, u32[]{:S(2)}) collective-permute-start(f32[96,512]{1,0:T(8,128)S(1)} %get-tuple-element.53), channel_id=1, source_target_pairs={{0,3},{1,2},{2,5},{3,4},{4,7},{5,6},{6,1},{7,0},{8,11},{9,10},{10,... | collective-permute-start | bytes 589832 | tf_op jit(solution)/shard_map/ppermute | solution.py:208
  109.5 14.9 %collective-permute-start.20 = (f32[96,512]{1,0:T(8,128)S(1)}, f32[96,512]{1,0:T(8,128)S(1)}, u32[]{:S(2)}, u32[]{:S(2)}) collective-permute-start(f32[96,512]{1,0:T(8,128)S(1)} %get-tuple-element.52), channel_id=1, source_target_pairs={{0,5},{1,4},{2,7},{3,6},{4,1},{5,0},{6,3},{7,2},{8,13},{9,12},{10,... | collective-permute-start | bytes 589832 | tf_op jit(solution)/shard_map/ppermute | solution.py:208
  114.3 14.2 %collective-permute-start.21 = (f32[96,512]{1,0:T(8,128)S(1)}, f32[96,512]{1,0:T(8,128)S(1)}, u32[]{:S(2)}, u32[]{:S(2)}) collective-permute-start(f32[96,512]{1,0:T(8,128)S(1)} %get-tuple-element.51), channel_id=1, source_target_pairs={{0,4},{1,5},{2,6},{3,7},{4,0},{5,1},{6,2},{7,3},{8,12},{9,13},{10,... | collective-permute-start | bytes 589832 | tf_op jit(solution)/shard_map/ppermute | solution.py:208
  128.7 5.8 %copy-start.9 = (f32[896,256]{1,0:T(8,128)S(1)}, f32[896,256]{1,0:T(8,128)}, u32[]{:S(2)}) copy-start(f32[896,256]{1,0:T(8,128)} %copy-done.8) | copy-start | bytes 2752516
  128.7 5.8 %copy-start.11 = (f32[896,256]{1,0:T(8,128)S(1)}, f32[896,256]{1,0:T(8,128)}, u32[]{:S(2)}) copy-start(f32[896,256]{1,0:T(8,128)} %copy-done.10) | copy-start | bytes 2752516
  128.7 5.8 %copy-start.13 = (f32[896,256]{1,0:T(8,128)S(1)}, f32[896,256]{1,0:T(8,128)}, u32[]{:S(2)}) copy-start(f32[896,256]{1,0:T(8,128)} %copy-done.12) | copy-start | bytes 2752516
  128.7 17.8 %collective-permute-start.27 = (f32[96,512]{1,0:T(8,128)S(1)}, f32[96,512]{1,0:T(8,128)S(1)}, u32[]{:S(2)}, u32[]{:S(2)}) collective-permute-start(f32[96,512]{1,0:T(8,128)S(1)} %fusion.2), channel_id=1, source_target_pairs={{0,5},{1,4},{2,7},{3,6},{4,1},{5,0},{6,3},{7,2},{8,13},{9,12},{10,... | collective-permute-start | bytes 589832 | tf_op jit(solution)/shard_map/ppermute | solution.py:212
  130.5 18.1 %collective-permute-start.28 = (f32[96,512]{1,0:T(8,128)S(1)}, f32[96,512]{1,0:T(8,128)S(1)}, u32[]{:S(2)}, u32[]{:S(2)}) collective-permute-start(f32[96,512]{1,0:T(8,128)S(1)} %fusion.2), channel_id=1, source_target_pairs={{0,4},{1,5},{2,6},{3,7},{4,0},{5,1},{6,2},{7,3},{8,12},{9,13},{10,... | collective-permute-start | bytes 589832 | tf_op jit(solution)/shard_map/ppermute | solution.py:212
  142.1 10.0 %collective-permute-start.29 = (f32[96,512]{1,0:T(8,128)S(1)}, f32[96,512]{1,0:T(8,128)S(1)}, u32[]{:S(2)}, u32[]{:S(2)}) collective-permute-start(f32[96,512]{1,0:T(8,128)S(1)} %fusion.2), channel_id=1, source_target_pairs={{0,3},{1,2},{2,5},{3,4},{4,7},{5,6},{6,1},{7,0},{8,11},{9,10},{10,... | collective-permute-start | bytes 589832 | tf_op jit(solution)/shard_map/ppermute | solution.py:212
  142.2 12.5 %collective-permute-start.30 = (f32[96,512]{1,0:T(8,128)S(1)}, f32[96,512]{1,0:T(8,128)S(1)}, u32[]{:S(2)}, u32[]{:S(2)}) collective-permute-start(f32[96,512]{1,0:T(8,128)S(1)} %fusion.2), channel_id=1, source_target_pairs={{0,2},{1,3},{2,4},{3,5},{4,6},{5,7},{6,0},{7,1},{8,10},{9,11},{10,... | collective-permute-start | bytes 589832 | tf_op jit(solution)/shard_map/ppermute | solution.py:212
  143.6 11.1 %collective-permute-start.31 = (f32[96,512]{1,0:T(8,128)S(1)}, f32[96,512]{1,0:T(8,128)S(1)}, u32[]{:S(2)}, u32[]{:S(2)}) collective-permute-start(f32[96,512]{1,0:T(8,128)S(1)} %fusion.2), channel_id=1, source_target_pairs={{0,7},{1,6},{2,1},{3,0},{4,3},{5,2},{6,5},{7,4},{8,15},{9,14},{10,... | collective-permute-start | bytes 589832 | tf_op jit(solution)/shard_map/ppermute | solution.py:212
  146.6 9.2 %collective-permute-start.32 = (f32[96,512]{1,0:T(8,128)S(1)}, f32[96,512]{1,0:T(8,128)S(1)}, u32[]{:S(2)}, u32[]{:S(2)}) collective-permute-start(f32[96,512]{1,0:T(8,128)S(1)} %fusion.2), channel_id=1, source_target_pairs={{0,6},{1,7},{2,0},{3,1},{4,2},{5,3},{6,4},{7,5},{8,14},{9,15},{10,... | collective-permute-start | bytes 589832 | tf_op jit(solution)/shard_map/ppermute | solution.py:212
  148.6 8.0 %collective-permute-start.33 = (f32[96,512]{1,0:T(8,128)S(1)}, f32[96,512]{1,0:T(8,128)S(1)}, u32[]{:S(2)}, u32[]{:S(2)}) collective-permute-start(f32[96,512]{1,0:T(8,128)S(1)} %fusion.2), channel_id=1, source_target_pairs={{0,1},{1,0},{2,3},{3,2},{4,5},{5,4},{6,7},{7,6},{8,9},{9,8},{10,11... | collective-permute-start | bytes 589832 | tf_op jit(solution)/shard_map/ppermute | solution.py:212
  156.7 11.8 %copy-start.1 = (f32[28672]{0:T(1024)S(1)}, f32[28672]{0:T(1024)}, u32[]{:S(2)}) copy-start(f32[28672]{0:T(1024)} %param.11) | copy-start | bytes 344068
  (17 other events, 30.2 us)

commit v3 on v0

--- a/solution.py
+++ b/solution.py
@@ -98,9 +98,9 @@
     quarter = own[0].shape[0]
     return pl.pallas_call(
         place_body,
-        out_shape=pltpu.HBM((PLANES * quarter, 2 * PAIR), F32),
+        out_shape=pltpu.VMEM((PLANES * quarter, 2 * PAIR), F32),
         in_specs=[SM] + [VM] * (2 * PLANES),
-        out_specs=HBM,
+        out_specs=VM,
         scratch_shapes=[pltpu.SemaphoreType.DMA((2, PLANES))],
         compiler_params=pltpu.CompilerParams(vmem_limit_bytes=8 << 20),
         cost_estimate=pl.CostEstimate(flops=1, bytes_accessed=quarter * PAIR * 64, transcendentals=0),
@@ -110,6 +110,13 @@
 
 def dot(a, b):
     return jnp.dot(a, b, precision=lax.Precision.HIGH, preferred_element_type=F32)
+
+
+def across(dy, dx):
+    return [(c, ((c // 2 + dy) % 4) * 2 + (c % 2 ^ dx)) for c in range(COLS)]
+
+
+TURNS = ((2, 1), (2, 0), (1, 1), (3, 1), (1, 0), (3, 0), (0, 1), (0, 0))
 
 
 def shards(gradient, basis, panel_index, input_eigen, output_eigen, input_pick, output_pick):
@@ -125,7 +132,7 @@
     pieces = lax.all_to_all(basis.reshape(16, -1, PANEL), "rows", 0, 0)
     at = jnp.arange(PLANES, dtype=jnp.int32) * way.astype(jnp.int32)
     at = jnp.concatenate([(z - at + 4) % 4, (z + at + 4) % 4])
-    pieces, *g = lax.optimization_barrier((pieces, *rotate(at, gradient)))
+    pieces, damped, *g = lax.optimization_barrier((pieces, damped, *rotate(at, gradient)))
     mine_a, mine_b, give = pick(jnp.append(panel_index, core).astype(jnp.int32), pieces)
     got = lax.ppermute(give, "rows", CORE)
     halves = [ordered(even, mine_a, got[0]), ordered(even, mine_b, got[1])]
@@ -162,10 +169,20 @@
     p = jnp.concatenate(total, axis=1)
     v = place(at, v_own, v_oth)
 
-    blocks = lax.all_to_all(p.reshape(COLS, rows // COLS, NSEL * PANEL), "cols", 0, 0)
-    scaled = jnp.sum(blocks, axis=0) / damped[None, :]
-    scaled = jnp.broadcast_to(scaled[None], (COLS,) + scaled.shape)
-    scaled = lax.all_to_all(scaled, "cols", 0, 0).reshape(rows, NSEL * PANEL)
+    mine = lax.axis_index("cols")
+    block = rows // COLS
+    there = [((mine // 2 + dy) % 4) * 2 + (mine % 2 ^ dx) for dy, dx in TURNS]
+    back = [((mine // 2 - dy) % 4) * 2 + (mine % 2 ^ dx) for dy, dx in TURNS]
+    sums = []
+    for at_rows, turn in zip(there, TURNS):
+        part = lax.dynamic_slice(p, (at_rows * block, 0), (block, NSEL * PANEL))
+        sums.append(part if turn == (0, 0) else lax.ppermute(part, "cols", across(*turn)))
+    v, *sums = lax.optimization_barrier((v, *sums))
+    scaled_block = sum(sums[1:], sums[0]) / damped[None, :]
+    scaled = jnp.zeros((rows, NSEL * PANEL), F32)
+    for at_rows, turn in zip(back, TURNS):
+        part = scaled_block if turn == (0, 0) else lax.ppermute(scaled_block, "cols", across(*turn))
+        scaled = lax.dynamic_update_slice(scaled, part, (at_rows * block, 0))
     return lax.dot_general(
         scaled, v, (((1,), (1,)), ((), ())), precision=lax.Precision.HIGH, preferred_element_type=F32
     )

time: 159 us -> 155 us (0.975)
  waiting for transfers between devices: 75.2 us -> 65.3 us
  starting transfers between devices: 21.7 us -> 29.8 us
  Pallas kernels: 12.1 us -> 10.2 us
    all_to_all x2 -> x0, waiting for transfers between devices: 27 us -> none  [the longest x1 15.6 us: shards(): lax.all_to_all(p.reshape(COLS, rows // COLS, NSEL * PANEL), 'cols', 0, 0)]
    ppermute x0 -> x14, waiting for transfers between devices: none -> 26.8 us  [the longest x7 15.2 us: shards(): lax.ppermute(scaled_block, 'cols', across(*turn))]
    ppermute x0 -> x14, starting transfers between devices: none -> 17.5 us  [the longest x7 9.4 us: shards(): lax.ppermute(scaled_block, 'cols', across(*turn))]
    all_to_all x2 -> x0, starting transfers between devices: 9.45 us -> none  [the longest x1 4.78 us: shards(): scaled = lax.all_to_all(scaled, 'cols', 0, 0).reshape(rows, NSEL * PANEL)]
    all_to_all x1, waiting for transfers between devices: 14.8 us -> 8.44 us  [shards(): pieces = lax.all_to_all(basis.reshape(16, -1, PANEL), 'rows', 0, 0)]
    ppermute x6, waiting for transfers between devices: 22.5 us -> 19.1 us  [shards(): own[c].append(lax.ppermute(held, 'rows', RING))]
    pallas_call x1, Pallas kernels: 3.68 us -> 1.77 us  [place(): pl.pallas_call(place_body, out_shape=pltpu.VMEM((PLANES * quarter, 2 * PA...]
    unnamed x67 -> x75, local copies, waits for them, and re-layouts: 9.6 us -> 11.4 us
  transfers between devices with their start and end apart: 20 -> 32, of which waited for: 12 -> 18; matrix products, arithmetic and copies ran while one was open for 13% -> 14% of each run, Pallas kernels for 7% -> 6%
where the time goes in v3:
time: 155 us
  waiting for transfers between devices  65.3 us (42%)
  starting transfers between devices  29.8 us (19%)
  matrix products  24.9 us (16%)
  local copies, waits for them, and re-layouts  18.3 us (12%)
  Pallas kernels  10.2 us (7%)
  other arithmetic  5.3 us (3%)
    ppermute x6, waiting for transfers between devices, shards(): own[c].append(lax.ppermute(held, 'rows', RING))  19.1 us
    ppermute x7, waiting for transfers between devices, shards(): lax.ppermute(scaled_block, 'cols', across(*turn))  15.2 us
    dot_general x1, matrix products, shards(): lax.dot_general(scaled, v, (((1,), (1,)), ((), ())), precision=lax.Precis...  13.6 us
    ppermute x7, waiting for transfers between devices, shards(): lax.ppermute(part, 'cols', across(*turn))  11.6 us
    unnamed x75, local copies, waits for them, and re-layouts  11.4 us
    dot_general x8, matrix products, dot(): jnp.dot(a, b, precision=lax.Precision.HIGH, preferred_element_type=F32)  11.3 us
    ppermute x7, starting transfers between devices, shards(): lax.ppermute(scaled_block, 'cols', across(*turn))  9.4 us
    ppermute x2, waiting for transfers between devices, shards(): own[c].append(ordered(x == 0, half, lax.ppermute(half, 'rows', XPAIR)))  9.1 us
  transfers between devices with their start and end apart: 32, of which 18 were waited for; matrix products, arithmetic and copies ran while one was open for 14% of the time, Pallas kernels for 6%

profile of v3, /device:TPU:0, one launch (start us, length us, event | category | flops | bytes accessed | tf_op | source)
XLA Modules:
  0.0 154.6 jit_solution(6433118886355821912)
XLA Ops:
  0.0 8.2 %all-to-all-start = ((f32[16,224,128]{2,1,0:T(8,128)}), f32[16,224,128]{2,1,0:T(8,128)}, u32[]{:S(2)}, u32[]{:S(2)}) async-start(f32[16,224,128]{2,1,0:T(8,128)} %bitcast.35), calls=%async_computation | async-start | bytes 3670016 | tf_op jit(solution)/shard_map/all_to_all | solution.py:132
  8.3 6.9 %rotate.1 = (f32[768,896]{1,0:T(8,128)S(1)}, f32[768,896]{1,0:T(8,128)S(1)}, f32[768,896]{1,0:T(8,128)S(1)}, f32[768,896]{1,0:T(8,128)S(1)}) custom-call(s32[8]{0:T(128)S(1)} %pad_add_fusion.at_ref, f32[768,3584]{1,0:T(8,128)} %refs_3_.1, f32[768,3584]{1,0:T(8,128)} %refs_3_.1, f32[768,3584]{1,0:T(8,128)} %refs_3_.1, f32[768,3584]{1,0:T(8,128)} %refs_3_.1), custom_call_target="tpu_custom_call" | custom-call | flops 1 | bytes 22020096 | tf_op jit(solution)/shard_map/rotate/pallas_call | solution.py:45
  15.2 1.5 copy-done.3
  16.8 1.5 copy-done.5
  18.2 1.5 copy-done.7
  19.8 3.1 %gather_fusion = f32[512]{0:T(512)S(1)} fusion(f32[8192]{0:T(1024)S(1)} %copy-done.23, s32[1024]{0:T(1024)S(1)} %pad_clamp_fusion.1), kind=kCustom, calls=%fused_computation | custom fusion | bytes 6144 | tf_op jit(solution)/shard_map/gather | solution.py:129
  23.0 3.1 %gather_fusion.1 = f32[512]{0:T(512)S(1)} fusion(f32[28672]{0:T(1024)S(1)} %copy-done, s32[1024]{0:T(1024)S(1)} %pad_clamp_fusion), kind=kCustom, calls=%fused_computation.1 | custom fusion | bytes 6144 | tf_op jit(solution)/shard_map/gather | solution.py:129
  26.3 8.4 %all-to-all-done.pieces_ref = f32[16,224,128]{2,1,0:T(8,128)} async-done(((f32[16,224,128]{2,1,0:T(8,128)}), f32[16,224,128]{2,1,0:T(8,128)}, u32[]{:S(2)}, u32[]{:S(2)}) %all-to-all-start) | async-done | bytes 1835040 | tf_op jit(solution)/shard_map/all_to_all | solution.py:132
  34.7 1.5 %pick.1 = (f32[224,128]{1,0:T(8,128)S(1)}, f32[224,128]{1,0:T(8,128)S(1)}, f32[2,224,128]{2,1,0:T(8,128)S(1)}) custom-call(s32[5]{0:T(128)S(1)} %pad_add_fusion.1.at_ref, f32[16,224,128]{2,1,0:T(8,128)} %all-to-all-done.pieces_ref), custom_call_target="tpu_custom_call" | custom-call | flops 1 | bytes 458752 | tf_op jit(solution)/shard_map/pick/pallas_call | solution.py:71
  36.3 1.5 collective-permute-done
  38.8 2.8 %collective-permute-start.2 = (f32[448,128]{1,0:T(8,128)S(1)}, f32[448,128]{1,0:T(8,128)S(1)}, u32[]{:S(2)}, u32[]{:S(2)}) collective-permute-start(f32[448,128]{1,0:T(8,128)S(1)} %pad_maximum_fusion.3), channel_id=1, source_target_pairs={{0,16},{8,24},{16,0},{24,8},{32,48},{40,56},{48,32},{56,40},{64,80... | collective-permute-start | bytes 688136 | tf_op jit(solution)/shard_map/ppermute | solution.py:141
  41.6 6.4 %collective-permute-done.1 = f32[448,128]{1,0:T(8,128)} collective-permute-done((f32[448,128]{1,0:T(8,128)S(1)}, f32[448,128]{1,0:T(8,128)}, u32[]{:S(2)}, u32[]{:S(2)}) %collective-permute-start.1) | collective-permute-done | bytes 229408 | tf_op jit(solution)/shard_map/ppermute | solution.py:141
  48.1 1.1 broadcast_select_fusion.3
  49.4 2.6 %collective-permute-done.2 = f32[448,128]{1,0:T(8,128)S(1)} collective-permute-done((f32[448,128]{1,0:T(8,128)S(1)}, f32[448,128]{1,0:T(8,128)S(1)}, u32[]{:S(2)}, u32[]{:S(2)}) %collective-permute-start.2) | collective-permute-done | bytes 229408 | tf_op jit(solution)/shard_map/ppermute | solution.py:141
  52.3 1.4 fusion.16
  53.8 5.2 %collective-permute-done.3 = f32[896,128]{1,0:T(8,128)S(1)} collective-permute-done((f32[896,128]{1,0:T(8,128)S(1)}, f32[896,128]{1,0:T(8,128)S(1)}, u32[]{:S(2)}, u32[]{:S(2)}) %collective-permute-start.3) | collective-permute-done | bytes 458784 | tf_op jit(solution)/shard_map/ppermute | solution.py:163
  59.2 1.4 fusion.18
  60.6 3.3 %collective-permute-done.4 = f32[896,128]{1,0:T(8,128)S(1)} collective-permute-done((f32[896,128]{1,0:T(8,128)S(1)}, f32[896,128]{1,0:T(8,128)S(1)}, u32[]{:S(2)}, u32[]{:S(2)}) %collective-permute-start.4) | collective-permute-done | bytes 458784 | tf_op jit(solution)/shard_map/ppermute | solution.py:163
  64.0 1.4 fusion.19
  65.4 3.4 %collective-permute-done.6 = f32[896,128]{1,0:T(8,128)S(1)} collective-permute-done((f32[896,128]{1,0:T(8,128)S(1)}, f32[896,128]{1,0:T(8,128)S(1)}, u32[]{:S(2)}, u32[]{:S(2)}) %collective-permute-start.6) | collective-permute-done | bytes 458784 | tf_op jit(solution)/shard_map/ppermute | solution.py:163
  69.0 4.8 %collective-permute-done.7 = f32[896,128]{1,0:T(8,128)S(1)} collective-permute-done((f32[896,128]{1,0:T(8,128)S(1)}, f32[896,128]{1,0:T(8,128)S(1)}, u32[]{:S(2)}, u32[]{:S(2)}) %collective-permute-start.7) | collective-permute-done | bytes 458784 | tf_op jit(solution)/shard_map/ppermute | solution.py:163
  73.9 1.9 %copy-done.4 = f32[768,896]{1,0:T(8,128)S(1)} copy-done((f32[768,896]{1,0:T(8,128)S(1)}, f32[768,896]{1,0:T(8,128)}, u32[]{:S(2)}) %copy-start.4) | copy-done | bytes 2752536
  75.9 1.4 convolution_add_fusion.4
  77.3 1.4 collective-permute-done.10
  78.8 1.4 convolution_add_fusion.1
  81.2 1.4 convolution_add_fusion.3
  82.6 1.0 collective-permute-done.11
  83.6 1.4 convolution_add_fusion.2
  85.4 1.4 convolution_add_fusion
  87.8 3.0 %collective-permute-start.22 = (f32[96,512]{1,0:T(8,128)S(1)}, f32[96,512]{1,0:T(8,128)S(1)}, u32[]{:S(2)}, u32[]{:S(2)}) collective-permute-start(f32[96,512]{1,0:T(8,128)S(1)} %get-tuple-element.76), channel_id=1, source_target_pairs={{0,6},{1,7},{2,0},{3,1},{4,2},{5,3},{6,4},{7,5},{8,14},{9,15},{10,... | collective-permute-start | bytes 589832 | tf_op jit(solution)/shard_map/ppermute | solution.py:179
  91.4 1.6 %fusion = (f32[96,512]{1,0:T(8,128)S(1)}, f32[96,512]{1,0:T(8,128)S(1)}, f32[96,512]{1,0:T(8,128)S(1)}, f32[96,512]{1,0:T(8,128)S(1)}, f32[96,512]{1,0:T(8,128)S(1)}, /*index=5*/f32[96,512]{1,0:T(8,128)S(1)}) fusion(s32[]{:T(128)S(6)} %select_n.262, f32[768,256]{1,0:T(8,128)} %copy-done.24, f32[768,256]{1,0:T(8,128)} %copy-done.25, s32[]{:T(128)S(6)} %select_n.252, ...), kind=kLoop, calls=%fused_computation.28 | loop fusion | flops 294912 | bytes 2752536 | tf_op jit(solution)/shard_map/concatenate | solution.py:169
  93.0 1.5 collective-permute-start.17
  94.6 2.9 %collective-permute-start.18 = (f32[96,512]{1,0:T(8,128)S(1)}, f32[96,512]{1,0:T(8,128)S(1)}, u32[]{:S(2)}, u32[]{:S(2)}) collective-permute-start(f32[96,512]{1,0:T(8,128)S(1)} %get-tuple-element.71), channel_id=1, source_target_pairs={{0,4},{1,5},{2,6},{3,7},{4,0},{5,1},{6,2},{7,3},{8,12},{9,13},{10,... | collective-permute-start | bytes 589832 | tf_op jit(solution)/shard_map/ppermute | solution.py:179
  97.5 6.3 %collective-permute-done.22 = f32[96,512]{1,0:T(8,128)S(1)} collective-permute-done((f32[96,512]{1,0:T(8,128)S(1)}, f32[96,512]{1,0:T(8,128)S(1)}, u32[]{:S(2)}, u32[]{:S(2)}) %collective-permute-start.22) | collective-permute-done | bytes 196640 | tf_op jit(solution)/shard_map/ppermute | solution.py:179
  104.9 1.8 %place.1 = f32[3584,512]{1,0:T(8,128)S(1)} custom-call(s32[8]{0:T(128)S(1)} %pad_add_fusion.at_ref, f32[896,256]{1,0:T(8,128)S(1)} %maximum_maximum_fusion.refs_0_, f32[896,256]{1,0:T(8,128)S(1)} %copy-done.20, f32[896,256]{1,0:T(8,128)S(1)} %copy-done.18, f32[896,256]{1,0:T(8,128)S(1)} %copy-done.10, f32[896,256]{1,0:T(8,128)S(1)} %copy-done.22, ...), custom_call_target="tpu_custom_call" | custom-call | flops 1 | bytes 14680064 | tf_op jit(solution)/shard_map/place/pallas_call | solution.py:99
  106.7 2.9 %copy-done.2 = f32[3584,512]{1,0:T(8,128)} copy-done((f32[3584,512]{1,0:T(8,128)}, f32[3584,512]{1,0:T(8,128)S(1)}, u32[]{:S(2)}) %copy-start.2) | copy-done | bytes 7340056
  109.6 1.2 collective-permute-done.18
  110.8 4.1 %collective-permute-done.21 = f32[96,512]{1,0:T(8,128)S(1)} collective-permute-done((f32[96,512]{1,0:T(8,128)S(1)}, f32[96,512]{1,0:T(8,128)S(1)}, u32[]{:S(2)}, u32[]{:S(2)}) %collective-permute-start.21) | collective-permute-done | bytes 196640 | tf_op jit(solution)/shard_map/ppermute | solution.py:179
  114.9 1.1 add_divide_fusion
  116.0 2.3 %collective-permute-start.24 = (f32[96,512]{1,0:T(8,128)S(1)}, f32[96,512]{1,0:T(8,128)S(1)}, u32[]{:S(2)}, u32[]{:S(2)}) collective-permute-start(f32[96,512]{1,0:T(8,128)S(1)} %add_divide_fusion), channel_id=1, source_target_pairs={{0,5},{1,4},{2,7},{3,6},{4,1},{5,0},{6,3},{7,2},{8,13},{9,12},{10,... | collective-permute-start | bytes 589832 | tf_op jit(solution)/shard_map/ppermute | solution.py:184
  118.3 1.6 %collective-permute-start.25 = (f32[96,512]{1,0:T(8,128)S(1)}, f32[96,512]{1,0:T(8,128)S(1)}, u32[]{:S(2)}, u32[]{:S(2)}) collective-permute-start(f32[96,512]{1,0:T(8,128)S(1)} %add_divide_fusion), channel_id=1, source_target_pairs={{0,4},{1,5},{2,6},{3,7},{4,0},{5,1},{6,2},{7,3},{8,12},{9,13},{10,... | collective-permute-start | bytes 589832 | tf_op jit(solution)/shard_map/ppermute | solution.py:184
  119.9 2.2 %collective-permute-start.26 = (f32[96,512]{1,0:T(8,128)S(1)}, f32[96,512]{1,0:T(8,128)S(1)}, u32[]{:S(2)}, u32[]{:S(2)}) collective-permute-start(f32[96,512]{1,0:T(8,128)S(1)} %add_divide_fusion), channel_id=1, source_target_pairs={{0,3},{1,2},{2,5},{3,4},{4,7},{5,6},{6,1},{7,0},{8,11},{9,10},{10,... | collective-permute-start | bytes 589832 | tf_op jit(solution)/shard_map/ppermute | solution.py:184
  122.1 2.0 %collective-permute-start.27 = (f32[96,512]{1,0:T(8,128)S(1)}, f32[96,512]{1,0:T(8,128)S(1)}, u32[]{:S(2)}, u32[]{:S(2)}) collective-permute-start(f32[96,512]{1,0:T(8,128)S(1)} %add_divide_fusion), channel_id=1, source_target_pairs={{0,7},{1,6},{2,1},{3,0},{4,3},{5,2},{6,5},{7,4},{8,15},{9,14},{10,... | collective-permute-start | bytes 589832 | tf_op jit(solution)/shard_map/ppermute | solution.py:184
  124.1 2.3 %collective-permute-done.24 = f32[96,512]{1,0:T(8,128)S(1)} collective-permute-done((f32[96,512]{1,0:T(8,128)S(1)}, f32[96,512]{1,0:T(8,128)S(1)}, u32[]{:S(2)}, u32[]{:S(2)}) %collective-permute-start.24) | collective-permute-done | bytes 196640 | tf_op jit(solution)/shard_map/ppermute | solution.py:184
  127.5 6.6 %collective-permute-done.25 = f32[96,512]{1,0:T(8,128)S(1)} collective-permute-done((f32[96,512]{1,0:T(8,128)S(1)}, f32[96,512]{1,0:T(8,128)S(1)}, u32[]{:S(2)}, u32[]{:S(2)}) %collective-permute-start.25) | collective-permute-done | bytes 196640 | tf_op jit(solution)/shard_map/ppermute | solution.py:184
  134.7 3.4 %collective-permute-done.28 = f32[96,512]{1,0:T(8,128)S(1)} collective-permute-done((f32[96,512]{1,0:T(8,128)S(1)}, f32[96,512]{1,0:T(8,128)S(1)}, u32[]{:S(2)}, u32[]{:S(2)}) %collective-permute-start.28) | collective-permute-done | bytes 196640 | tf_op jit(solution)/shard_map/ppermute | solution.py:184
  138.1 2.8 %collective-permute-done.30 = f32[96,512]{1,0:T(8,128)S(1)} collective-permute-done((f32[96,512]{1,0:T(8,128)S(1)}, f32[96,512]{1,0:T(8,128)S(1)}, u32[]{:S(2)}, u32[]{:S(2)}) %collective-permute-start.30) | collective-permute-done | bytes 196640 | tf_op jit(solution)/shard_map/ppermute | solution.py:184
  141.0 13.6 %fusion.20 = f32[768,3584]{1,0:T(8,128)} fusion(f32[768,512]{1,0:T(8,128)S(1)} %constant_dynamic-update-slice_fusion.14, f32[3584,512]{1,0:T(8,128)} %copy-done.2), kind=kOutput, calls=%fused_computation.92 | convolution fusion | flops 8455716864 | bytes 19922944 | tf_op jit(solution)/shard_map/dot_general | solution.py:186
  (142 shorter events, 7.7 us)
Async XLA Ops:
  0.0 23.0 %copy-start = (f32[28672]{0:T(1024)S(1)}, f32[28672]{0:T(1024)}, u32[]{:S(2)}) copy-start(f32[28672]{0:T(1024)} %param.11) | copy-start | bytes 344068
  0.0 34.7 %all-to-all-start = ((f32[16,224,128]{2,1,0:T(8,128)}), f32[16,224,128]{2,1,0:T(8,128)}, u32[]{:S(2)}, u32[]{:S(2)}) async-start(f32[16,224,128]{2,1,0:T(8,128)} %bitcast.35), calls=%async_computation | async-start | bytes 3670016 | tf_op jit(solution)/shard_map/all_to_all | solution.py:132
  8.3 11.5 %copy-start.31 = (s32[4,128]{1,0:T(4,128)S(1)}, s32[4,128]{1,0:T(4,128)}, u32[]{:S(2)}) copy-start(s32[4,128]{1,0:T(4,128)} %param.12) | copy-start | bytes 6148
  8.3 11.5 %copy-start.32 = (s32[4,128]{1,0:T(4,128)S(1)}, s32[4,128]{1,0:T(4,128)}, u32[]{:S(2)}) copy-start(s32[4,128]{1,0:T(4,128)} %param.13) | copy-start | bytes 6148
  8.3 11.5 %copy-start.23 = (f32[8192]{0:T(1024)S(1)}, f32[8192]{0:T(1024)}, u32[]{:S(2)}) copy-start(f32[8192]{0:T(1024)} %param.10) | copy-start | bytes 98308
  36.3 1.6 %collective-permute-start = (f32[2,224,128]{2,1,0:T(8,128)S(1)}, f32[2,224,128]{2,1,0:T(8,128)S(1)}, u32[]{:S(2)}, u32[]{:S(2)}) collective-permute-start(f32[2,224,128]{2,1,0:T(8,128)S(1)} %get-tuple-element.43), channel_id=1, source_target_pairs={{0,8},{8,0},{16,24},{24,16},{32,40},{40,32},{48,56},{56,48},{64,72... | collective-permute-start | bytes 688136 | tf_op jit(solution)/shard_map/ppermute | solution.py:137
  37.9 3.8 %copy-start.29 = (f32[224,128]{1,0:T(8,128)}, f32[224,128]{1,0:T(8,128)S(1)}, u32[]{:S(2)}) copy-start(f32[224,128]{1,0:T(8,128)S(1)} %get-tuple-element.81) | copy-start | bytes 344068
  37.9 3.7 %copy-start.30 = (f32[224,128]{1,0:T(8,128)}, f32[224,128]{1,0:T(8,128)S(1)}, u32[]{:S(2)}) copy-start(f32[224,128]{1,0:T(8,128)S(1)} %get-tuple-element.82) | copy-start | bytes 344068
  37.9 10.2 %collective-permute-start.1 = (f32[448,128]{1,0:T(8,128)S(1)}, f32[448,128]{1,0:T(8,128)}, u32[]{:S(2)}, u32[]{:S(2)}) collective-permute-start(f32[448,128]{1,0:T(8,128)S(1)} %pad_maximum_fusion.2), channel_id=1, source_target_pairs={{0,16},{8,24},{16,0},{24,8},{32,48},{40,56},{48,32},{56,40},{64,80... | collective-permute-start | bytes 688136 | tf_op jit(solution)/shard_map/ppermute | solution.py:141
  38.8 13.3 %collective-permute-start.2 = (f32[448,128]{1,0:T(8,128)S(1)}, f32[448,128]{1,0:T(8,128)S(1)}, u32[]{:S(2)}, u32[]{:S(2)}) collective-permute-start(f32[448,128]{1,0:T(8,128)S(1)} %pad_maximum_fusion.3), channel_id=1, source_target_pairs={{0,16},{8,24},{16,0},{24,8},{32,48},{40,56},{48,32},{56,40},{64,80... | collective-permute-start | bytes 688136 | tf_op jit(solution)/shard_map/ppermute | solution.py:141
  49.2 9.8 %collective-permute-start.3 = (f32[896,128]{1,0:T(8,128)S(1)}, f32[896,128]{1,0:T(8,128)S(1)}, u32[]{:S(2)}, u32[]{:S(2)}) collective-permute-start(f32[896,128]{1,0:T(8,128)S(1)} %pad_maximum_fusion), channel_id=1, source_target_pairs={{0,32},{8,104},{16,48},{24,120},{32,64},{40,8},{48,80},{56,24},{64... | collective-permute-start | bytes 1376264 | tf_op jit(solution)/shard_map/ppermute | solution.py:163
  49.3 9.7 %collective-permute-start.5 = (f32[896,128]{1,0:T(8,128)S(1)}, f32[896,128]{1,0:T(8,128)S(1)}, u32[]{:S(2)}, u32[]{:S(2)}) collective-permute-start(f32[896,128]{1,0:T(8,128)S(1)} %pad_maximum_fusion), channel_id=1, source_target_pairs={{0,8},{8,0},{16,24},{24,16},{32,40},{40,32},{48,56},{56,48},{64,72... | collective-permute-start | bytes 1376264 | tf_op jit(solution)/shard_map/ppermute | solution.py:164
  52.2 6.9 %collective-permute-start.9 = (f32[896,128]{1,0:T(8,128)S(1)}, f32[896,128]{1,0:T(8,128)S(1)}, u32[]{:S(2)}, u32[]{:S(2)}) collective-permute-start(f32[896,128]{1,0:T(8,128)S(1)} %pad_maximum_fusion.1), channel_id=1, source_target_pairs={{0,8},{8,0},{16,24},{24,16},{32,40},{40,32},{48,56},{56,48},{64,72... | collective-permute-start | bytes 1376264 | tf_op jit(solution)/shard_map/ppermute | solution.py:164
  52.3 11.7 %collective-permute-start.4 = (f32[896,128]{1,0:T(8,128)S(1)}, f32[896,128]{1,0:T(8,128)S(1)}, u32[]{:S(2)}, u32[]{:S(2)}) collective-permute-start(f32[896,128]{1,0:T(8,128)S(1)} %pad_maximum_fusion.1), channel_id=1, source_target_pairs={{0,32},{8,104},{16,48},{24,120},{32,64},{40,8},{48,80},{56,24},{64... | collective-permute-start | bytes 1376264 | tf_op jit(solution)/shard_map/ppermute | solution.py:163
  59.0 9.8 %collective-permute-start.6 = (f32[896,128]{1,0:T(8,128)S(1)}, f32[896,128]{1,0:T(8,128)S(1)}, u32[]{:S(2)}, u32[]{:S(2)}) collective-permute-start(f32[896,128]{1,0:T(8,128)S(1)} %collective-permute-done.3), channel_id=1, source_target_pairs={{0,32},{8,104},{16,48},{24,120},{32,64},{40,8},{48,80},{56,24},{64... | collective-permute-start | bytes 1376264 | tf_op jit(solution)/shard_map/ppermute | solution.py:163
  59.0 9.8 %collective-permute-start.8 = (f32[896,128]{1,0:T(8,128)S(1)}, f32[896,128]{1,0:T(8,128)S(1)}, u32[]{:S(2)}, u32[]{:S(2)}) collective-permute-start(f32[896,128]{1,0:T(8,128)S(1)} %collective-permute-done.3), channel_id=1, source_target_pairs={{0,8},{8,0},{16,24},{24,16},{32,40},{40,32},{48,56},{56,48},{64,72... | collective-permute-start | bytes 1376264 | tf_op jit(solution)/shard_map/ppermute | solution.py:164
  63.9 10.0 %collective-permute-start.12 = (f32[896,128]{1,0:T(8,128)S(1)}, f32[896,128]{1,0:T(8,128)S(1)}, u32[]{:S(2)}, u32[]{:S(2)}) collective-permute-start(f32[896,128]{1,0:T(8,128)S(1)} %collective-permute-done.4), channel_id=1, source_target_pairs={{0,8},{8,0},{16,24},{24,16},{32,40},{40,32},{48,56},{56,48},{64,72... | collective-permute-start | bytes 1376264 | tf_op jit(solution)/shard_map/ppermute | solution.py:164
  63.9 9.8 %collective-permute-start.7 = (f32[896,128]{1,0:T(8,128)S(1)}, f32[896,128]{1,0:T(8,128)S(1)}, u32[]{:S(2)}, u32[]{:S(2)}) collective-permute-start(f32[896,128]{1,0:T(8,128)S(1)} %collective-permute-done.4), channel_id=1, source_target_pairs={{0,32},{8,104},{16,48},{24,120},{32,64},{40,8},{48,80},{56,24},{64... | collective-permute-start | bytes 1376264 | tf_op jit(solution)/shard_map/ppermute | solution.py:163
  68.8 9.8 %collective-permute-start.10 = (f32[896,128]{1,0:T(8,128)S(1)}, f32[896,128]{1,0:T(8,128)S(1)}, u32[]{:S(2)}, u32[]{:S(2)}) collective-permute-start(f32[896,128]{1,0:T(8,128)S(1)} %collective-permute-done.6), channel_id=1, source_target_pairs={{0,32},{8,104},{16,48},{24,120},{32,64},{40,8},{48,80},{56,24},{64... | collective-permute-start | bytes 1376264 | tf_op jit(solution)/shard_map/ppermute | solution.py:163
  68.8 9.8 %collective-permute-start.13 = (f32[896,128]{1,0:T(8,128)S(1)}, f32[896,128]{1,0:T(8,128)S(1)}, u32[]{:S(2)}, u32[]{:S(2)}) collective-permute-start(f32[896,128]{1,0:T(8,128)S(1)} %collective-permute-done.6), channel_id=1, source_target_pairs={{0,8},{8,0},{16,24},{24,16},{32,40},{40,32},{48,56},{56,48},{64,72... | collective-permute-start | bytes 1376264 | tf_op jit(solution)/shard_map/ppermute | solution.py:164
  73.7 5.0 %collective-permute-start.14 = (f32[896,128]{1,0:T(8,128)S(1)}, f32[896,128]{1,0:T(8,128)S(1)}, u32[]{:S(2)}, u32[]{:S(2)}) collective-permute-start(f32[896,128]{1,0:T(8,128)S(1)} %collective-permute-done.7), channel_id=1, source_target_pairs={{0,8},{8,0},{16,24},{24,16},{32,40},{40,32},{48,56},{56,48},{64,72... | collective-permute-start | bytes 1376264 | tf_op jit(solution)/shard_map/ppermute | solution.py:164
  73.7 9.8 %collective-permute-start.11 = (f32[896,128]{1,0:T(8,128)S(1)}, f32[896,128]{1,0:T(8,128)S(1)}, u32[]{:S(2)}, u32[]{:S(2)}) collective-permute-start(f32[896,128]{1,0:T(8,128)S(1)} %collective-permute-done.7), channel_id=1, source_target_pairs={{0,32},{8,104},{16,48},{24,120},{32,64},{40,8},{48,80},{56,24},{64... | collective-permute-start | bytes 1376264 | tf_op jit(solution)/shard_map/ppermute | solution.py:163
  73.9 7.3 %copy-start.17 = (f32[896,256]{1,0:T(8,128)}, f32[896,256]{1,0:T(8,128)S(1)}, u32[]{:S(2)}) copy-start(f32[896,256]{1,0:T(8,128)S(1)} %constant_dynamic-update-slice_fusion.2.refs_2_) | copy-start | bytes 2752516
  78.7 6.4 %collective-permute-start.15 = (f32[896,128]{1,0:T(8,128)S(1)}, f32[896,128]{1,0:T(8,128)S(1)}, u32[]{:S(2)}, u32[]{:S(2)}) collective-permute-start(f32[896,128]{1,0:T(8,128)S(1)} %collective-permute-done.10), channel_id=1, source_target_pairs={{0,8},{8,0},{16,24},{24,16},{32,40},{40,32},{48,56},{56,48},{64,72... | collective-permute-start | bytes 1376264 | tf_op jit(solution)/shard_map/ppermute | solution.py:164
  83.6 1.8 %collective-permute-start.16 = (f32[896,128]{1,0:T(8,128)S(1)}, f32[896,128]{1,0:T(8,128)S(1)}, u32[]{:S(2)}, u32[]{:S(2)}) collective-permute-start(f32[896,128]{1,0:T(8,128)S(1)} %collective-permute-done.11), channel_id=1, source_target_pairs={{0,8},{8,0},{16,24},{24,16},{32,40},{40,32},{48,56},{56,48},{64,72... | collective-permute-start | bytes 1376264 | tf_op jit(solution)/shard_map/ppermute | solution.py:164
  86.9 16.9 %copy-start.27 = (f32[448,128]{1,0:T(8,128)S(1)}, f32[448,128]{1,0:T(8,128)}, u32[]{:S(2)}) copy-start(f32[448,128]{1,0:T(8,128)} %copy-done.26) | copy-start | bytes 688132
  86.9 17.9 %copy-start.20 = (f32[896,256]{1,0:T(8,128)S(1)}, f32[896,256]{1,0:T(8,128)}, u32[]{:S(2)}) copy-start(f32[896,256]{1,0:T(8,128)} %copy-done.19) | copy-start | bytes 2752516
  86.9 17.9 %copy-start.22 = (f32[896,256]{1,0:T(8,128)S(1)}, f32[896,256]{1,0:T(8,128)}, u32[]{:S(2)}) copy-start(f32[896,256]{1,0:T(8,128)} %copy-done.21) | copy-start | bytes 2752516
  87.8 16.0 %collective-permute-start.22 = (f32[96,512]{1,0:T(8,128)S(1)}, f32[96,512]{1,0:T(8,128)S(1)}, u32[]{:S(2)}, u32[]{:S(2)}) collective-permute-start(f32[96,512]{1,0:T(8,128)S(1)} %get-tuple-element.76), channel_id=1, source_target_pairs={{0,6},{1,7},{2,0},{3,1},{4,2},{5,3},{6,4},{7,5},{8,14},{9,15},{10,... | collective-permute-start | bytes 589832 | tf_op jit(solution)/shard_map/ppermute | solution.py:179
  90.8 13.0 %collective-permute-start.23 = (f32[96,512]{1,0:T(8,128)S(1)}, f32[96,512]{1,0:T(8,128)}, u32[]{:S(2)}, u32[]{:S(2)}) collective-permute-start(f32[96,512]{1,0:T(8,128)S(1)} %get-tuple-element.75), channel_id=1, source_target_pairs={{0,1},{1,0},{2,3},{3,2},{4,5},{5,4},{6,7},{7,6},{8,9},{9,8},{10,11... | collective-permute-start | bytes 589832 | tf_op jit(solution)/shard_map/ppermute | solution.py:179
  91.4 13.4 %copy-start.14 = (f32[896,256]{1,0:T(8,128)S(1)}, f32[896,256]{1,0:T(8,128)}, u32[]{:S(2)}) copy-start(f32[896,256]{1,0:T(8,128)} %copy-done.13) | copy-start | bytes 2752516
  91.4 13.4 %copy-start.16 = (f32[896,256]{1,0:T(8,128)S(1)}, f32[896,256]{1,0:T(8,128)}, u32[]{:S(2)}) copy-start(f32[896,256]{1,0:T(8,128)} %copy-done.15) | copy-start | bytes 2752516
  91.4 13.5 %copy-start.18 = (f32[896,256]{1,0:T(8,128)S(1)}, f32[896,256]{1,0:T(8,128)}, u32[]{:S(2)}) copy-start(f32[896,256]{1,0:T(8,128)} %copy-done.17) | copy-start | bytes 2752516
  93.0 11.9 %copy-start.10 = (f32[896,256]{1,0:T(8,128)S(1)}, f32[896,256]{1,0:T(8,128)}, u32[]{:S(2)}) copy-start(f32[896,256]{1,0:T(8,128)} %copy-done.9) | copy-start | bytes 2752516
  93.0 11.9 %copy-start.12 = (f32[896,256]{1,0:T(8,128)S(1)}, f32[896,256]{1,0:T(8,128)}, u32[]{:S(2)}) copy-start(f32[896,256]{1,0:T(8,128)} %copy-done.11) | copy-start | bytes 2752516
  93.0 16.5 %collective-permute-start.17 = (f32[96,512]{1,0:T(8,128)S(1)}, f32[96,512]{1,0:T(8,128)S(1)}, u32[]{:S(2)}, u32[]{:S(2)}) collective-permute-start(f32[96,512]{1,0:T(8,128)S(1)} %get-tuple-element.70), channel_id=1, source_target_pairs={{0,5},{1,4},{2,7},{3,6},{4,1},{5,0},{6,3},{7,2},{8,13},{9,12},{10,... | collective-permute-start | bytes 589832 | tf_op jit(solution)/shard_map/ppermute | solution.py:179
  94.6 16.2 %collective-permute-start.18 = (f32[96,512]{1,0:T(8,128)S(1)}, f32[96,512]{1,0:T(8,128)S(1)}, u32[]{:S(2)}, u32[]{:S(2)}) collective-permute-start(f32[96,512]{1,0:T(8,128)S(1)} %get-tuple-element.71), channel_id=1, source_target_pairs={{0,4},{1,5},{2,6},{3,7},{4,0},{5,1},{6,2},{7,3},{8,12},{9,13},{10,... | collective-permute-start | bytes 589832 | tf_op jit(solution)/shard_map/ppermute | solution.py:179
  97.5 13.3 %collective-permute-start.19 = (f32[96,512]{1,0:T(8,128)S(1)}, f32[96,512]{1,0:T(8,128)S(1)}, u32[]{:S(2)}, u32[]{:S(2)}) collective-permute-start(f32[96,512]{1,0:T(8,128)S(1)} %get-tuple-element.72), channel_id=1, source_target_pairs={{0,3},{1,2},{2,5},{3,4},{4,7},{5,6},{6,1},{7,0},{8,11},{9,10},{10,... | collective-permute-start | bytes 589832 | tf_op jit(solution)/shard_map/ppermute | solution.py:179
  103.8 7.0 %collective-permute-start.20 = (f32[96,512]{1,0:T(8,128)S(1)}, f32[96,512]{1,0:T(8,128)S(1)}, u32[]{:S(2)}, u32[]{:S(2)}) collective-permute-start(f32[96,512]{1,0:T(8,128)S(1)} %get-tuple-element.73), channel_id=1, source_target_pairs={{0,7},{1,6},{2,1},{3,0},{4,3},{5,2},{6,5},{7,4},{8,15},{9,14},{10,... | collective-permute-start | bytes 589832 | tf_op jit(solution)/shard_map/ppermute | solution.py:179
  103.8 11.1 %collective-permute-start.21 = (f32[96,512]{1,0:T(8,128)S(1)}, f32[96,512]{1,0:T(8,128)S(1)}, u32[]{:S(2)}, u32[]{:S(2)}) collective-permute-start(f32[96,512]{1,0:T(8,128)S(1)} %get-tuple-element.74), channel_id=1, source_target_pairs={{0,2},{1,3},{2,4},{3,5},{4,6},{5,7},{6,0},{7,1},{8,10},{9,11},{10,... | collective-permute-start | bytes 589832 | tf_op jit(solution)/shard_map/ppermute | solution.py:179
  116.0 10.4 %collective-permute-start.24 = (f32[96,512]{1,0:T(8,128)S(1)}, f32[96,512]{1,0:T(8,128)S(1)}, u32[]{:S(2)}, u32[]{:S(2)}) collective-permute-start(f32[96,512]{1,0:T(8,128)S(1)} %add_divide_fusion), channel_id=1, source_target_pairs={{0,5},{1,4},{2,7},{3,6},{4,1},{5,0},{6,3},{7,2},{8,13},{9,12},{10,... | collective-permute-start | bytes 589832 | tf_op jit(solution)/shard_map/ppermute | solution.py:184
  118.3 15.9 %collective-permute-start.25 = (f32[96,512]{1,0:T(8,128)S(1)}, f32[96,512]{1,0:T(8,128)S(1)}, u32[]{:S(2)}, u32[]{:S(2)}) collective-permute-start(f32[96,512]{1,0:T(8,128)S(1)} %add_divide_fusion), channel_id=1, source_target_pairs={{0,4},{1,5},{2,6},{3,7},{4,0},{5,1},{6,2},{7,3},{8,12},{9,13},{10,... | collective-permute-start | bytes 589832 | tf_op jit(solution)/shard_map/ppermute | solution.py:184
  119.9 14.7 %collective-permute-start.26 = (f32[96,512]{1,0:T(8,128)S(1)}, f32[96,512]{1,0:T(8,128)S(1)}, u32[]{:S(2)}, u32[]{:S(2)}) collective-permute-start(f32[96,512]{1,0:T(8,128)S(1)} %add_divide_fusion), channel_id=1, source_target_pairs={{0,3},{1,2},{2,5},{3,4},{4,7},{5,6},{6,1},{7,0},{8,11},{9,10},{10,... | collective-permute-start | bytes 589832 | tf_op jit(solution)/shard_map/ppermute | solution.py:184
  122.1 12.5 %collective-permute-start.27 = (f32[96,512]{1,0:T(8,128)S(1)}, f32[96,512]{1,0:T(8,128)S(1)}, u32[]{:S(2)}, u32[]{:S(2)}) collective-permute-start(f32[96,512]{1,0:T(8,128)S(1)} %add_divide_fusion), channel_id=1, source_target_pairs={{0,7},{1,6},{2,1},{3,0},{4,3},{5,2},{6,5},{7,4},{8,15},{9,14},{10,... | collective-permute-start | bytes 589832 | tf_op jit(solution)/shard_map/ppermute | solution.py:184
  124.1 13.9 %collective-permute-start.28 = (f32[96,512]{1,0:T(8,128)S(1)}, f32[96,512]{1,0:T(8,128)S(1)}, u32[]{:S(2)}, u32[]{:S(2)}) collective-permute-start(f32[96,512]{1,0:T(8,128)S(1)} %add_divide_fusion), channel_id=1, source_target_pairs={{0,2},{1,3},{2,4},{3,5},{4,6},{5,7},{6,0},{7,1},{8,10},{9,11},{10,... | collective-permute-start | bytes 589832 | tf_op jit(solution)/shard_map/ppermute | solution.py:184
  126.4 11.6 %collective-permute-start.29 = (f32[96,512]{1,0:T(8,128)S(1)}, f32[96,512]{1,0:T(8,128)S(1)}, u32[]{:S(2)}, u32[]{:S(2)}) collective-permute-start(f32[96,512]{1,0:T(8,128)S(1)} %add_divide_fusion), channel_id=1, source_target_pairs={{0,6},{1,7},{2,0},{3,1},{4,2},{5,3},{6,4},{7,5},{8,14},{9,15},{10,... | collective-permute-start | bytes 589832 | tf_op jit(solution)/shard_map/ppermute | solution.py:184
  134.2 6.7 %collective-permute-start.30 = (f32[96,512]{1,0:T(8,128)S(1)}, f32[96,512]{1,0:T(8,128)S(1)}, u32[]{:S(2)}, u32[]{:S(2)}) collective-permute-start(f32[96,512]{1,0:T(8,128)S(1)} %add_divide_fusion), channel_id=1, source_target_pairs={{0,1},{1,0},{2,3},{3,2},{4,5},{5,4},{6,7},{7,6},{8,9},{9,8},{10,11... | collective-permute-start | bytes 589832 | tf_op jit(solution)/shard_map/ppermute | solution.py:184
  141.0 13.6 %copy-start.1 = (f32[28672]{0:T(1024)S(1)}, f32[28672]{0:T(1024)}, u32[]{:S(2)}) copy-start(f32[28672]{0:T(1024)} %param.11) | copy-start | bytes 344068
  (18 other events, 32.9 us)

commit v4 on v2

--- a/solution.py
+++ b/solution.py
@@ -15,7 +15,6 @@
 
 
 CORE = [(r, r ^ 1) for r in range(16)]
-CHIPS = [[r for r in range(16) if r % 2 == core] for core in range(2)]
 XPAIR = [(r, r ^ 2) for r in range(16)]
 RING = [(r, ((r // 4 + (1 if r % 2 == 0 else 3)) % 4) * 4 + r % 4) for r in range(16)]
 
@@ -35,11 +34,12 @@
 
 
 def rotate_body(at_ref, *refs):
-    for i in range(PLANES):
-        refs[PLANES + i][...] = refs[i][...]
-
-
-def rotate(at, gradient, tile=96):
+    count = len(refs) // 2
+    for i in range(count):
+        refs[count + i][...] = refs[i][...]
+
+
+def rotate(at, gradient, steps, tile=96):
     rows, width = gradient.shape
     quarter = width // PLANES
     spec = lambda i: pl.BlockSpec((tile, quarter), lambda r, at_ref: (r, at_ref[i]))
@@ -48,34 +48,41 @@
         grid_spec=pltpu.PrefetchScalarGridSpec(
             num_scalar_prefetch=1,
             grid=(rows // tile,),
-            in_specs=[spec(i) for i in range(PLANES)],
-            out_specs=[pl.BlockSpec((tile, quarter), lambda r, at_ref: (r, 0))] * PLANES,
+            in_specs=[spec(i) for i in steps],
+            out_specs=[pl.BlockSpec((tile, quarter), lambda r, at_ref: (r, 0))] * len(steps),
         ),
-        out_shape=[jax.ShapeDtypeStruct((rows, quarter), F32)] * PLANES,
+        out_shape=[jax.ShapeDtypeStruct((rows, quarter), F32)] * len(steps),
         compiler_params=pltpu.CompilerParams(vmem_limit_bytes=16 << 20),
-        cost_estimate=pl.CostEstimate(flops=1, bytes_accessed=rows * width * 8, transcendentals=0),
+        cost_estimate=pl.CostEstimate(flops=1, bytes_accessed=rows * quarter * 8 * len(steps), transcendentals=0),
         name="rotate",
-    )(at, *[stay(gradient)] * PLANES)
-
-
-def pick_body(at_ref, pieces_ref, mine_ref, give_ref):
-    core = at_ref[NSEL]
+    )(at, *[stay(gradient)] * len(steps))
+
+
+def pick_body(at_ref, *refs):
+    pieces, (mine_ref, give_ref) = refs[:-2], refs[-2:]
+    core, z, x = at_ref[NSEL], at_ref[NSEL + 1], at_ref[NSEL + 2]
     for i in range(2):
-        mine_ref[i] = pieces_ref[at_ref[2 * core + i] // 2]
-        give_ref[i] = pieces_ref[at_ref[2 - 2 * core + i] // 2]
+        for out, slot in ((mine_ref, 2 * core + i), (give_ref, 2 - 2 * core + i)):
+            panel = at_ref[slot]
+            came = ((z + PLANES - panel // 4) % PLANES) * 2 + (x + panel // 2) % 2
+            for j, piece in enumerate(pieces):
+
+                @pl.when(came == j)
+                def _():
+                    out[i] = piece[...]
 
 
 def pick(at, pieces):
-    two = jax.ShapeDtypeStruct((2, *pieces.shape[1:]), F32)
+    two = jax.ShapeDtypeStruct((2, *pieces[0].shape), F32)
     return pl.pallas_call(
         pick_body,
         out_shape=[two, two],
-        in_specs=[SM, VM],
+        in_specs=[SM] + [VM] * len(pieces),
         out_specs=[VM] * 2,
         compiler_params=pltpu.CompilerParams(vmem_limit_bytes=8 << 20),
-        cost_estimate=pl.CostEstimate(flops=1, bytes_accessed=pieces.size, transcendentals=0),
+        cost_estimate=pl.CostEstimate(flops=1, bytes_accessed=pieces[0].size * 32, transcendentals=0),
         name="pick",
-    )(at, pieces)
+    )(at, *pieces)
 
 
 def settle_body(at_ref, mine_ref, got_ref, *outs):
@@ -125,21 +132,31 @@
     return pl.pallas_call(
         place_body,
         out_shape=pltpu.VMEM((PLANES * quarter, 2 * PAIR), F32),
-        in_specs=[SM] + [VM] * (2 * PLANES),
+        in_specs=[SM] + [HBM] * (2 * PLANES),
         out_specs=VM,
         scratch_shapes=[pltpu.SemaphoreType.DMA((2, PLANES))],
         compiler_params=pltpu.CompilerParams(vmem_limit_bytes=8 << 20),
         cost_estimate=pl.CostEstimate(flops=1, bytes_accessed=quarter * PAIR * 64, transcendentals=0),
         name="place",
-    )(at, *own, *oth)
+    )(at, *[stay(v) for v in (*own, *oth)])
 
 
 def dot(a, b):
     return jnp.dot(a, b, precision=lax.Precision.HIGH, preferred_element_type=F32)
 
 
+def away(dz, dx):
+    return [(r, ((r // 4 + dz) % 4) * 4 + ((r // 2 % 2) ^ dx) * 2 + r % 2) for r in range(16)]
+
+
+SPREAD = ((2, 1), (2, 0), (1, 1), (3, 1), (0, 1), (1, 0), (3, 0))
+
+
 def across(dy, dx):
     return [(c, ((c // 2 + dy) % 4) * 2 + (c % 2 ^ dx)) for c in range(COLS)]
+
+
+TURNS = ((2, 1), (2, 0), (1, 1), (3, 1), (1, 0), (3, 0), (0, 1), (0, 0))
 
 
 def shards(gradient, basis, panel_index, input_eigen, output_eigen, input_pick, output_pick):
@@ -152,21 +169,28 @@
     damped = (input_eigen[input_pick] * output_eigen[output_pick] + 0.05).reshape(-1)
     damped = jnp.where(even, damped, jnp.roll(damped, PAIR))
 
-    pieces = lax.all_to_all(basis.reshape(8, -1, PANEL), "rows", 0, 0, axis_index_groups=CHIPS)
     at = jnp.arange(PLANES, dtype=jnp.int32) * way.astype(jnp.int32)
     at = jnp.concatenate([(z - at + 4) % 4, (z + at + 4) % 4])
-    pieces, *g = lax.optimization_barrier((pieces, *rotate(at, gradient)))
-    chosen = jnp.append(panel_index, core).astype(jnp.int32)
+
+    deep = basis.shape[1] // (2 * PLANES)
+    eighth = lambda dz, dx: lax.dynamic_slice(
+        basis[0], ((((z + dz) % 4) * 2 + (x ^ dx)) * deep, 0), (deep, PANEL))
+    arrived = {(0, 0): eighth(0, 0)}
+    for dz, dx in SPREAD:
+        arrived[dz, dx] = lax.ppermute(eighth(dz, dx), "rows", away(dz, dx))
+    pieces = [arrived[dz, dx] for dz in range(PLANES) for dx in range(2)]
+    g = rotate(at, gradient, (0, 1))
+    *pieces, g0, g1 = lax.optimization_barrier((*pieces, *g))
+    chosen = jnp.concatenate([panel_index, jnp.stack([core, z, x]).astype(jnp.int32)])
     mine, give = pick(chosen, pieces)
-    half_a, half_b = settle(chosen, mine, lax.ppermute(give, "rows", CORE))
-
-    def other_x(half):
-        return ordered(x == 0, half, lax.ppermute(half, "rows", XPAIR))
-
-    own, halves = [[other_x(half_a)], []], [half_b]
-    for step in range(PLANES - 1):
-        halves.append(lax.ppermute(halves[step], "rows", RING))
-    own[1] = [other_x(half) for half in halves]
+    halves = settle(chosen, mine, lax.ppermute(give, "rows", CORE))
+    own = [[], []]
+    for c, half in enumerate(halves):
+        own[c].append(ordered(x == 0, half, lax.ppermute(half, "rows", XPAIR)))
+
+    g = rotate(at, gradient, (2, 3))
+    own[0][0], g2, g3 = lax.optimization_barrier((own[0][0], *g))
+    g = [g0, g1, g2, g3]
 
     v_own, v_oth, total, waiting = [], [], None, None
 
@@ -187,8 +211,10 @@
                     held, last_oth[0], *total = lax.optimization_barrier((held, last_oth[0], *total))
                 else:
                     held, last_oth[0] = lax.optimization_barrier((held, last_oth[0]))
-            if c == 0 and step < PLANES - 1:
+            if step < PLANES - 1:
                 own[c].append(lax.ppermute(held, "rows", RING))
+                if (c, step) == (0, 0):
+                    own[0][1], damped = lax.optimization_barrier((own[0][1], damped))
             oth[c] = lax.ppermute(held, "rows", CORE)
         if waiting is not None:
             total = product(*waiting, total)
@@ -199,16 +225,15 @@
 
     mine = lax.axis_index("cols")
     block = rows // COLS
-    turns = [(dy, dx) for dy in (2, 1, 3, 0) for dx in (1, 0)]
-    there = [((mine // 2 + dy) % 4) * 2 + (mine % 2 ^ dx) for dy, dx in turns]
-    back = [((mine // 2 - dy) % 4) * 2 + (mine % 2 ^ dx) for dy, dx in turns]
+    there = [((mine // 2 + dy) % 4) * 2 + (mine % 2 ^ dx) for dy, dx in TURNS]
+    back = [((mine // 2 - dy) % 4) * 2 + (mine % 2 ^ dx) for dy, dx in TURNS]
     sums = []
-    for at_rows, turn in zip(there, turns):
+    for at_rows, turn in zip(there, TURNS):
         part = lax.dynamic_slice(p, (at_rows * block, 0), (block, NSEL * PANEL))
         sums.append(part if turn == (0, 0) else lax.ppermute(part, "cols", across(*turn)))
     scaled_block = sum(sums[1:], sums[0]) / damped[None, :]
     scaled = jnp.zeros((rows, NSEL * PANEL), F32)
-    for at_rows, turn in zip(back, turns):
+    for at_rows, turn in zip(back, TURNS):
         part = scaled_block if turn == (0, 0) else lax.ppermute(scaled_block, "cols", across(*turn))
         scaled = lax.dynamic_update_slice(scaled, part, (at_rows * block, 0))
     return lax.dot_general(

time: 169 us -> 172 us (1.018)
  waiting for transfers between devices: 65.7 us -> 46.5 us
  starting transfers between devices: 40.2 us -> 55.5 us
  Pallas kernels: 12.8 us -> 18.5 us
  local copies, waits for them, and re-layouts: 19.7 us -> 23.1 us
  other arithmetic: 6.02 us -> 4.18 us
    ppermute x9 -> x10, waiting for transfers between devices: 27 us -> 11.3 us  [the longest x7 6.91 us: shards(): arrived[dz, dx] = lax.ppermute(eighth(dz, dx), 'rows', away(dz, dx))]
    all_to_all x1 -> x0, waiting for transfers between devices: 14.1 us -> none  [shards(): lax.all_to_all(basis.reshape(8, -1, PANEL), 'rows', 0, 0, axis_index_grou...]
    ppermute x9 -> x10, starting transfers between devices: 8.59 us -> 20.9 us  [the longest x7 14.3 us: shards(): arrived[dz, dx] = lax.ppermute(eighth(dz, dx), 'rows', away(dz, dx))]
    all_to_all x1 -> x0, starting transfers between devices: 8.02 us -> none  [shards(): lax.all_to_all(basis.reshape(8, -1, PANEL), 'rows', 0, 0, axis_index_grou...]
    ppermute x3 -> x6, waiting for transfers between devices: 3.5 us -> 11.5 us  [shards(): own[c].append(lax.ppermute(held, 'rows', RING))]
    ppermute x8, starting transfers between devices: 1.85 us -> 8.33 us  [shards(): oth[c] = lax.ppermute(held, 'rows', CORE)]
    pallas_call x1 -> x2, Pallas kernels: 6.89 us -> 11 us  [rotate(): pl.pallas_call(rotate_body, grid_spec=pltpu.PrefetchScalarGridSpec(num_sc...]
    ppermute x3 -> x6, starting transfers between devices: 0.23 us -> 3.88 us  [shards(): own[c].append(lax.ppermute(held, 'rows', RING))]
  transfers between devices with their start and end apart: 35 -> 38, of which waited for: 17 -> 17; matrix products, arithmetic and copies ran while one was open for 13% -> 12% of each run, Pallas kernels for 5% -> 9%
where the time goes in v4:
time: 172 us
  starting transfers between devices  55.5 us (32%)
  waiting for transfers between devices  46.5 us (27%)
  matrix products  23.2 us (13%)
  local copies, waits for them, and re-layouts  23.1 us (13%)
  Pallas kernels  18.5 us (11%)
  other arithmetic  4.18 us (2%)
    ppermute x7, waiting for transfers between devices, shards(): lax.ppermute(part, 'cols', across(*turn))  15.5 us
    ppermute x7, starting transfers between devices, shards(): arrived[dz, dx] = lax.ppermute(eighth(dz, dx), 'rows', away(dz, dx))  14.3 us
    unnamed x81, local copies, waits for them, and re-layouts  13.2 us
    dot_general x1, matrix products, shards(): lax.dot_general(scaled, v, (((1,), (1,)), ((), ())), precision=lax.Precis...  11.8 us
    ppermute x6, waiting for transfers between devices, shards(): own[c].append(lax.ppermute(held, 'rows', RING))  11.5 us
    ppermute x7, starting transfers between devices, shards(): lax.ppermute(scaled_block, 'cols', across(*turn))  11.4 us
    dot_general x8, matrix products, dot(): jnp.dot(a, b, precision=lax.Precision.HIGH, preferred_element_type=F32)  11.4 us
    pallas_call x2, Pallas kernels, rotate(): pl.pallas_call(rotate_body, grid_spec=pltpu.PrefetchScalarGridSpec(num_sc...  11 us
  transfers between devices with their start and end apart: 38, of which 17 were waited for; matrix products, arithmetic and copies ran while one was open for 12% of the time, Pallas kernels for 9%

profile of v4, /device:TPU:0, one launch (start us, length us, event | category | flops | bytes accessed | tf_op | source)
XLA Modules:
  0.0 171.7 jit_solution(14431783288703792514)
XLA Ops:
  0.0 2.6 %dynamic-slice_bitcast_fusion = (f32[448,128]{1,0:T(8,128)}, f32[448,128]{1,0:T(8,128)}, f32[448,128]{1,0:T(8,128)}, f32[448,128]{1,0:T(8,128)}, f32[448,128]{1,...) fusion(f32[1,3584,128]{2,1,0:T(8,128)} %param.8, s32[]{:T(128)S(6)} %select_n.272, ...), kind=kLoop, calls=%fused_computation.26 | loop fusion | bytes 3670048 | tf_op jit(solution)/shard_map/dynamic_slice | solution.py:176
  2.6 3.2 %collective-permute-start = (f32[448,128]{1,0:T(8,128)S(1)}, f32[448,128]{1,0:T(8,128)S(1)}, u32[]{:S(2)}, u32[]{:S(2)}) collective-permute-start(f32[448,128]{1,0:T(8,128)S(1)} %get-tuple-element.76), channel_id=1, source_target_pairs={{0,16},{8,24},{16,0},{24,8},{32,48},{40,56},{48,32},{56,40},{64,80... | collective-permute-start | bytes 688136 | tf_op jit(solution)/shard_map/ppermute | solution.py:180
  5.8 1.9 %collective-permute-start.1 = (f32[448,128]{1,0:T(8,128)S(1)}, f32[448,128]{1,0:T(8,128)S(1)}, u32[]{:S(2)}, u32[]{:S(2)}) collective-permute-start(f32[448,128]{1,0:T(8,128)S(1)} %get-tuple-element.75), channel_id=1, source_target_pairs={{0,32},{8,40},{16,48},{24,56},{32,64},{40,72},{48,80},{56,88},{64,... | collective-permute-start | bytes 688136 | tf_op jit(solution)/shard_map/ppermute | solution.py:180
  7.7 1.9 %collective-permute-start.2 = (f32[448,128]{1,0:T(8,128)}, f32[448,128]{1,0:T(8,128)S(1)}, u32[]{:S(2)}, u32[]{:S(2)}) collective-permute-start(f32[448,128]{1,0:T(8,128)} %get-tuple-element.74), channel_id=1, source_target_pairs={{0,48},{8,56},{16,32},{24,40},{32,80},{40,88},{48,64},{56,72},{64,... | collective-permute-start | bytes 688136 | tf_op jit(solution)/shard_map/ppermute | solution.py:180
  9.6 1.7 %collective-permute-start.3 = (f32[448,128]{1,0:T(8,128)}, f32[448,128]{1,0:T(8,128)S(1)}, u32[]{:S(2)}, u32[]{:S(2)}) collective-permute-start(f32[448,128]{1,0:T(8,128)} %get-tuple-element.73), channel_id=1, source_target_pairs={{0,64},{8,72},{16,80},{24,88},{32,96},{40,104},{48,112},{56,120},{... | collective-permute-start | bytes 688136 | tf_op jit(solution)/shard_map/ppermute | solution.py:180
  11.3 4.3 %collective-permute-start.4 = (f32[448,128]{1,0:T(8,128)}, f32[448,128]{1,0:T(8,128)}, u32[]{:S(2)}, u32[]{:S(2)}) collective-permute-start(f32[448,128]{1,0:T(8,128)} %get-tuple-element.72), channel_id=1, source_target_pairs={{0,80},{8,88},{16,64},{24,72},{32,112},{40,120},{48,96},{56,104},{... | collective-permute-start | bytes 688136 | tf_op jit(solution)/shard_map/ppermute | solution.py:180
  17.6 6.9 %collective-permute-done.1.refs_2_ = f32[448,128]{1,0:T(8,128)S(1)} collective-permute-done((f32[448,128]{1,0:T(8,128)S(1)}, f32[448,128]{1,0:T(8,128)S(1)}, u32[]{:S(2)}, u32[]{:S(2)}) %collective-permute-start.1) | collective-permute-done | bytes 229408 | tf_op jit(solution)/shard_map/ppermute | solution.py:180
  25.3 5.5 %rotate.2 = (f32[768,896]{1,0:T(8,128)S(1)}, f32[768,896]{1,0:T(8,128)S(1)}) custom-call(s32[8]{0:T(128)S(1)} %pad_add_fusion.1.at_ref, f32[768,3584]{1,0:T(8,128)} %refs_1_.3, f32[768,3584]{1,0:T(8,128)} %refs_1_.3), custom_call_target="tpu_custom_call" | custom-call | flops 1 | bytes 11010048 | tf_op jit(solution)/shard_map/rotate/pallas_call | solution.py:46
  30.8 1.5 copy-done.4
  36.3 2.0 %pick.1 = (f32[2,448,128]{2,1,0:T(8,128)S(1)}, f32[2,448,128]{2,1,0:T(8,128)}) custom-call(s32[7]{0:T(128)S(1)} %pad_add_fusion.at_ref, f32[448,128]{1,0:T(8,128)S(1)} %get-tuple-element.40.refs_0_, f32[448,128]{1,0:T(8,128)S(1)} %copy-done.9, f32[448,128]{1,0:T(8,128)S(1)} %copy-done.11, f32[448,128]{1,0:T(8,128)S(1)} %copy-done.13, ...), custom_call_target="tpu_custom_call" | custom-call | flops 1 | bytes 1835008 | tf_op jit(solution)/shard_map/pick/pallas_call | solution.py:77
  38.3 3.6 %gather_fusion = f32[512]{0:T(512)S(1)} fusion(f32[8192]{0:T(1024)} %param.10, s32[1024]{0:T(1024)} %pad_clamp_fusion.1), kind=kCustom, calls=%fused_computation | custom fusion | bytes 6144 | tf_op jit(solution)/shard_map/gather | solution.py:169
  41.9 3.1 %gather_fusion.1 = f32[512]{0:T(512)S(1)} fusion(f32[28672]{0:T(1024)S(1)} %copy-done, s32[1024]{0:T(1024)S(1)} %pad_clamp_fusion), kind=kCustom, calls=%fused_computation.1 | custom fusion | bytes 6144 | tf_op jit(solution)/shard_map/gather | solution.py:169
  45.8 1.8 %settle.1 = (f32[448,128]{1,0:T(8,128)}, f32[448,128]{1,0:T(8,128)S(1)}) custom-call(s32[7]{0:T(128)S(1)} %copy-done.20, f32[2,448,128]{2,1,0:T(8,128)S(1)} %get-tuple-element.48.mine_ref, f32[2,448,128]{2,1,0:T(8,128)} %collective-permute-done.7.got_ref), custom_call_target="tpu_custom_call" | custom-call | flops 1 | bytes 917504 | tf_op jit(solution)/shard_map/settle/pallas_call | solution.py:104
  47.6 6.7 %collective-permute-start.8 = (f32[448,128]{1,0:T(8,128)}, f32[448,128]{1,0:T(8,128)S(1)}, u32[]{:S(2)}, u32[]{:S(2)}) collective-permute-start(f32[448,128]{1,0:T(8,128)} %get-tuple-element.50), channel_id=1, source_target_pairs={{0,16},{8,24},{16,0},{24,8},{32,48},{40,56},{48,32},{56,40},{64,80... | collective-permute-start | bytes 688136 | tf_op jit(solution)/shard_map/ppermute | solution.py:189
  54.9 5.5 %rotate.3 = (f32[768,896]{1,0:T(8,128)S(1)}, f32[768,896]{1,0:T(8,128)S(1)}) custom-call(s32[8]{0:T(128)S(1)} %copy-done.17, f32[768,3584]{1,0:T(8,128)} %refs_1_.3, f32[768,3584]{1,0:T(8,128)} %refs_1_.3), custom_call_target="tpu_custom_call" | custom-call | flops 1 | bytes 11010048 | tf_op jit(solution)/shard_map/rotate/pallas_call | solution.py:46
  60.4 1.5 copy-done.2
  61.8 1.6 copy-done.6
  65.9 2.4 %collective-permute-start.10 = (f32[896,128]{1,0:T(8,128)S(1)}, f32[896,128]{1,0:T(8,128)S(1)}, u32[]{:S(2)}, u32[]{:S(2)}) collective-permute-start(f32[896,128]{1,0:T(8,128)S(1)} %pad_maximum_fusion), channel_id=1, source_target_pairs={{0,8},{8,0},{16,24},{24,16},{32,40},{40,32},{48,56},{56,48},{64,72... | collective-permute-start | bytes 1376264 | tf_op jit(solution)/shard_map/ppermute | solution.py:218
  68.3 4.4 %collective-permute-done.13 = f32[448,128]{1,0:T(8,128)S(1)} collective-permute-done((f32[448,128]{1,0:T(8,128)S(1)}, f32[448,128]{1,0:T(8,128)S(1)}, u32[]{:S(2)}, u32[]{:S(2)}) %collective-permute-start.13) | collective-permute-done | bytes 229408 | tf_op jit(solution)/shard_map/ppermute | solution.py:189
  72.9 1.4 fusion.14
  74.8 2.4 %collective-permute-start.11 = (f32[896,128]{1,0:T(8,128)S(1)}, f32[896,128]{1,0:T(8,128)S(1)}, u32[]{:S(2)}, u32[]{:S(2)}) collective-permute-start(f32[896,128]{1,0:T(8,128)S(1)} %collective-permute-done.9), channel_id=1, source_target_pairs={{0,32},{8,104},{16,48},{24,120},{32,64},{40,8},{48,80},{56,24},{64... | collective-permute-start | bytes 1376264 | tf_op jit(solution)/shard_map/ppermute | solution.py:215
  80.1 3.1 %collective-permute-done.17 = f32[896,128]{1,0:T(8,128)S(1)} collective-permute-done((f32[896,128]{1,0:T(8,128)S(1)}, f32[896,128]{1,0:T(8,128)S(1)}, u32[]{:S(2)}, u32[]{:S(2)}) %collective-permute-start.17) | collective-permute-done | bytes 458784 | tf_op jit(solution)/shard_map/ppermute | solution.py:215
  83.2 1.4 fusion.17
  84.7 3.4 %collective-permute-done.11 = f32[896,128]{1,0:T(8,128)S(1)} collective-permute-done((f32[896,128]{1,0:T(8,128)S(1)}, f32[896,128]{1,0:T(8,128)S(1)}, u32[]{:S(2)}, u32[]{:S(2)}) %collective-permute-start.11) | collective-permute-done | bytes 458784 | tf_op jit(solution)/shard_map/ppermute | solution.py:215
  88.1 2.2 %collective-permute-start.16 = (f32[896,128]{1,0:T(8,128)S(1)}, f32[896,128]{1,0:T(8,128)S(1)}, u32[]{:S(2)}, u32[]{:S(2)}) collective-permute-start(f32[896,128]{1,0:T(8,128)S(1)} %collective-permute-done.11), channel_id=1, source_target_pairs={{0,8},{8,0},{16,24},{24,16},{32,40},{40,32},{48,56},{56,48},{64,72... | collective-permute-start | bytes 1376264 | tf_op jit(solution)/shard_map/ppermute | solution.py:218
  90.4 2.6 %collective-permute-done.19 = f32[896,128]{1,0:T(8,128)S(1)} collective-permute-done((f32[896,128]{1,0:T(8,128)S(1)}, f32[896,128]{1,0:T(8,128)S(1)}, u32[]{:S(2)}, u32[]{:S(2)}) %collective-permute-start.19) | collective-permute-done | bytes 458784 | tf_op jit(solution)/shard_map/ppermute | solution.py:215
  93.0 2.2 %collective-permute-start.21 = (f32[896,128]{1,0:T(8,128)S(1)}, f32[896,128]{1,0:T(8,128)S(1)}, u32[]{:S(2)}, u32[]{:S(2)}) collective-permute-start(f32[896,128]{1,0:T(8,128)S(1)} %collective-permute-done.19), channel_id=1, source_target_pairs={{0,8},{8,0},{16,24},{24,16},{32,40},{40,32},{48,56},{56,48},{64,72... | collective-permute-start | bytes 1376264 | tf_op jit(solution)/shard_map/ppermute | solution.py:218
  95.4 1.9 %copy-done.7 = f32[768,896]{1,0:T(8,128)S(1)} copy-done((f32[768,896]{1,0:T(8,128)S(1)}, f32[768,896]{1,0:T(8,128)}, u32[]{:S(2)}) %copy-start.7) | copy-done | bytes 2752536
  97.4 1.4 convolution_add_fusion.4
  99.5 1.4 convolution_add_fusion.3
  100.9 2.0 %collective-permute-done.20 = f32[896,128]{1,0:T(8,128)S(1)} collective-permute-done((f32[896,128]{1,0:T(8,128)S(1)}, f32[896,128]{1,0:T(8,128)S(1)}, u32[]{:S(2)}, u32[]{:S(2)}) %collective-permute-start.20) | collective-permute-done | bytes 458784 | tf_op jit(solution)/shard_map/ppermute | solution.py:215
  102.9 1.4 convolution_add_fusion.2
  104.4 1.4 convolution_add_fusion.1
  106.0 1.4 convolution_add_fusion
  108.3 3.1 %collective-permute-start.29 = (f32[96,512]{1,0:T(8,128)S(1)}, f32[96,512]{1,0:T(8,128)S(1)}, u32[]{:S(2)}, u32[]{:S(2)}) collective-permute-start(f32[96,512]{1,0:T(8,128)S(1)} %get-tuple-element.84), channel_id=1, source_target_pairs={{0,6},{1,7},{2,0},{3,1},{4,2},{5,3},{6,4},{7,5},{8,14},{9,15},{10,... | collective-permute-start | bytes 589832 | tf_op jit(solution)/shard_map/ppermute | solution.py:233
  111.4 4.1 %collective-permute-start.27 = (f32[96,512]{1,0:T(8,128)S(1)}, f32[96,512]{1,0:T(8,128)S(1)}, u32[]{:S(2)}, u32[]{:S(2)}) collective-permute-start(f32[96,512]{1,0:T(8,128)S(1)} %get-tuple-element.82), channel_id=1, source_target_pairs={{0,7},{1,6},{2,1},{3,0},{4,3},{5,2},{6,5},{7,4},{8,15},{9,14},{10,... | collective-permute-start | bytes 589832 | tf_op jit(solution)/shard_map/ppermute | solution.py:233
  115.5 3.0 %collective-permute-start.24 = (f32[96,512]{1,0:T(8,128)S(1)}, f32[96,512]{1,0:T(8,128)S(1)}, u32[]{:S(2)}, u32[]{:S(2)}) collective-permute-start(f32[96,512]{1,0:T(8,128)S(1)} %get-tuple-element.80), channel_id=1, source_target_pairs={{0,5},{1,4},{2,7},{3,6},{4,1},{5,0},{6,3},{7,2},{8,13},{9,12},{10,... | collective-permute-start | bytes 589832 | tf_op jit(solution)/shard_map/ppermute | solution.py:233
  120.8 5.6 %collective-permute-done.26 = f32[96,512]{1,0:T(8,128)S(1)} collective-permute-done((f32[96,512]{1,0:T(8,128)S(1)}, f32[96,512]{1,0:T(8,128)S(1)}, u32[]{:S(2)}, u32[]{:S(2)}) %collective-permute-start.26) | collective-permute-done | bytes 196640 | tf_op jit(solution)/shard_map/ppermute | solution.py:233
  126.3 3.9 %collective-permute-done.24 = f32[96,512]{1,0:T(8,128)S(1)} collective-permute-done((f32[96,512]{1,0:T(8,128)S(1)}, f32[96,512]{1,0:T(8,128)S(1)}, u32[]{:S(2)}, u32[]{:S(2)}) %collective-permute-start.24) | collective-permute-done | bytes 196640 | tf_op jit(solution)/shard_map/ppermute | solution.py:233
  130.2 3.8 %collective-permute-done.25 = f32[96,512]{1,0:T(8,128)S(1)} collective-permute-done((f32[96,512]{1,0:T(8,128)S(1)}, f32[96,512]{1,0:T(8,128)S(1)}, u32[]{:S(2)}, u32[]{:S(2)}) %collective-permute-start.25) | collective-permute-done | bytes 196640 | tf_op jit(solution)/shard_map/ppermute | solution.py:233
  135.1 1.9 %collective-permute-start.31 = (f32[96,512]{1,0:T(8,128)S(1)}, f32[96,512]{1,0:T(8,128)S(1)}, u32[]{:S(2)}, u32[]{:S(2)}) collective-permute-start(f32[96,512]{1,0:T(8,128)S(1)} %fusion.2), channel_id=1, source_target_pairs={{0,5},{1,4},{2,7},{3,6},{4,1},{5,0},{6,3},{7,2},{8,13},{9,12},{10,... | collective-permute-start | bytes 589832 | tf_op jit(solution)/shard_map/ppermute | solution.py:237
  137.0 2.1 %collective-permute-start.32 = (f32[96,512]{1,0:T(8,128)S(1)}, f32[96,512]{1,0:T(8,128)S(1)}, u32[]{:S(2)}, u32[]{:S(2)}) collective-permute-start(f32[96,512]{1,0:T(8,128)S(1)} %fusion.2), channel_id=1, source_target_pairs={{0,4},{1,5},{2,6},{3,7},{4,0},{5,1},{6,2},{7,3},{8,12},{9,13},{10,... | collective-permute-start | bytes 589832 | tf_op jit(solution)/shard_map/ppermute | solution.py:237
  140.1 3.7 %place.1 = f32[3584,512]{1,0:T(8,128)S(1)} custom-call(s32[8]{0:T(128)S(1)} %copy-done.18, f32[896,256]{1,0:T(8,128)} %maximum_maximum_fusion.refs_0_, f32[896,256]{1,0:T(8,128)} %copy-done.28, f32[896,256]{1,0:T(8,128)} %copy-done.27, f32[896,256]{1,0:T(8,128)} %copy-done.25, f32[896,256]{1,0:T(8,128)} %copy-done.29, f32[896,256]{1,0:T(8,128)} %copy-done.24, ...), custom_call_target="tpu_custom_call" | custom-call | flops 1 | bytes 14680064 | tf_op jit(solution)/shard_map/place/pallas_call | solution.py:132
  143.9 4.1 %collective-permute-start.34 = (f32[96,512]{1,0:T(8,128)S(1)}, f32[96,512]{1,0:T(8,128)S(1)}, u32[]{:S(2)}, u32[]{:S(2)}) collective-permute-start(f32[96,512]{1,0:T(8,128)S(1)} %fusion.2), channel_id=1, source_target_pairs={{0,7},{1,6},{2,1},{3,0},{4,3},{5,2},{6,5},{7,4},{8,15},{9,14},{10,... | collective-permute-start | bytes 589832 | tf_op jit(solution)/shard_map/ppermute | solution.py:237
  148.0 3.2 %collective-permute-start.36 = (f32[96,512]{1,0:T(8,128)S(1)}, f32[96,512]{1,0:T(8,128)S(1)}, u32[]{:S(2)}, u32[]{:S(2)}) collective-permute-start(f32[96,512]{1,0:T(8,128)S(1)} %fusion.2), channel_id=1, source_target_pairs={{0,6},{1,7},{2,0},{3,1},{4,2},{5,3},{6,4},{7,5},{8,14},{9,15},{10,... | collective-permute-start | bytes 589832 | tf_op jit(solution)/shard_map/ppermute | solution.py:237
  151.5 2.5 %collective-permute-done.32 = f32[96,512]{1,0:T(8,128)S(1)} collective-permute-done((f32[96,512]{1,0:T(8,128)S(1)}, f32[96,512]{1,0:T(8,128)S(1)}, u32[]{:S(2)}, u32[]{:S(2)}) %collective-permute-start.32) | collective-permute-done | bytes 196640 | tf_op jit(solution)/shard_map/ppermute | solution.py:237
  156.3 2.7 %collective-permute-done.35 = f32[96,512]{1,0:T(8,128)S(1)} collective-permute-done((f32[96,512]{1,0:T(8,128)S(1)}, f32[96,512]{1,0:T(8,128)S(1)}, u32[]{:S(2)}, u32[]{:S(2)}) %collective-permute-start.35) | collective-permute-done | bytes 196640 | tf_op jit(solution)/shard_map/ppermute | solution.py:237
  159.9 11.8 %fusion.18 = f32[768,3584]{1,0:T(8,128)} fusion(f32[768,512]{1,0:T(8,128)S(1)} %constant_dynamic-update-slice_fusion.14, f32[3584,512]{1,0:T(8,128)S(1)} %place.1), kind=kOutput, calls=%fused_computation.93 | convolution fusion | flops 8455716864 | bytes 19922944 | tf_op jit(solution)/shard_map/dot_general | solution.py:239
  (160 shorter events, 23.7 us)
Async XLA Ops:
  0.0 41.9 %copy-start = (f32[28672]{0:T(1024)S(1)}, f32[28672]{0:T(1024)}, u32[]{:S(2)}) copy-start(f32[28672]{0:T(1024)} %param.11) | copy-start | bytes 344068
  0.0 15.6 %copy-start.34 = (s32[4,128]{1,0:T(4,128)S(1)}, s32[4,128]{1,0:T(4,128)}, u32[]{:S(2)}) copy-start(s32[4,128]{1,0:T(4,128)} %param.12) | copy-start | bytes 6148
  0.0 15.6 %copy-start.35 = (s32[4,128]{1,0:T(4,128)S(1)}, s32[4,128]{1,0:T(4,128)}, u32[]{:S(2)}) copy-start(s32[4,128]{1,0:T(4,128)} %param.13) | copy-start | bytes 6148
  2.6 13.0 %collective-permute-start = (f32[448,128]{1,0:T(8,128)S(1)}, f32[448,128]{1,0:T(8,128)S(1)}, u32[]{:S(2)}, u32[]{:S(2)}) collective-permute-start(f32[448,128]{1,0:T(8,128)S(1)} %get-tuple-element.76), channel_id=1, source_target_pairs={{0,16},{8,24},{16,0},{24,8},{32,48},{40,56},{48,32},{56,40},{64,80... | collective-permute-start | bytes 688136 | tf_op jit(solution)/shard_map/ppermute | solution.py:180
  5.8 18.7 %collective-permute-start.1 = (f32[448,128]{1,0:T(8,128)S(1)}, f32[448,128]{1,0:T(8,128)S(1)}, u32[]{:S(2)}, u32[]{:S(2)}) collective-permute-start(f32[448,128]{1,0:T(8,128)S(1)} %get-tuple-element.75), channel_id=1, source_target_pairs={{0,32},{8,40},{16,48},{24,56},{32,64},{40,72},{48,80},{56,88},{64,... | collective-permute-start | bytes 688136 | tf_op jit(solution)/shard_map/ppermute | solution.py:180
  7.7 25.3 %collective-permute-start.2 = (f32[448,128]{1,0:T(8,128)}, f32[448,128]{1,0:T(8,128)S(1)}, u32[]{:S(2)}, u32[]{:S(2)}) collective-permute-start(f32[448,128]{1,0:T(8,128)} %get-tuple-element.74), channel_id=1, source_target_pairs={{0,48},{8,56},{16,32},{24,40},{32,80},{40,88},{48,64},{56,72},{64,... | collective-permute-start | bytes 688136 | tf_op jit(solution)/shard_map/ppermute | solution.py:180
  9.6 24.1 %collective-permute-start.3 = (f32[448,128]{1,0:T(8,128)}, f32[448,128]{1,0:T(8,128)S(1)}, u32[]{:S(2)}, u32[]{:S(2)}) collective-permute-start(f32[448,128]{1,0:T(8,128)} %get-tuple-element.73), channel_id=1, source_target_pairs={{0,64},{8,72},{16,80},{24,88},{32,96},{40,104},{48,112},{56,120},{... | collective-permute-start | bytes 688136 | tf_op jit(solution)/shard_map/ppermute | solution.py:180
  11.3 23.1 %collective-permute-start.4 = (f32[448,128]{1,0:T(8,128)}, f32[448,128]{1,0:T(8,128)}, u32[]{:S(2)}, u32[]{:S(2)}) collective-permute-start(f32[448,128]{1,0:T(8,128)} %get-tuple-element.72), channel_id=1, source_target_pairs={{0,80},{8,88},{16,64},{24,72},{32,112},{40,120},{48,96},{56,104},{... | collective-permute-start | bytes 688136 | tf_op jit(solution)/shard_map/ppermute | solution.py:180
  16.3 18.1 %collective-permute-start.5 = (f32[448,128]{1,0:T(8,128)}, f32[448,128]{1,0:T(8,128)S(1)}, u32[]{:S(2)}, u32[]{:S(2)}) collective-permute-start(f32[448,128]{1,0:T(8,128)} %get-tuple-element.78), channel_id=1, source_target_pairs={{0,96},{8,104},{16,112},{24,120},{32,0},{40,8},{48,16},{56,24},{64... | collective-permute-start | bytes 688136 | tf_op jit(solution)/shard_map/ppermute | solution.py:180
  25.2 9.2 %collective-permute-start.6 = (f32[448,128]{1,0:T(8,128)}, f32[448,128]{1,0:T(8,128)S(1)}, u32[]{:S(2)}, u32[]{:S(2)}) collective-permute-start(f32[448,128]{1,0:T(8,128)} %get-tuple-element.71), channel_id=1, source_target_pairs={{0,112},{8,120},{16,96},{24,104},{32,16},{40,24},{48,0},{56,8},{64... | collective-permute-start | bytes 688136 | tf_op jit(solution)/shard_map/ppermute | solution.py:180
  25.3 7.1 %copy-start.36 = (s32[4]{0:T(128)S(1)}, s32[4]{0:T(128)}, u32[]{:S(2)}) copy-start(s32[4]{0:T(128)} %param.9) | copy-start | bytes 52
  25.3 9.1 %copy-start.9 = (f32[448,128]{1,0:T(8,128)S(1)}, f32[448,128]{1,0:T(8,128)}, u32[]{:S(2)}) copy-start(f32[448,128]{1,0:T(8,128)} %copy-done.8) | copy-start | bytes 688132
  25.3 9.1 %copy-start.11 = (f32[448,128]{1,0:T(8,128)S(1)}, f32[448,128]{1,0:T(8,128)}, u32[]{:S(2)}) copy-start(f32[448,128]{1,0:T(8,128)} %copy-done.10) | copy-start | bytes 688132
  38.3 6.8 %collective-permute-start.7 = (f32[2,448,128]{2,1,0:T(8,128)}, f32[2,448,128]{2,1,0:T(8,128)}, u32[]{:S(2)}, u32[]{:S(2)}) collective-permute-start(f32[2,448,128]{2,1,0:T(8,128)} %get-tuple-element.49), channel_id=1, source_target_pairs={{0,8},{8,0},{16,24},{24,16},{32,40},{40,32},{48,56},{56,48},{64,72... | collective-permute-start | bytes 1376264 | tf_op jit(solution)/shard_map/ppermute | solution.py:186
  47.6 15.9 %collective-permute-start.8 = (f32[448,128]{1,0:T(8,128)}, f32[448,128]{1,0:T(8,128)S(1)}, u32[]{:S(2)}, u32[]{:S(2)}) collective-permute-start(f32[448,128]{1,0:T(8,128)} %get-tuple-element.50), channel_id=1, source_target_pairs={{0,16},{8,24},{16,0},{24,8},{32,48},{40,56},{48,32},{56,40},{64,80... | collective-permute-start | bytes 688136 | tf_op jit(solution)/shard_map/ppermute | solution.py:189
  63.4 9.2 %collective-permute-start.13 = (f32[448,128]{1,0:T(8,128)S(1)}, f32[448,128]{1,0:T(8,128)S(1)}, u32[]{:S(2)}, u32[]{:S(2)}) collective-permute-start(f32[448,128]{1,0:T(8,128)S(1)} %get-tuple-element.57), channel_id=1, source_target_pairs={{0,16},{8,24},{16,0},{24,8},{32,48},{40,56},{48,32},{56,40},{64,80... | collective-permute-start | bytes 688136 | tf_op jit(solution)/shard_map/ppermute | solution.py:189
  64.4 8.5 %copy-start.5 = (f32[768,896]{1,0:T(8,128)S(1)}, f32[768,896]{1,0:T(8,128)}, u32[]{:S(2)}) copy-start(f32[768,896]{1,0:T(8,128)} %copy-done.4) | copy-start | bytes 8257540
  64.5 10.3 %collective-permute-start.9 = (f32[896,128]{1,0:T(8,128)S(1)}, f32[896,128]{1,0:T(8,128)S(1)}, u32[]{:S(2)}, u32[]{:S(2)}) collective-permute-start(f32[896,128]{1,0:T(8,128)S(1)} %pad_maximum_fusion), channel_id=1, source_target_pairs={{0,32},{8,104},{16,48},{24,120},{32,64},{40,8},{48,80},{56,24},{64... | collective-permute-start | bytes 1376264 | tf_op jit(solution)/shard_map/ppermute | solution.py:215
  65.9 9.0 %collective-permute-start.10 = (f32[896,128]{1,0:T(8,128)S(1)}, f32[896,128]{1,0:T(8,128)S(1)}, u32[]{:S(2)}, u32[]{:S(2)}) collective-permute-start(f32[896,128]{1,0:T(8,128)S(1)} %pad_maximum_fusion), channel_id=1, source_target_pairs={{0,8},{8,0},{16,24},{24,16},{32,40},{40,32},{48,56},{56,48},{64,72... | collective-permute-start | bytes 1376264 | tf_op jit(solution)/shard_map/ppermute | solution.py:218
  72.8 5.8 %collective-permute-start.14 = (f32[896,128]{1,0:T(8,128)S(1)}, f32[896,128]{1,0:T(8,128)S(1)}, u32[]{:S(2)}, u32[]{:S(2)}) collective-permute-start(f32[896,128]{1,0:T(8,128)S(1)} %pad_maximum_fusion.1), channel_id=1, source_target_pairs={{0,8},{8,0},{16,24},{24,16},{32,40},{40,32},{48,56},{56,48},{64,72... | collective-permute-start | bytes 1376264 | tf_op jit(solution)/shard_map/ppermute | solution.py:218
  72.8 10.3 %collective-permute-start.17 = (f32[896,128]{1,0:T(8,128)S(1)}, f32[896,128]{1,0:T(8,128)S(1)}, u32[]{:S(2)}, u32[]{:S(2)}) collective-permute-start(f32[896,128]{1,0:T(8,128)S(1)} %pad_maximum_fusion.1), channel_id=1, source_target_pairs={{0,32},{8,104},{16,48},{24,120},{32,64},{40,8},{48,80},{56,24},{64... | collective-permute-start | bytes 1376264 | tf_op jit(solution)/shard_map/ppermute | solution.py:215
  74.8 13.3 %collective-permute-start.11 = (f32[896,128]{1,0:T(8,128)S(1)}, f32[896,128]{1,0:T(8,128)S(1)}, u32[]{:S(2)}, u32[]{:S(2)}) collective-permute-start(f32[896,128]{1,0:T(8,128)S(1)} %collective-permute-done.9), channel_id=1, source_target_pairs={{0,32},{8,104},{16,48},{24,120},{32,64},{40,8},{48,80},{56,24},{64... | collective-permute-start | bytes 1376264 | tf_op jit(solution)/shard_map/ppermute | solution.py:215
  77.2 10.9 %collective-permute-start.12 = (f32[896,128]{1,0:T(8,128)S(1)}, f32[896,128]{1,0:T(8,128)S(1)}, u32[]{:S(2)}, u32[]{:S(2)}) collective-permute-start(f32[896,128]{1,0:T(8,128)S(1)} %collective-permute-done.9), channel_id=1, source_target_pairs={{0,8},{8,0},{16,24},{24,16},{32,40},{40,32},{48,56},{56,48},{64,72... | collective-permute-start | bytes 1376264 | tf_op jit(solution)/shard_map/ppermute | solution.py:218
  83.2 12.2 %collective-permute-start.18 = (f32[896,128]{1,0:T(8,128)S(1)}, f32[896,128]{1,0:T(8,128)S(1)}, u32[]{:S(2)}, u32[]{:S(2)}) collective-permute-start(f32[896,128]{1,0:T(8,128)S(1)} %collective-permute-done.17), channel_id=1, source_target_pairs={{0,8},{8,0},{16,24},{24,16},{32,40},{40,32},{48,56},{56,48},{64,72... | collective-permute-start | bytes 1376264 | tf_op jit(solution)/shard_map/ppermute | solution.py:218
  83.2 9.8 %collective-permute-start.19 = (f32[896,128]{1,0:T(8,128)S(1)}, f32[896,128]{1,0:T(8,128)S(1)}, u32[]{:S(2)}, u32[]{:S(2)}) collective-permute-start(f32[896,128]{1,0:T(8,128)S(1)} %collective-permute-done.17), channel_id=1, source_target_pairs={{0,32},{8,104},{16,48},{24,120},{32,64},{40,8},{48,80},{56,24},{64... | collective-permute-start | bytes 1376264 | tf_op jit(solution)/shard_map/ppermute | solution.py:215
  88.1 10.7 %collective-permute-start.15 = (f32[896,128]{1,0:T(8,128)S(1)}, f32[896,128]{1,0:T(8,128)S(1)}, u32[]{:S(2)}, u32[]{:S(2)}) collective-permute-start(f32[896,128]{1,0:T(8,128)S(1)} %collective-permute-done.11), channel_id=1, source_target_pairs={{0,32},{8,104},{16,48},{24,120},{32,64},{40,8},{48,80},{56,24},{64... | collective-permute-start | bytes 1376264 | tf_op jit(solution)/shard_map/ppermute | solution.py:215
  88.1 10.7 %collective-permute-start.16 = (f32[896,128]{1,0:T(8,128)S(1)}, f32[896,128]{1,0:T(8,128)S(1)}, u32[]{:S(2)}, u32[]{:S(2)}) collective-permute-start(f32[896,128]{1,0:T(8,128)S(1)} %collective-permute-done.11), channel_id=1, source_target_pairs={{0,8},{8,0},{16,24},{24,16},{32,40},{40,32},{48,56},{56,48},{64,72... | collective-permute-start | bytes 1376264 | tf_op jit(solution)/shard_map/ppermute | solution.py:218
  93.0 9.8 %collective-permute-start.20 = (f32[896,128]{1,0:T(8,128)S(1)}, f32[896,128]{1,0:T(8,128)S(1)}, u32[]{:S(2)}, u32[]{:S(2)}) collective-permute-start(f32[896,128]{1,0:T(8,128)S(1)} %collective-permute-done.19), channel_id=1, source_target_pairs={{0,32},{8,104},{16,48},{24,120},{32,64},{40,8},{48,80},{56,24},{64... | collective-permute-start | bytes 1376264 | tf_op jit(solution)/shard_map/ppermute | solution.py:215
  93.0 11.3 %collective-permute-start.21 = (f32[896,128]{1,0:T(8,128)S(1)}, f32[896,128]{1,0:T(8,128)S(1)}, u32[]{:S(2)}, u32[]{:S(2)}) collective-permute-start(f32[896,128]{1,0:T(8,128)S(1)} %collective-permute-done.19), channel_id=1, source_target_pairs={{0,8},{8,0},{16,24},{24,16},{32,40},{40,32},{48,56},{56,48},{64,72... | collective-permute-start | bytes 1376264 | tf_op jit(solution)/shard_map/ppermute | solution.py:218
  98.9 7.0 %collective-permute-start.22 = (f32[896,128]{1,0:T(8,128)S(1)}, f32[896,128]{1,0:T(8,128)S(1)}, u32[]{:S(2)}, u32[]{:S(2)}) collective-permute-start(f32[896,128]{1,0:T(8,128)S(1)} %collective-permute-done.15), channel_id=1, source_target_pairs={{0,8},{8,0},{16,24},{24,16},{32,40},{40,32},{48,56},{56,48},{64,72... | collective-permute-start | bytes 1376264 | tf_op jit(solution)/shard_map/ppermute | solution.py:218
  102.8 3.1 %collective-permute-start.23 = (f32[896,128]{1,0:T(8,128)S(1)}, f32[896,128]{1,0:T(8,128)S(1)}, u32[]{:S(2)}, u32[]{:S(2)}) collective-permute-start(f32[896,128]{1,0:T(8,128)S(1)} %collective-permute-done.20), channel_id=1, source_target_pairs={{0,8},{8,0},{16,24},{24,16},{32,40},{40,32},{48,56},{56,48},{64,72... | collective-permute-start | bytes 1376264 | tf_op jit(solution)/shard_map/ppermute | solution.py:218
  107.4 8.0 %collective-permute-start.30 = (f32[96,512]{1,0:T(8,128)S(1)}, f32[96,512]{1,0:T(8,128)S(1)}, u32[]{:S(2)}, u32[]{:S(2)}) collective-permute-start(f32[96,512]{1,0:T(8,128)S(1)} %fusion.9), channel_id=1, source_target_pairs={{0,1},{1,0},{2,3},{3,2},{4,5},{5,4},{6,7},{7,6},{8,9},{9,8},{10,11... | collective-permute-start | bytes 589832 | tf_op jit(solution)/shard_map/ppermute | solution.py:233
  108.3 11.5 %collective-permute-start.29 = (f32[96,512]{1,0:T(8,128)S(1)}, f32[96,512]{1,0:T(8,128)S(1)}, u32[]{:S(2)}, u32[]{:S(2)}) collective-permute-start(f32[96,512]{1,0:T(8,128)S(1)} %get-tuple-element.84), channel_id=1, source_target_pairs={{0,6},{1,7},{2,0},{3,1},{4,2},{5,3},{6,4},{7,5},{8,14},{9,15},{10,... | collective-permute-start | bytes 589832 | tf_op jit(solution)/shard_map/ppermute | solution.py:233
  111.4 8.4 %collective-permute-start.28 = (f32[96,512]{1,0:T(8,128)S(1)}, f32[96,512]{1,0:T(8,128)S(1)}, u32[]{:S(2)}, u32[]{:S(2)}) collective-permute-start(f32[96,512]{1,0:T(8,128)S(1)} %get-tuple-element.83), channel_id=1, source_target_pairs={{0,2},{1,3},{2,4},{3,5},{4,6},{5,7},{6,0},{7,1},{8,10},{9,11},{10,... | collective-permute-start | bytes 589832 | tf_op jit(solution)/shard_map/ppermute | solution.py:233
  111.4 9.4 %collective-permute-start.27 = (f32[96,512]{1,0:T(8,128)S(1)}, f32[96,512]{1,0:T(8,128)S(1)}, u32[]{:S(2)}, u32[]{:S(2)}) collective-permute-start(f32[96,512]{1,0:T(8,128)S(1)} %get-tuple-element.82), channel_id=1, source_target_pairs={{0,7},{1,6},{2,1},{3,0},{4,3},{5,2},{6,5},{7,4},{8,15},{9,14},{10,... | collective-permute-start | bytes 589832 | tf_op jit(solution)/shard_map/ppermute | solution.py:233
  115.5 10.9 %collective-permute-start.26 = (f32[96,512]{1,0:T(8,128)S(1)}, f32[96,512]{1,0:T(8,128)S(1)}, u32[]{:S(2)}, u32[]{:S(2)}) collective-permute-start(f32[96,512]{1,0:T(8,128)S(1)} %get-tuple-element.81), channel_id=1, source_target_pairs={{0,3},{1,2},{2,5},{3,4},{4,7},{5,6},{6,1},{7,0},{8,11},{9,10},{10,... | collective-permute-start | bytes 589832 | tf_op jit(solution)/shard_map/ppermute | solution.py:233
  115.5 14.7 %collective-permute-start.24 = (f32[96,512]{1,0:T(8,128)S(1)}, f32[96,512]{1,0:T(8,128)S(1)}, u32[]{:S(2)}, u32[]{:S(2)}) collective-permute-start(f32[96,512]{1,0:T(8,128)S(1)} %get-tuple-element.80), channel_id=1, source_target_pairs={{0,5},{1,4},{2,7},{3,6},{4,1},{5,0},{6,3},{7,2},{8,13},{9,12},{10,... | collective-permute-start | bytes 589832 | tf_op jit(solution)/shard_map/ppermute | solution.py:233
  119.8 14.2 %collective-permute-start.25 = (f32[96,512]{1,0:T(8,128)S(1)}, f32[96,512]{1,0:T(8,128)S(1)}, u32[]{:S(2)}, u32[]{:S(2)}) collective-permute-start(f32[96,512]{1,0:T(8,128)S(1)} %get-tuple-element.79), channel_id=1, source_target_pairs={{0,4},{1,5},{2,6},{3,7},{4,0},{5,1},{6,2},{7,3},{8,12},{9,13},{10,... | collective-permute-start | bytes 589832 | tf_op jit(solution)/shard_map/ppermute | solution.py:233
  119.8 19.3 %copy-start.31 = (f32[448,128]{1,0:T(8,128)S(1)}, f32[448,128]{1,0:T(8,128)}, u32[]{:S(2)}) copy-start(f32[448,128]{1,0:T(8,128)} %copy-done.30) | copy-start | bytes 688132
  119.8 19.3 %copy-start.33 = (f32[448,128]{1,0:T(8,128)S(1)}, f32[448,128]{1,0:T(8,128)}, u32[]{:S(2)}) copy-start(f32[448,128]{1,0:T(8,128)} %copy-done.32) | copy-start | bytes 688132
  135.1 12.9 %collective-permute-start.31 = (f32[96,512]{1,0:T(8,128)S(1)}, f32[96,512]{1,0:T(8,128)S(1)}, u32[]{:S(2)}, u32[]{:S(2)}) collective-permute-start(f32[96,512]{1,0:T(8,128)S(1)} %fusion.2), channel_id=1, source_target_pairs={{0,5},{1,4},{2,7},{3,6},{4,1},{5,0},{6,3},{7,2},{8,13},{9,12},{10,... | collective-permute-start | bytes 589832 | tf_op jit(solution)/shard_map/ppermute | solution.py:237
  137.0 16.9 %collective-permute-start.32 = (f32[96,512]{1,0:T(8,128)S(1)}, f32[96,512]{1,0:T(8,128)S(1)}, u32[]{:S(2)}, u32[]{:S(2)}) collective-permute-start(f32[96,512]{1,0:T(8,128)S(1)} %fusion.2), channel_id=1, source_target_pairs={{0,4},{1,5},{2,6},{3,7},{4,0},{5,1},{6,2},{7,3},{8,12},{9,13},{10,... | collective-permute-start | bytes 589832 | tf_op jit(solution)/shard_map/ppermute | solution.py:237
  143.8 11.0 %collective-permute-start.33 = (f32[96,512]{1,0:T(8,128)S(1)}, f32[96,512]{1,0:T(8,128)S(1)}, u32[]{:S(2)}, u32[]{:S(2)}) collective-permute-start(f32[96,512]{1,0:T(8,128)S(1)} %fusion.2), channel_id=1, source_target_pairs={{0,3},{1,2},{2,5},{3,4},{4,7},{5,6},{6,1},{7,0},{8,11},{9,10},{10,... | collective-permute-start | bytes 589832 | tf_op jit(solution)/shard_map/ppermute | solution.py:237
  143.9 12.4 %collective-permute-start.34 = (f32[96,512]{1,0:T(8,128)S(1)}, f32[96,512]{1,0:T(8,128)S(1)}, u32[]{:S(2)}, u32[]{:S(2)}) collective-permute-start(f32[96,512]{1,0:T(8,128)S(1)} %fusion.2), channel_id=1, source_target_pairs={{0,7},{1,6},{2,1},{3,0},{4,3},{5,2},{6,5},{7,4},{8,15},{9,14},{10,... | collective-permute-start | bytes 589832 | tf_op jit(solution)/shard_map/ppermute | solution.py:237
  148.0 10.9 %collective-permute-start.35 = (f32[96,512]{1,0:T(8,128)S(1)}, f32[96,512]{1,0:T(8,128)S(1)}, u32[]{:S(2)}, u32[]{:S(2)}) collective-permute-start(f32[96,512]{1,0:T(8,128)S(1)} %fusion.2), channel_id=1, source_target_pairs={{0,2},{1,3},{2,4},{3,5},{4,6},{5,7},{6,0},{7,1},{8,10},{9,11},{10,... | collective-permute-start | bytes 589832 | tf_op jit(solution)/shard_map/ppermute | solution.py:237
  148.0 10.9 %collective-permute-start.36 = (f32[96,512]{1,0:T(8,128)S(1)}, f32[96,512]{1,0:T(8,128)S(1)}, u32[]{:S(2)}, u32[]{:S(2)}) collective-permute-start(f32[96,512]{1,0:T(8,128)S(1)} %fusion.2), channel_id=1, source_target_pairs={{0,6},{1,7},{2,0},{3,1},{4,2},{5,3},{6,4},{7,5},{8,14},{9,15},{10,... | collective-permute-start | bytes 589832 | tf_op jit(solution)/shard_map/ppermute | solution.py:237
  154.0 5.9 %collective-permute-start.37 = (f32[96,512]{1,0:T(8,128)S(1)}, f32[96,512]{1,0:T(8,128)S(1)}, u32[]{:S(2)}, u32[]{:S(2)}) collective-permute-start(f32[96,512]{1,0:T(8,128)S(1)} %fusion.2), channel_id=1, source_target_pairs={{0,1},{1,0},{2,3},{3,2},{4,5},{5,4},{6,7},{7,6},{8,9},{9,8},{10,11... | collective-permute-start | bytes 589832 | tf_op jit(solution)/shard_map/ppermute | solution.py:237
  159.9 11.8 %copy-start.1 = (f32[28672]{0:T(1024)S(1)}, f32[28672]{0:T(1024)}, u32[]{:S(2)}) copy-start(f32[28672]{0:T(1024)} %param.11) | copy-start | bytes 344068
  (27 other events, 51.4 us)

commit v5 on v4

--- a/solution.py
+++ b/solution.py
@@ -179,8 +179,8 @@
     for dz, dx in SPREAD:
         arrived[dz, dx] = lax.ppermute(eighth(dz, dx), "rows", away(dz, dx))
     pieces = [arrived[dz, dx] for dz in range(PLANES) for dx in range(2)]
-    g = rotate(at, gradient, (0, 1))
-    *pieces, g0, g1 = lax.optimization_barrier((*pieces, *g))
+    g = rotate(at, gradient, (0, 1, 3))
+    *pieces, g0, g1, g3 = lax.optimization_barrier((*pieces, *g))
     chosen = jnp.concatenate([panel_index, jnp.stack([core, z, x]).astype(jnp.int32)])
     mine, give = pick(chosen, pieces)
     halves = settle(chosen, mine, lax.ppermute(give, "rows", CORE))
@@ -188,14 +188,16 @@
     for c, half in enumerate(halves):
         own[c].append(ordered(x == 0, half, lax.ppermute(half, "rows", XPAIR)))
 
-    g = rotate(at, gradient, (2, 3))
-    own[0][0], g2, g3 = lax.optimization_barrier((own[0][0], *g))
+    g = rotate(at, gradient, (2,))
+    own[0][0], g2 = lax.optimization_barrier((own[0][0], *g))
     g = [g0, g1, g2, g3]
 
     v_own, v_oth, total, waiting = [], [], None, None
 
     def product(step, own, oth, total):
         mine, other = jnp.concatenate(own, axis=1), jnp.concatenate(oth, axis=1)
+        mine, = lax.optimization_barrier((mine,))
+        other, = lax.optimization_barrier((other,))
         v_own.append(mine)
         v_oth.append(other)
         mine, other = dot(g[step], mine), dot(g[-step % PLANES], other)
@@ -213,8 +215,6 @@
                     held, last_oth[0] = lax.optimization_barrier((held, last_oth[0]))
             if step < PLANES - 1:
                 own[c].append(lax.ppermute(held, "rows", RING))
-                if (c, step) == (0, 0):
-                    own[0][1], damped = lax.optimization_barrier((own[0][1], damped))
             oth[c] = lax.ppermute(held, "rows", CORE)
         if waiting is not None:
             total = product(*waiting, total)

time: 172 us -> 166 us (0.965)
  local copies, waits for them, and re-layouts: 23.1 us -> 15.1 us
  waiting for transfers between devices: 46.5 us -> 50.4 us
  Pallas kernels: 18.5 us -> 16.1 us
  starting transfers between devices: 55.5 us -> 57.5 us
  other arithmetic: 4.18 us -> 2.18 us
    unnamed x81 -> x40, local copies, waits for them, and re-layouts: 13.2 us -> 6.74 us
    ppermute x6, waiting for transfers between devices: 11.5 us -> 15.1 us  [shards(): own[c].append(lax.ppermute(held, 'rows', RING))]
    ppermute x1, waiting for transfers between devices: 0.01 us -> 1.73 us  [shards(): halves = settle(chosen, mine, lax.ppermute(give, 'rows', CORE))]
  transfers between devices with their start and end apart: 38 -> 38, of which waited for: 17 -> 15; matrix products, arithmetic and copies ran while one was open for 12% -> 11% of each run, Pallas kernels for 9% -> 9%
where the time goes in v5:
time: 166 us; the launch traced here: 165 us
  starting transfers between devices  57.5 us (35%)
  waiting for transfers between devices  50.4 us (30%)
  matrix products  23.2 us (14%)
  Pallas kernels  16.1 us (10%)
  local copies, waits for them, and re-layouts  15.1 us (9%)
  other arithmetic  2.18 us (1%)
    ppermute x6, waiting for transfers between devices, shards(): own[c].append(lax.ppermute(held, 'rows', RING))  15.1 us
    ppermute x7, starting transfers between devices, shards(): arrived[dz, dx] = lax.ppermute(eighth(dz, dx), 'rows', away(dz, dx))  14.3 us
    ppermute x7, waiting for transfers between devices, shards(): lax.ppermute(part, 'cols', across(*turn))  14 us
    ppermute x7, starting transfers between devices, shards(): lax.ppermute(scaled_block, 'cols', across(*turn))  13.1 us
    dot_general x1, matrix products, shards(): lax.dot_general(scaled, v, (((1,), (1,)), ((), ())), precision=lax.Precis...  11.8 us
    ppermute x7, starting transfers between devices, shards(): lax.ppermute(part, 'cols', across(*turn))  11.4 us
    dot_general x8, matrix products, dot(): jnp.dot(a, b, precision=lax.Precision.HIGH, preferred_element_type=F32)  11.4 us
    pallas_call x2, Pallas kernels, rotate(): pl.pallas_call(rotate_body, grid_spec=pltpu.PrefetchScalarGridSpec(num_sc...  11 us
  transfers between devices with their start and end apart: 38, of which 15 were waited for; matrix products, arithmetic and copies ran while one was open for 11% of the time, Pallas kernels for 9%

profile of v5, /device:TPU:0, one launch (start us, length us, event | category | flops | bytes accessed | tf_op | source)
XLA Modules:
  0.0 165.2 jit_solution(10039601328036432559)
XLA Ops:
  0.0 1.7 %dynamic-slice_bitcast_fusion = (f32[448,128]{1,0:T(8,128)S(1)}, f32[448,128]{1,0:T(8,128)S(1)}, f32[448,128]{1,0:T(8,128)S(1)}, f32[448,128]{1,0:T(8,128)S(1)},...) fusion(f32[1,3584,128]{2,1,0:T(8,128)} %param.8, ...), kind=kLoop, calls=%fused_computation.33 | loop fusion | bytes 3670048 | tf_op jit(solution)/shard_map/dynamic_slice | solution.py:176
  1.7 3.2 %collective-permute-start = (f32[448,128]{1,0:T(8,128)S(1)}, f32[448,128]{1,0:T(8,128)S(1)}, u32[]{:S(2)}, u32[]{:S(2)}) collective-permute-start(f32[448,128]{1,0:T(8,128)S(1)} %get-tuple-element.70), channel_id=1, source_target_pairs={{0,16},{8,24},{16,0},{24,8},{32,48},{40,56},{48,32},{56,40},{64,80... | collective-permute-start | bytes 688136 | tf_op jit(solution)/shard_map/ppermute | solution.py:180
  4.9 1.9 %collective-permute-start.1 = (f32[448,128]{1,0:T(8,128)S(1)}, f32[448,128]{1,0:T(8,128)S(1)}, u32[]{:S(2)}, u32[]{:S(2)}) collective-permute-start(f32[448,128]{1,0:T(8,128)S(1)} %get-tuple-element.69), channel_id=1, source_target_pairs={{0,32},{8,40},{16,48},{24,56},{32,64},{40,72},{48,80},{56,88},{64,... | collective-permute-start | bytes 688136 | tf_op jit(solution)/shard_map/ppermute | solution.py:180
  6.8 1.9 %collective-permute-start.2 = (f32[448,128]{1,0:T(8,128)S(1)}, f32[448,128]{1,0:T(8,128)S(1)}, u32[]{:S(2)}, u32[]{:S(2)}) collective-permute-start(f32[448,128]{1,0:T(8,128)S(1)} %get-tuple-element.68), channel_id=1, source_target_pairs={{0,48},{8,56},{16,32},{24,40},{32,80},{40,88},{48,64},{56,72},{64,... | collective-permute-start | bytes 688136 | tf_op jit(solution)/shard_map/ppermute | solution.py:180
  8.7 1.7 %collective-permute-start.3 = (f32[448,128]{1,0:T(8,128)S(1)}, f32[448,128]{1,0:T(8,128)S(1)}, u32[]{:S(2)}, u32[]{:S(2)}) collective-permute-start(f32[448,128]{1,0:T(8,128)S(1)} %get-tuple-element.67), channel_id=1, source_target_pairs={{0,64},{8,72},{16,80},{24,88},{32,96},{40,104},{48,112},{56,120},{... | collective-permute-start | bytes 688136 | tf_op jit(solution)/shard_map/ppermute | solution.py:180
  10.4 4.3 %collective-permute-start.4 = (f32[448,128]{1,0:T(8,128)S(1)}, f32[448,128]{1,0:T(8,128)S(1)}, u32[]{:S(2)}, u32[]{:S(2)}) collective-permute-start(f32[448,128]{1,0:T(8,128)S(1)} %get-tuple-element.66), channel_id=1, source_target_pairs={{0,80},{8,88},{16,64},{24,72},{32,112},{40,120},{48,96},{56,104},{... | collective-permute-start | bytes 688136 | tf_op jit(solution)/shard_map/ppermute | solution.py:180
  16.0 7.5 %collective-permute-done.1.refs_2_ = f32[448,128]{1,0:T(8,128)S(1)} collective-permute-done((f32[448,128]{1,0:T(8,128)S(1)}, f32[448,128]{1,0:T(8,128)S(1)}, u32[]{:S(2)}, u32[]{:S(2)}) %collective-permute-start.1) | collective-permute-done | bytes 229408 | tf_op jit(solution)/shard_map/ppermute | solution.py:180
  23.6 6.2 %rotate.2 = (f32[768,896]{1,0:T(8,128)S(1)}, f32[768,896]{1,0:T(8,128)S(1)}, f32[768,896]{1,0:T(8,128)S(1)}) custom-call(s32[8]{0:T(128)S(1)} %pad_add_fusion.1.at_ref, f32[768,3584]{1,0:T(8,128)} %refs_0_.3, f32[768,3584]{1,0:T(8,128)} %refs_0_.3, f32[768,3584]{1,0:T(8,128)} %refs_0_.3), custom_call_target="tpu_custom_call" | custom-call | flops 1 | bytes 16515072 | tf_op jit(solution)/shard_map/rotate/pallas_call | solution.py:46
  29.8 1.5 copy-done.2
  31.4 1.5 copy-done.4
  32.9 1.5 copy-done.6
  35.5 1.7 %collective-permute-done.7.got_ref = f32[2,448,128]{2,1,0:T(8,128)S(1)} collective-permute-done((f32[2,448,128]{2,1,0:T(8,128)S(1)}, f32[2,448,128]{2,1,0:T(8,128)S(1)}, u32[]{:S(2)}, u32[]{:S(2)}) %collective-permute-start.7) | collective-permute-done | bytes 458784 | tf_op jit(solution)/shard_map/ppermute | solution.py:186
  37.9 6.8 %collective-permute-start.8 = (f32[448,128]{1,0:T(8,128)S(1)}, f32[448,128]{1,0:T(8,128)}, u32[]{:S(2)}, u32[]{:S(2)}) collective-permute-start(f32[448,128]{1,0:T(8,128)S(1)} %get-tuple-element.48), channel_id=1, source_target_pairs={{0,16},{8,24},{16,0},{24,8},{32,48},{40,56},{48,32},{56,40},{64,80... | collective-permute-start | bytes 688136 | tf_op jit(solution)/shard_map/ppermute | solution.py:189
  44.7 4.8 %rotate.3 = f32[768,896]{1,0:T(8,128)S(1)} custom-call(s32[8]{0:T(128)S(1)} %pad_add_fusion.1.at_ref, f32[768,3584]{1,0:T(8,128)} %refs_0_.3), custom_call_target="tpu_custom_call" | custom-call | flops 1 | bytes 5505024 | tf_op jit(solution)/shard_map/rotate/pallas_call | solution.py:46
  50.3 3.1 %gather_fusion = f32[512]{0:T(512)S(1)} fusion(f32[8192]{0:T(1024)S(1)} %copy-done.8, s32[1024]{0:T(1024)S(1)} %pad_clamp_fusion.1), kind=kCustom, calls=%fused_computation | custom fusion | bytes 6144 | tf_op jit(solution)/shard_map/gather | solution.py:169
  53.4 3.1 %gather_fusion.1 = f32[512]{0:T(512)S(1)} fusion(f32[28672]{0:T(1024)S(1)} %copy-done, s32[1024]{0:T(1024)S(1)} %pad_clamp_fusion), kind=kCustom, calls=%fused_computation.1 | custom fusion | bytes 6144 | tf_op jit(solution)/shard_map/gather | solution.py:169
  59.1 2.1 %collective-permute-start.10 = (f32[896,128]{1,0:T(8,128)S(1)}, f32[896,128]{1,0:T(8,128)S(1)}, u32[]{:S(2)}, u32[]{:S(2)}) collective-permute-start(f32[896,128]{1,0:T(8,128)S(1)} %pad_maximum_fusion.7), channel_id=1, source_target_pairs={{0,8},{8,0},{16,24},{24,16},{32,40},{40,32},{48,56},{56,48},{64,72... | collective-permute-start | bytes 1376264 | tf_op jit(solution)/shard_map/ppermute | solution.py:218
  61.2 4.3 %collective-permute-done.13 = f32[448,128]{1,0:T(8,128)S(1)} collective-permute-done((f32[448,128]{1,0:T(8,128)S(1)}, f32[448,128]{1,0:T(8,128)S(1)}, u32[]{:S(2)}, u32[]{:S(2)}) %collective-permute-start.13) | collective-permute-done | bytes 229408 | tf_op jit(solution)/shard_map/ppermute | solution.py:189
  65.9 1.5 copy-done.7
  68.8 1.4 collective-permute-start.11
  73.0 3.1 %collective-permute-done.17 = f32[896,128]{1,0:T(8,128)S(1)} collective-permute-done((f32[896,128]{1,0:T(8,128)S(1)}, f32[896,128]{1,0:T(8,128)S(1)}, u32[]{:S(2)}, u32[]{:S(2)}) %collective-permute-start.17) | collective-permute-done | bytes 458784 | tf_op jit(solution)/shard_map/ppermute | solution.py:217
  76.4 1.4 fusion.17
  77.9 3.1 %collective-permute-done.11 = f32[896,128]{1,0:T(8,128)S(1)} collective-permute-done((f32[896,128]{1,0:T(8,128)S(1)}, f32[896,128]{1,0:T(8,128)S(1)}, u32[]{:S(2)}, u32[]{:S(2)}) %collective-permute-start.11) | collective-permute-done | bytes 458784 | tf_op jit(solution)/shard_map/ppermute | solution.py:217
  81.0 2.2 %collective-permute-start.16 = (f32[896,128]{1,0:T(8,128)S(1)}, f32[896,128]{1,0:T(8,128)S(1)}, u32[]{:S(2)}, u32[]{:S(2)}) collective-permute-start(f32[896,128]{1,0:T(8,128)S(1)} %collective-permute-done.11), channel_id=1, source_target_pairs={{0,8},{8,0},{16,24},{24,16},{32,40},{40,32},{48,56},{56,48},{64,72... | collective-permute-start | bytes 1376264 | tf_op jit(solution)/shard_map/ppermute | solution.py:218
  83.3 2.8 %collective-permute-done.19 = f32[896,128]{1,0:T(8,128)S(1)} collective-permute-done((f32[896,128]{1,0:T(8,128)S(1)}, f32[896,128]{1,0:T(8,128)S(1)}, u32[]{:S(2)}, u32[]{:S(2)}) %collective-permute-start.19) | collective-permute-done | bytes 458784 | tf_op jit(solution)/shard_map/ppermute | solution.py:217
  86.3 2.1 %collective-permute-start.21 = (f32[896,128]{1,0:T(8,128)S(1)}, f32[896,128]{1,0:T(8,128)S(1)}, u32[]{:S(2)}, u32[]{:S(2)}) collective-permute-start(f32[896,128]{1,0:T(8,128)S(1)} %collective-permute-done.19), channel_id=1, source_target_pairs={{0,8},{8,0},{16,24},{24,16},{32,40},{40,32},{48,56},{56,48},{64,72... | collective-permute-start | bytes 1376264 | tf_op jit(solution)/shard_map/ppermute | solution.py:218
  88.4 1.4 convolution_add_fusion.4
  91.0 4.9 %collective-permute-done.20 = f32[896,128]{1,0:T(8,128)S(1)} collective-permute-done((f32[896,128]{1,0:T(8,128)S(1)}, f32[896,128]{1,0:T(8,128)S(1)}, u32[]{:S(2)}, u32[]{:S(2)}) %collective-permute-start.20) | collective-permute-done | bytes 458784 | tf_op jit(solution)/shard_map/ppermute | solution.py:217
  96.1 1.4 convolution_add_fusion.3
  98.1 1.4 convolution_add_fusion.2
  99.6 1.4 convolution_add_fusion.1
  103.5 3.1 %collective-permute-start.29 = (f32[96,512]{1,0:T(8,128)S(1)}, f32[96,512]{1,0:T(8,128)S(1)}, u32[]{:S(2)}, u32[]{:S(2)}) collective-permute-start(f32[96,512]{1,0:T(8,128)S(1)} %get-tuple-element.78), channel_id=1, source_target_pairs={{0,6},{1,7},{2,0},{3,1},{4,2},{5,3},{6,4},{7,5},{8,14},{9,15},{10,... | collective-permute-start | bytes 589832 | tf_op jit(solution)/shard_map/ppermute | solution.py:233
  106.5 4.1 %collective-permute-start.27 = (f32[96,512]{1,0:T(8,128)S(1)}, f32[96,512]{1,0:T(8,128)S(1)}, u32[]{:S(2)}, u32[]{:S(2)}) collective-permute-start(f32[96,512]{1,0:T(8,128)S(1)} %get-tuple-element.76), channel_id=1, source_target_pairs={{0,7},{1,6},{2,1},{3,0},{4,3},{5,2},{6,5},{7,4},{8,15},{9,14},{10,... | collective-permute-start | bytes 589832 | tf_op jit(solution)/shard_map/ppermute | solution.py:233
  110.7 3.1 %collective-permute-start.24 = (f32[96,512]{1,0:T(8,128)S(1)}, f32[96,512]{1,0:T(8,128)S(1)}, u32[]{:S(2)}, u32[]{:S(2)}) collective-permute-start(f32[96,512]{1,0:T(8,128)S(1)} %get-tuple-element.74), channel_id=1, source_target_pairs={{0,5},{1,4},{2,7},{3,6},{4,1},{5,0},{6,3},{7,2},{8,13},{9,12},{10,... | collective-permute-start | bytes 589832 | tf_op jit(solution)/shard_map/ppermute | solution.py:233
  114.2 1.7 %collective-permute-done.27 = f32[96,512]{1,0:T(8,128)S(1)} collective-permute-done((f32[96,512]{1,0:T(8,128)S(1)}, f32[96,512]{1,0:T(8,128)S(1)}, u32[]{:S(2)}, u32[]{:S(2)}) %collective-permute-start.27) | collective-permute-done | bytes 196640 | tf_op jit(solution)/shard_map/ppermute | solution.py:233
  115.9 5.6 %collective-permute-done.26 = f32[96,512]{1,0:T(8,128)S(1)} collective-permute-done((f32[96,512]{1,0:T(8,128)S(1)}, f32[96,512]{1,0:T(8,128)S(1)}, u32[]{:S(2)}, u32[]{:S(2)}) %collective-permute-start.26) | collective-permute-done | bytes 196640 | tf_op jit(solution)/shard_map/ppermute | solution.py:233
  121.5 3.4 %collective-permute-done.24 = f32[96,512]{1,0:T(8,128)S(1)} collective-permute-done((f32[96,512]{1,0:T(8,128)S(1)}, f32[96,512]{1,0:T(8,128)S(1)}, u32[]{:S(2)}, u32[]{:S(2)}) %collective-permute-start.24) | collective-permute-done | bytes 196640 | tf_op jit(solution)/shard_map/ppermute | solution.py:233
  124.9 3.3 %collective-permute-done.25 = f32[96,512]{1,0:T(8,128)S(1)} collective-permute-done((f32[96,512]{1,0:T(8,128)S(1)}, f32[96,512]{1,0:T(8,128)S(1)}, u32[]{:S(2)}, u32[]{:S(2)}) %collective-permute-start.25) | collective-permute-done | bytes 196640 | tf_op jit(solution)/shard_map/ppermute | solution.py:233
  128.4 2.0 %collective-permute-start.31 = (f32[96,512]{1,0:T(8,128)S(1)}, f32[96,512]{1,0:T(8,128)S(1)}, u32[]{:S(2)}, u32[]{:S(2)}) collective-permute-start(f32[96,512]{1,0:T(8,128)S(1)} %fusion.2), channel_id=1, source_target_pairs={{0,5},{1,4},{2,7},{3,6},{4,1},{5,0},{6,3},{7,2},{8,13},{9,12},{10,... | collective-permute-start | bytes 589832 | tf_op jit(solution)/shard_map/ppermute | solution.py:237
  130.4 2.0 %collective-permute-start.32 = (f32[96,512]{1,0:T(8,128)S(1)}, f32[96,512]{1,0:T(8,128)S(1)}, u32[]{:S(2)}, u32[]{:S(2)}) collective-permute-start(f32[96,512]{1,0:T(8,128)S(1)} %fusion.2), channel_id=1, source_target_pairs={{0,4},{1,5},{2,6},{3,7},{4,0},{5,1},{6,2},{7,3},{8,12},{9,13},{10,... | collective-permute-start | bytes 589832 | tf_op jit(solution)/shard_map/ppermute | solution.py:237
  132.5 3.7 %place.1 = f32[3584,512]{1,0:T(8,128)S(1)} custom-call(s32[8]{0:T(128)S(1)} %pad_add_fusion.1.at_ref, f32[896,256]{1,0:T(8,128)} %copy-done.14, f32[896,256]{1,0:T(8,128)} %copy-done.16, f32[896,256]{1,0:T(8,128)} %copy-done.10, f32[896,256]{1,0:T(8,128)} %copy-done.11, f32[896,256]{1,0:T(8,128)} %copy-done.15, f32[896,256]{1,0:T(8,128)} %copy-done.9, ...), custom_call_target="tpu_custom_call" | custom-call | flops 1 | bytes 14680064 | tf_op jit(solution)/shard_map/place/pallas_call | solution.py:132
  136.3 4.1 %collective-permute-start.34 = (f32[96,512]{1,0:T(8,128)S(1)}, f32[96,512]{1,0:T(8,128)S(1)}, u32[]{:S(2)}, u32[]{:S(2)}) collective-permute-start(f32[96,512]{1,0:T(8,128)S(1)} %fusion.2), channel_id=1, source_target_pairs={{0,7},{1,6},{2,1},{3,0},{4,3},{5,2},{6,5},{7,4},{8,15},{9,14},{10,... | collective-permute-start | bytes 589832 | tf_op jit(solution)/shard_map/ppermute | solution.py:237
  140.4 3.2 %collective-permute-start.36 = (f32[96,512]{1,0:T(8,128)S(1)}, f32[96,512]{1,0:T(8,128)S(1)}, u32[]{:S(2)}, u32[]{:S(2)}) collective-permute-start(f32[96,512]{1,0:T(8,128)S(1)} %fusion.2), channel_id=1, source_target_pairs={{0,6},{1,7},{2,0},{3,1},{4,2},{5,3},{6,4},{7,5},{8,14},{9,15},{10,... | collective-permute-start | bytes 589832 | tf_op jit(solution)/shard_map/ppermute | solution.py:237
  143.9 3.1 %collective-permute-done.32 = f32[96,512]{1,0:T(8,128)S(1)} collective-permute-done((f32[96,512]{1,0:T(8,128)S(1)}, f32[96,512]{1,0:T(8,128)S(1)}, u32[]{:S(2)}, u32[]{:S(2)}) %collective-permute-start.32) | collective-permute-done | bytes 196640 | tf_op jit(solution)/shard_map/ppermute | solution.py:237
  146.9 1.6 collective-permute-start.37
  148.7 3.0 %collective-permute-done.35 = f32[96,512]{1,0:T(8,128)S(1)} collective-permute-done((f32[96,512]{1,0:T(8,128)S(1)}, f32[96,512]{1,0:T(8,128)S(1)}, u32[]{:S(2)}, u32[]{:S(2)}) %collective-permute-start.35) | collective-permute-done | bytes 196640 | tf_op jit(solution)/shard_map/ppermute | solution.py:237
  151.7 1.6 collective-permute-done.37
  153.4 11.8 %fusion.18 = f32[768,3584]{1,0:T(8,128)} fusion(f32[768,512]{1,0:T(8,128)S(1)} %constant_dynamic-update-slice_fusion, f32[3584,512]{1,0:T(8,128)S(1)} %place.1), kind=kOutput, calls=%fused_computation.86 | convolution fusion | flops 8455716864 | bytes 19922944 | tf_op jit(solution)/shard_map/dot_general | solution.py:239
  (119 shorter events, 16.6 us)
Async XLA Ops:
  0.0 53.4 %copy-start = (f32[28672]{0:T(1024)S(1)}, f32[28672]{0:T(1024)}, u32[]{:S(2)}) copy-start(f32[28672]{0:T(1024)} %param.11) | copy-start | bytes 344068
  1.7 13.0 %collective-permute-start = (f32[448,128]{1,0:T(8,128)S(1)}, f32[448,128]{1,0:T(8,128)S(1)}, u32[]{:S(2)}, u32[]{:S(2)}) collective-permute-start(f32[448,128]{1,0:T(8,128)S(1)} %get-tuple-element.70), channel_id=1, source_target_pairs={{0,16},{8,24},{16,0},{24,8},{32,48},{40,56},{48,32},{56,40},{64,80... | collective-permute-start | bytes 688136 | tf_op jit(solution)/shard_map/ppermute | solution.py:180
  4.9 18.6 %collective-permute-start.1 = (f32[448,128]{1,0:T(8,128)S(1)}, f32[448,128]{1,0:T(8,128)S(1)}, u32[]{:S(2)}, u32[]{:S(2)}) collective-permute-start(f32[448,128]{1,0:T(8,128)S(1)} %get-tuple-element.69), channel_id=1, source_target_pairs={{0,32},{8,40},{16,48},{24,56},{32,64},{40,72},{48,80},{56,88},{64,... | collective-permute-start | bytes 688136 | tf_op jit(solution)/shard_map/ppermute | solution.py:180
  6.8 27.7 %collective-permute-start.2 = (f32[448,128]{1,0:T(8,128)S(1)}, f32[448,128]{1,0:T(8,128)S(1)}, u32[]{:S(2)}, u32[]{:S(2)}) collective-permute-start(f32[448,128]{1,0:T(8,128)S(1)} %get-tuple-element.68), channel_id=1, source_target_pairs={{0,48},{8,56},{16,32},{24,40},{32,80},{40,88},{48,64},{56,72},{64,... | collective-permute-start | bytes 688136 | tf_op jit(solution)/shard_map/ppermute | solution.py:180
  8.7 25.8 %collective-permute-start.3 = (f32[448,128]{1,0:T(8,128)S(1)}, f32[448,128]{1,0:T(8,128)S(1)}, u32[]{:S(2)}, u32[]{:S(2)}) collective-permute-start(f32[448,128]{1,0:T(8,128)S(1)} %get-tuple-element.67), channel_id=1, source_target_pairs={{0,64},{8,72},{16,80},{24,88},{32,96},{40,104},{48,112},{56,120},{... | collective-permute-start | bytes 688136 | tf_op jit(solution)/shard_map/ppermute | solution.py:180
  10.4 24.1 %collective-permute-start.4 = (f32[448,128]{1,0:T(8,128)S(1)}, f32[448,128]{1,0:T(8,128)S(1)}, u32[]{:S(2)}, u32[]{:S(2)}) collective-permute-start(f32[448,128]{1,0:T(8,128)S(1)} %get-tuple-element.66), channel_id=1, source_target_pairs={{0,80},{8,88},{16,64},{24,72},{32,112},{40,120},{48,96},{56,104},{... | collective-permute-start | bytes 688136 | tf_op jit(solution)/shard_map/ppermute | solution.py:180
  14.7 19.8 %collective-permute-start.5 = (f32[448,128]{1,0:T(8,128)S(1)}, f32[448,128]{1,0:T(8,128)S(1)}, u32[]{:S(2)}, u32[]{:S(2)}) collective-permute-start(f32[448,128]{1,0:T(8,128)S(1)} %get-tuple-element.72), channel_id=1, source_target_pairs={{0,96},{8,104},{16,112},{24,120},{32,0},{40,8},{48,16},{56,24},{64... | collective-permute-start | bytes 688136 | tf_op jit(solution)/shard_map/ppermute | solution.py:180
  23.5 11.0 %collective-permute-start.6 = (f32[448,128]{1,0:T(8,128)S(1)}, f32[448,128]{1,0:T(8,128)S(1)}, u32[]{:S(2)}, u32[]{:S(2)}) collective-permute-start(f32[448,128]{1,0:T(8,128)S(1)} %get-tuple-element.65), channel_id=1, source_target_pairs={{0,112},{8,120},{16,96},{24,104},{32,16},{40,24},{48,0},{56,8},{64... | collective-permute-start | bytes 688136 | tf_op jit(solution)/shard_map/ppermute | solution.py:180
  23.6 10.8 %copy-start.19 = (s32[4]{0:T(128)S(1)}, s32[4]{0:T(128)}, u32[]{:S(2)}) copy-start(s32[4]{0:T(128)} %param.9) | copy-start | bytes 52
  35.4 1.9 %collective-permute-start.7 = (f32[2,448,128]{2,1,0:T(8,128)S(1)}, f32[2,448,128]{2,1,0:T(8,128)S(1)}, u32[]{:S(2)}, u32[]{:S(2)}) collective-permute-start(f32[2,448,128]{2,1,0:T(8,128)S(1)} %get-tuple-element.47), channel_id=1, source_target_pairs={{0,8},{8,0},{16,24},{24,16},{32,40},{40,32},{48,56},{56,48},{64,72... | collective-permute-start | bytes 1376264 | tf_op jit(solution)/shard_map/ppermute | solution.py:186
  37.9 18.8 %collective-permute-start.8 = (f32[448,128]{1,0:T(8,128)S(1)}, f32[448,128]{1,0:T(8,128)}, u32[]{:S(2)}, u32[]{:S(2)}) collective-permute-start(f32[448,128]{1,0:T(8,128)S(1)} %get-tuple-element.48), channel_id=1, source_target_pairs={{0,16},{8,24},{16,0},{24,8},{32,48},{40,56},{48,32},{56,40},{64,80... | collective-permute-start | bytes 688136 | tf_op jit(solution)/shard_map/ppermute | solution.py:189
  56.6 8.9 %collective-permute-start.13 = (f32[448,128]{1,0:T(8,128)S(1)}, f32[448,128]{1,0:T(8,128)S(1)}, u32[]{:S(2)}, u32[]{:S(2)}) collective-permute-start(f32[448,128]{1,0:T(8,128)S(1)} %get-tuple-element.52), channel_id=1, source_target_pairs={{0,16},{8,24},{16,0},{24,8},{32,48},{40,56},{48,32},{56,40},{64,80... | collective-permute-start | bytes 688136 | tf_op jit(solution)/shard_map/ppermute | solution.py:189
  57.7 11.1 %collective-permute-start.9 = (f32[896,128]{1,0:T(8,128)S(1)}, f32[896,128]{1,0:T(8,128)S(1)}, u32[]{:S(2)}, u32[]{:S(2)}) collective-permute-start(f32[896,128]{1,0:T(8,128)S(1)} %pad_maximum_fusion.7), channel_id=1, source_target_pairs={{0,32},{8,104},{16,48},{24,120},{32,64},{40,8},{48,80},{56,24},{64... | collective-permute-start | bytes 1376264 | tf_op jit(solution)/shard_map/ppermute | solution.py:217
  59.1 9.7 %collective-permute-start.10 = (f32[896,128]{1,0:T(8,128)S(1)}, f32[896,128]{1,0:T(8,128)S(1)}, u32[]{:S(2)}, u32[]{:S(2)}) collective-permute-start(f32[896,128]{1,0:T(8,128)S(1)} %pad_maximum_fusion.7), channel_id=1, source_target_pairs={{0,8},{8,0},{16,24},{24,16},{32,40},{40,32},{48,56},{56,48},{64,72... | collective-permute-start | bytes 1376264 | tf_op jit(solution)/shard_map/ppermute | solution.py:218
  65.6 1.8 %copy-start.7 = (f32[768,896]{1,0:T(8,128)S(1)}, f32[768,896]{1,0:T(8,128)}, u32[]{:S(2)}) copy-start(f32[768,896]{1,0:T(8,128)} %copy-done.6) | copy-start | bytes 8257540
  65.6 5.9 %collective-permute-start.14 = (f32[896,128]{1,0:T(8,128)S(1)}, f32[896,128]{1,0:T(8,128)S(1)}, u32[]{:S(2)}, u32[]{:S(2)}) collective-permute-start(f32[896,128]{1,0:T(8,128)S(1)} %pad_maximum_fusion.8), channel_id=1, source_target_pairs={{0,8},{8,0},{16,24},{24,16},{32,40},{40,32},{48,56},{56,48},{64,72... | collective-permute-start | bytes 1376264 | tf_op jit(solution)/shard_map/ppermute | solution.py:218
  65.7 10.4 %collective-permute-start.17 = (f32[896,128]{1,0:T(8,128)S(1)}, f32[896,128]{1,0:T(8,128)S(1)}, u32[]{:S(2)}, u32[]{:S(2)}) collective-permute-start(f32[896,128]{1,0:T(8,128)S(1)} %pad_maximum_fusion.8), channel_id=1, source_target_pairs={{0,32},{8,104},{16,48},{24,120},{32,64},{40,8},{48,80},{56,24},{64... | collective-permute-start | bytes 1376264 | tf_op jit(solution)/shard_map/ppermute | solution.py:217
  68.8 12.2 %collective-permute-start.11 = (f32[896,128]{1,0:T(8,128)S(1)}, f32[896,128]{1,0:T(8,128)S(1)}, u32[]{:S(2)}, u32[]{:S(2)}) collective-permute-start(f32[896,128]{1,0:T(8,128)S(1)} %collective-permute-done.9), channel_id=1, source_target_pairs={{0,32},{8,104},{16,48},{24,120},{32,64},{40,8},{48,80},{56,24},{64... | collective-permute-start | bytes 1376264 | tf_op jit(solution)/shard_map/ppermute | solution.py:217
  70.2 10.8 %collective-permute-start.12 = (f32[896,128]{1,0:T(8,128)S(1)}, f32[896,128]{1,0:T(8,128)S(1)}, u32[]{:S(2)}, u32[]{:S(2)}) collective-permute-start(f32[896,128]{1,0:T(8,128)S(1)} %collective-permute-done.9), channel_id=1, source_target_pairs={{0,8},{8,0},{16,24},{24,16},{32,40},{40,32},{48,56},{56,48},{64,72... | collective-permute-start | bytes 1376264 | tf_op jit(solution)/shard_map/ppermute | solution.py:218
  71.6 4.8 %copy-start.3 = (f32[768,896]{1,0:T(8,128)S(1)}, f32[768,896]{1,0:T(8,128)}, u32[]{:S(2)}) copy-start(f32[768,896]{1,0:T(8,128)} %copy-done.2) | copy-start | bytes 8257540
  76.1 7.2 %collective-permute-start.18 = (f32[896,128]{1,0:T(8,128)S(1)}, f32[896,128]{1,0:T(8,128)S(1)}, u32[]{:S(2)}, u32[]{:S(2)}) collective-permute-start(f32[896,128]{1,0:T(8,128)S(1)} %collective-permute-done.17), channel_id=1, source_target_pairs={{0,8},{8,0},{16,24},{24,16},{32,40},{40,32},{48,56},{56,48},{64,72... | collective-permute-start | bytes 1376264 | tf_op jit(solution)/shard_map/ppermute | solution.py:218
  76.2 1.7 %copy-start.16 = (f32[896,256]{1,0:T(8,128)}, f32[896,256]{1,0:T(8,128)S(1)}, u32[]{:S(2)}) copy-start(f32[896,256]{1,0:T(8,128)S(1)} %pad_maximum_fusion.1.refs_1_) | copy-start | bytes 2752516
  76.2 9.9 %collective-permute-start.19 = (f32[896,128]{1,0:T(8,128)S(1)}, f32[896,128]{1,0:T(8,128)S(1)}, u32[]{:S(2)}, u32[]{:S(2)}) collective-permute-start(f32[896,128]{1,0:T(8,128)S(1)} %collective-permute-done.17), channel_id=1, source_target_pairs={{0,32},{8,104},{16,48},{24,120},{32,64},{40,8},{48,80},{56,24},{64... | collective-permute-start | bytes 1376264 | tf_op jit(solution)/shard_map/ppermute | solution.py:217
  81.0 10.0 %collective-permute-start.15 = (f32[896,128]{1,0:T(8,128)S(1)}, f32[896,128]{1,0:T(8,128)S(1)}, u32[]{:S(2)}, u32[]{:S(2)}) collective-permute-start(f32[896,128]{1,0:T(8,128)S(1)} %collective-permute-done.11), channel_id=1, source_target_pairs={{0,32},{8,104},{16,48},{24,120},{32,64},{40,8},{48,80},{56,24},{64... | collective-permute-start | bytes 1376264 | tf_op jit(solution)/shard_map/ppermute | solution.py:217
  81.0 10.0 %collective-permute-start.16 = (f32[896,128]{1,0:T(8,128)S(1)}, f32[896,128]{1,0:T(8,128)S(1)}, u32[]{:S(2)}, u32[]{:S(2)}) collective-permute-start(f32[896,128]{1,0:T(8,128)S(1)} %collective-permute-done.11), channel_id=1, source_target_pairs={{0,8},{8,0},{16,24},{24,16},{32,40},{40,32},{48,56},{56,48},{64,72... | collective-permute-start | bytes 1376264 | tf_op jit(solution)/shard_map/ppermute | solution.py:218
  83.3 5.1 %copy-start.9 = (f32[896,256]{1,0:T(8,128)}, f32[896,256]{1,0:T(8,128)S(1)}, u32[]{:S(2)}) copy-start(f32[896,256]{1,0:T(8,128)S(1)} %pad_maximum_fusion.2.refs_5_) | copy-start | bytes 2752516
  86.1 9.8 %collective-permute-start.20 = (f32[896,128]{1,0:T(8,128)S(1)}, f32[896,128]{1,0:T(8,128)S(1)}, u32[]{:S(2)}, u32[]{:S(2)}) collective-permute-start(f32[896,128]{1,0:T(8,128)S(1)} %collective-permute-done.19), channel_id=1, source_target_pairs={{0,32},{8,104},{16,48},{24,120},{32,64},{40,8},{48,80},{56,24},{64... | collective-permute-start | bytes 1376264 | tf_op jit(solution)/shard_map/ppermute | solution.py:217
  86.1 2.3 %copy-start.5 = (f32[768,896]{1,0:T(8,128)S(1)}, f32[768,896]{1,0:T(8,128)}, u32[]{:S(2)}) copy-start(f32[768,896]{1,0:T(8,128)} %copy-done.4) | copy-start | bytes 8257540
  86.2 9.9 %copy-start.10 = (f32[896,256]{1,0:T(8,128)}, f32[896,256]{1,0:T(8,128)S(1)}, u32[]{:S(2)}) copy-start(f32[896,256]{1,0:T(8,128)S(1)} %pad_maximum_fusion.3.refs_2_) | copy-start | bytes 2752516
  86.3 13.3 %collective-permute-start.21 = (f32[896,128]{1,0:T(8,128)S(1)}, f32[896,128]{1,0:T(8,128)S(1)}, u32[]{:S(2)}, u32[]{:S(2)}) collective-permute-start(f32[896,128]{1,0:T(8,128)S(1)} %collective-permute-done.19), channel_id=1, source_target_pairs={{0,8},{8,0},{16,24},{24,16},{32,40},{40,32},{48,56},{56,48},{64,72... | collective-permute-start | bytes 1376264 | tf_op jit(solution)/shard_map/ppermute | solution.py:218
  96.0 2.1 %copy-start.11 = (f32[896,256]{1,0:T(8,128)}, f32[896,256]{1,0:T(8,128)S(1)}, u32[]{:S(2)}) copy-start(f32[896,256]{1,0:T(8,128)S(1)} %pad_maximum_fusion.4.refs_3_) | copy-start | bytes 2752516
  96.0 5.1 %collective-permute-start.22 = (f32[896,128]{1,0:T(8,128)S(1)}, f32[896,128]{1,0:T(8,128)S(1)}, u32[]{:S(2)}, u32[]{:S(2)}) collective-permute-start(f32[896,128]{1,0:T(8,128)S(1)} %collective-permute-done.15), channel_id=1, source_target_pairs={{0,8},{8,0},{16,24},{24,16},{32,40},{40,32},{48,56},{56,48},{64,72... | collective-permute-start | bytes 1376264 | tf_op jit(solution)/shard_map/ppermute | solution.py:218
  97.6 3.5 %collective-permute-start.23 = (f32[896,128]{1,0:T(8,128)S(1)}, f32[896,128]{1,0:T(8,128)S(1)}, u32[]{:S(2)}, u32[]{:S(2)}) collective-permute-start(f32[896,128]{1,0:T(8,128)S(1)} %collective-permute-done.20), channel_id=1, source_target_pairs={{0,8},{8,0},{16,24},{24,16},{32,40},{40,32},{48,56},{56,48},{64,72... | collective-permute-start | bytes 1376264 | tf_op jit(solution)/shard_map/ppermute | solution.py:218
  102.6 8.0 %collective-permute-start.30 = (f32[96,512]{1,0:T(8,128)S(1)}, f32[96,512]{1,0:T(8,128)S(1)}, u32[]{:S(2)}, u32[]{:S(2)}) collective-permute-start(f32[96,512]{1,0:T(8,128)S(1)} %fusion.9), channel_id=1, source_target_pairs={{0,1},{1,0},{2,3},{3,2},{4,5},{5,4},{6,7},{7,6},{8,9},{9,8},{10,11... | collective-permute-start | bytes 589832 | tf_op jit(solution)/shard_map/ppermute | solution.py:233
  103.5 10.3 %collective-permute-start.29 = (f32[96,512]{1,0:T(8,128)S(1)}, f32[96,512]{1,0:T(8,128)S(1)}, u32[]{:S(2)}, u32[]{:S(2)}) collective-permute-start(f32[96,512]{1,0:T(8,128)S(1)} %get-tuple-element.78), channel_id=1, source_target_pairs={{0,6},{1,7},{2,0},{3,1},{4,2},{5,3},{6,4},{7,5},{8,14},{9,15},{10,... | collective-permute-start | bytes 589832 | tf_op jit(solution)/shard_map/ppermute | solution.py:233
  106.5 7.7 %collective-permute-start.28 = (f32[96,512]{1,0:T(8,128)S(1)}, f32[96,512]{1,0:T(8,128)S(1)}, u32[]{:S(2)}, u32[]{:S(2)}) collective-permute-start(f32[96,512]{1,0:T(8,128)S(1)} %get-tuple-element.77), channel_id=1, source_target_pairs={{0,2},{1,3},{2,4},{3,5},{4,6},{5,7},{6,0},{7,1},{8,10},{9,11},{10,... | collective-permute-start | bytes 589832 | tf_op jit(solution)/shard_map/ppermute | solution.py:233
  106.5 9.4 %collective-permute-start.27 = (f32[96,512]{1,0:T(8,128)S(1)}, f32[96,512]{1,0:T(8,128)S(1)}, u32[]{:S(2)}, u32[]{:S(2)}) collective-permute-start(f32[96,512]{1,0:T(8,128)S(1)} %get-tuple-element.76), channel_id=1, source_target_pairs={{0,7},{1,6},{2,1},{3,0},{4,3},{5,2},{6,5},{7,4},{8,15},{9,14},{10,... | collective-permute-start | bytes 589832 | tf_op jit(solution)/shard_map/ppermute | solution.py:233
  110.7 10.9 %collective-permute-start.26 = (f32[96,512]{1,0:T(8,128)S(1)}, f32[96,512]{1,0:T(8,128)S(1)}, u32[]{:S(2)}, u32[]{:S(2)}) collective-permute-start(f32[96,512]{1,0:T(8,128)S(1)} %get-tuple-element.75), channel_id=1, source_target_pairs={{0,3},{1,2},{2,5},{3,4},{4,7},{5,6},{6,1},{7,0},{8,11},{9,10},{10,... | collective-permute-start | bytes 589832 | tf_op jit(solution)/shard_map/ppermute | solution.py:233
  110.7 14.3 %collective-permute-start.24 = (f32[96,512]{1,0:T(8,128)S(1)}, f32[96,512]{1,0:T(8,128)S(1)}, u32[]{:S(2)}, u32[]{:S(2)}) collective-permute-start(f32[96,512]{1,0:T(8,128)S(1)} %get-tuple-element.74), channel_id=1, source_target_pairs={{0,5},{1,4},{2,7},{3,6},{4,1},{5,0},{6,3},{7,2},{8,13},{9,12},{10,... | collective-permute-start | bytes 589832 | tf_op jit(solution)/shard_map/ppermute | solution.py:233
  113.7 14.5 %collective-permute-start.25 = (f32[96,512]{1,0:T(8,128)S(1)}, f32[96,512]{1,0:T(8,128)S(1)}, u32[]{:S(2)}, u32[]{:S(2)}) collective-permute-start(f32[96,512]{1,0:T(8,128)S(1)} %get-tuple-element.73), channel_id=1, source_target_pairs={{0,4},{1,5},{2,6},{3,7},{4,0},{5,1},{6,2},{7,3},{8,12},{9,13},{10,... | collective-permute-start | bytes 589832 | tf_op jit(solution)/shard_map/ppermute | solution.py:233
  128.4 12.0 %collective-permute-start.31 = (f32[96,512]{1,0:T(8,128)S(1)}, f32[96,512]{1,0:T(8,128)S(1)}, u32[]{:S(2)}, u32[]{:S(2)}) collective-permute-start(f32[96,512]{1,0:T(8,128)S(1)} %fusion.2), channel_id=1, source_target_pairs={{0,5},{1,4},{2,7},{3,6},{4,1},{5,0},{6,3},{7,2},{8,13},{9,12},{10,... | collective-permute-start | bytes 589832 | tf_op jit(solution)/shard_map/ppermute | solution.py:237
  130.4 16.5 %collective-permute-start.32 = (f32[96,512]{1,0:T(8,128)S(1)}, f32[96,512]{1,0:T(8,128)S(1)}, u32[]{:S(2)}, u32[]{:S(2)}) collective-permute-start(f32[96,512]{1,0:T(8,128)S(1)} %fusion.2), channel_id=1, source_target_pairs={{0,4},{1,5},{2,6},{3,7},{4,0},{5,1},{6,2},{7,3},{8,12},{9,13},{10,... | collective-permute-start | bytes 589832 | tf_op jit(solution)/shard_map/ppermute | solution.py:237
  136.2 12.4 %collective-permute-start.33 = (f32[96,512]{1,0:T(8,128)S(1)}, f32[96,512]{1,0:T(8,128)S(1)}, u32[]{:S(2)}, u32[]{:S(2)}) collective-permute-start(f32[96,512]{1,0:T(8,128)S(1)} %fusion.2), channel_id=1, source_target_pairs={{0,3},{1,2},{2,5},{3,4},{4,7},{5,6},{6,1},{7,0},{8,11},{9,10},{10,... | collective-permute-start | bytes 589832 | tf_op jit(solution)/shard_map/ppermute | solution.py:237
  136.3 12.3 %collective-permute-start.34 = (f32[96,512]{1,0:T(8,128)S(1)}, f32[96,512]{1,0:T(8,128)S(1)}, u32[]{:S(2)}, u32[]{:S(2)}) collective-permute-start(f32[96,512]{1,0:T(8,128)S(1)} %fusion.2), channel_id=1, source_target_pairs={{0,7},{1,6},{2,1},{3,0},{4,3},{5,2},{6,5},{7,4},{8,15},{9,14},{10,... | collective-permute-start | bytes 589832 | tf_op jit(solution)/shard_map/ppermute | solution.py:237
  140.4 11.3 %collective-permute-start.35 = (f32[96,512]{1,0:T(8,128)S(1)}, f32[96,512]{1,0:T(8,128)S(1)}, u32[]{:S(2)}, u32[]{:S(2)}) collective-permute-start(f32[96,512]{1,0:T(8,128)S(1)} %fusion.2), channel_id=1, source_target_pairs={{0,2},{1,3},{2,4},{3,5},{4,6},{5,7},{6,0},{7,1},{8,10},{9,11},{10,... | collective-permute-start | bytes 589832 | tf_op jit(solution)/shard_map/ppermute | solution.py:237
  140.4 11.3 %collective-permute-start.36 = (f32[96,512]{1,0:T(8,128)S(1)}, f32[96,512]{1,0:T(8,128)S(1)}, u32[]{:S(2)}, u32[]{:S(2)}) collective-permute-start(f32[96,512]{1,0:T(8,128)S(1)} %fusion.2), channel_id=1, source_target_pairs={{0,6},{1,7},{2,0},{3,1},{4,2},{5,3},{6,4},{7,5},{8,14},{9,15},{10,... | collective-permute-start | bytes 589832 | tf_op jit(solution)/shard_map/ppermute | solution.py:237
  146.9 6.4 %collective-permute-start.37 = (f32[96,512]{1,0:T(8,128)S(1)}, f32[96,512]{1,0:T(8,128)S(1)}, u32[]{:S(2)}, u32[]{:S(2)}) collective-permute-start(f32[96,512]{1,0:T(8,128)S(1)} %fusion.2), channel_id=1, source_target_pairs={{0,1},{1,0},{2,3},{3,2},{4,5},{5,4},{6,7},{7,6},{8,9},{9,8},{10,11... | collective-permute-start | bytes 589832 | tf_op jit(solution)/shard_map/ppermute | solution.py:237
  153.4 11.8 %copy-start.1 = (f32[28672]{0:T(1024)S(1)}, f32[28672]{0:T(1024)}, u32[]{:S(2)}) copy-start(f32[28672]{0:T(1024)} %param.11) | copy-start | bytes 344068
  (10 other events, 13.2 us)

commit v6 on v5

--- a/solution.py
+++ b/solution.py
@@ -25,12 +25,6 @@
 
 def stay(value):
     return pltpu.with_memory_space_constraint(value, pltpu.HBM)
-
-
-def ordered(first, mine, other):
-    low = jnp.where(first, mine, other)
-    high = jnp.where(first, other, mine)
-    return jnp.concatenate([low, high], axis=0)
 
 
 def rotate_body(at_ref, *refs):
@@ -110,6 +104,25 @@
         cost_estimate=pl.CostEstimate(flops=1, bytes_accessed=mine.size * 8, transcendentals=0),
         name="settle",
     )(at, mine, got)
+
+
+def join_body(at_ref, mine_ref, other_ref, out_ref):
+    deep, x = mine_ref.shape[0], at_ref[NSEL + 2]
+    out_ref[pl.ds(pl.multiple_of(x * deep, 64), deep)] = mine_ref[...]
+    out_ref[pl.ds(pl.multiple_of((1 - x) * deep, 64), deep)] = other_ref[...]
+
+
+def join(at, mine, other):
+    deep, lanes = mine.shape
+    return pl.pallas_call(
+        join_body,
+        out_shape=jax.ShapeDtypeStruct((2 * deep, lanes), F32),
+        in_specs=[SM, VM, VM],
+        out_specs=VM,
+        compiler_params=pltpu.CompilerParams(vmem_limit_bytes=8 << 20),
+        cost_estimate=pl.CostEstimate(flops=1, bytes_accessed=mine.size * 16, transcendentals=0),
+        name="join",
+    )(at, mine, other)
 
 
 def place_body(at_ref, *refs):
@@ -186,7 +199,7 @@
     halves = settle(chosen, mine, lax.ppermute(give, "rows", CORE))
     own = [[], []]
     for c, half in enumerate(halves):
-        own[c].append(ordered(x == 0, half, lax.ppermute(half, "rows", XPAIR)))
+        own[c].append(join(chosen, half, lax.ppermute(half, "rows", XPAIR)))
 
     g = rotate(at, gradient, (2,))
     own[0][0], g2 = lax.optimization_barrier((own[0][0], *g))

time: 166 us -> 167 us (level)
  waiting for transfers between devices: 50.4 us -> 44.9 us
  local copies, waits for them, and re-layouts: 15.1 us -> 17.5 us
  starting transfers between devices: 57.5 us -> 59.5 us
    ppermute x7, starting transfers between devices: 11.4 us -> 16 us  [shards(): lax.ppermute(part, 'cols', across(*turn))]
    ppermute x2, waiting for transfers between devices: 4.34 us -> 0.01 us  [shards(): own[c].append(join(chosen, half, lax.ppermute(half, 'rows', XPAIR)))]
    ppermute x7, waiting for transfers between devices: 14 us -> 10.2 us  [shards(): lax.ppermute(part, 'cols', across(*turn))]
    ppermute x6, waiting for transfers between devices: 15.1 us -> 18 us  [shards(): own[c].append(lax.ppermute(held, 'rows', RING))]
    unnamed x40 -> x48, local copies, waits for them, and re-layouts: 6.74 us -> 6.34 us
  transfers between devices with their start and end apart: 38 -> 38, of which waited for: 15 -> 15; matrix products, arithmetic and copies ran while one was open for 11% -> 13% of each run, Pallas kernels for 9% -> 10%
where the time goes in v6:
time: 167 us; the launch traced here: 166 us
  starting transfers between devices  59.5 us (36%)
  waiting for transfers between devices  44.9 us (27%)
  matrix products  23.2 us (14%)
  Pallas kernels  17.7 us (11%)
  local copies, waits for them, and re-layouts  17.5 us (10%)
  other arithmetic  2.94 us (2%)
    ppermute x6, waiting for transfers between devices, shards(): own[c].append(lax.ppermute(held, 'rows', RING))  18 us
    ppermute x7, starting transfers between devices, shards(): lax.ppermute(part, 'cols', across(*turn))  16 us
    ppermute x7, starting transfers between devices, shards(): arrived[dz, dx] = lax.ppermute(eighth(dz, dx), 'rows', away(dz, dx))  14.3 us
    ppermute x7, starting transfers between devices, shards(): lax.ppermute(scaled_block, 'cols', across(*turn))  12 us
    dot_general x1, matrix products, shards(): lax.dot_general(scaled, v, (((1,), (1,)), ((), ())), precision=lax.Precis...  11.8 us
    dot_general x8, matrix products, dot(): jnp.dot(a, b, precision=lax.Precision.HIGH, preferred_element_type=F32)  11.4 us
    pallas_call x2, Pallas kernels, rotate(): pl.pallas_call(rotate_body, grid_spec=pltpu.PrefetchScalarGridSpec(num_sc...  11 us
    ppermute x7, waiting for transfers between devices, shards(): lax.ppermute(part, 'cols', across(*turn))  10.2 us
  transfers between devices with their start and end apart: 38, of which 15 were waited for; matrix products, arithmetic and copies ran while one was open for 13% of the time, Pallas kernels for 10%

profile of v6, /device:TPU:0, one launch (start us, length us, event | category | flops | bytes accessed | tf_op | source)
XLA Modules:
  0.0 166.4 jit_solution(8716907969490405355)
XLA Ops:
  0.0 1.7 %dynamic-slice_bitcast_fusion = (f32[448,128]{1,0:T(8,128)S(1)}, f32[448,128]{1,0:T(8,128)S(1)}, f32[448,128]{1,0:T(8,128)S(1)}, f32[448,128]{1,0:T(8,128)S(1)},...) fusion(f32[1,3584,128]{2,1,0:T(8,128)} %param.8, ...), kind=kLoop, calls=%fused_computation.31 | loop fusion | bytes 3670048 | tf_op jit(solution)/shard_map/dynamic_slice | solution.py:189
  1.7 3.2 %collective-permute-start = (f32[448,128]{1,0:T(8,128)S(1)}, f32[448,128]{1,0:T(8,128)S(1)}, u32[]{:S(2)}, u32[]{:S(2)}) collective-permute-start(f32[448,128]{1,0:T(8,128)S(1)} %get-tuple-element.70), channel_id=1, source_target_pairs={{0,16},{8,24},{16,0},{24,8},{32,48},{40,56},{48,32},{56,40},{64,80... | collective-permute-start | bytes 688136 | tf_op jit(solution)/shard_map/ppermute | solution.py:193
  4.9 1.9 %collective-permute-start.1 = (f32[448,128]{1,0:T(8,128)S(1)}, f32[448,128]{1,0:T(8,128)S(1)}, u32[]{:S(2)}, u32[]{:S(2)}) collective-permute-start(f32[448,128]{1,0:T(8,128)S(1)} %get-tuple-element.69), channel_id=1, source_target_pairs={{0,32},{8,40},{16,48},{24,56},{32,64},{40,72},{48,80},{56,88},{64,... | collective-permute-start | bytes 688136 | tf_op jit(solution)/shard_map/ppermute | solution.py:193
  6.9 1.9 %collective-permute-start.2 = (f32[448,128]{1,0:T(8,128)S(1)}, f32[448,128]{1,0:T(8,128)S(1)}, u32[]{:S(2)}, u32[]{:S(2)}) collective-permute-start(f32[448,128]{1,0:T(8,128)S(1)} %get-tuple-element.68), channel_id=1, source_target_pairs={{0,48},{8,56},{16,32},{24,40},{32,80},{40,88},{48,64},{56,72},{64,... | collective-permute-start | bytes 688136 | tf_op jit(solution)/shard_map/ppermute | solution.py:193
  8.7 1.7 %collective-permute-start.3 = (f32[448,128]{1,0:T(8,128)S(1)}, f32[448,128]{1,0:T(8,128)S(1)}, u32[]{:S(2)}, u32[]{:S(2)}) collective-permute-start(f32[448,128]{1,0:T(8,128)S(1)} %get-tuple-element.67), channel_id=1, source_target_pairs={{0,64},{8,72},{16,80},{24,88},{32,96},{40,104},{48,112},{56,120},{... | collective-permute-start | bytes 688136 | tf_op jit(solution)/shard_map/ppermute | solution.py:193
  10.4 4.3 %collective-permute-start.4 = (f32[448,128]{1,0:T(8,128)S(1)}, f32[448,128]{1,0:T(8,128)S(1)}, u32[]{:S(2)}, u32[]{:S(2)}) collective-permute-start(f32[448,128]{1,0:T(8,128)S(1)} %get-tuple-element.66), channel_id=1, source_target_pairs={{0,80},{8,88},{16,64},{24,72},{32,112},{40,120},{48,96},{56,104},{... | collective-permute-start | bytes 688136 | tf_op jit(solution)/shard_map/ppermute | solution.py:193
  16.0 7.5 %collective-permute-done.1.refs_2_ = f32[448,128]{1,0:T(8,128)S(1)} collective-permute-done((f32[448,128]{1,0:T(8,128)S(1)}, f32[448,128]{1,0:T(8,128)S(1)}, u32[]{:S(2)}, u32[]{:S(2)}) %collective-permute-start.1) | collective-permute-done | bytes 229408 | tf_op jit(solution)/shard_map/ppermute | solution.py:193
  23.6 6.2 %rotate.2 = (f32[768,896]{1,0:T(8,128)S(1)}, f32[768,896]{1,0:T(8,128)S(1)}, f32[768,896]{1,0:T(8,128)S(1)}) custom-call(s32[8]{0:T(128)S(1)} %pad_add_fusion.1.at_ref, f32[768,3584]{1,0:T(8,128)} %refs_0_.3, f32[768,3584]{1,0:T(8,128)} %refs_0_.3, f32[768,3584]{1,0:T(8,128)} %refs_0_.3), custom_call_target="tpu_custom_call" | custom-call | flops 1 | bytes 16515072 | tf_op jit(solution)/shard_map/rotate/pallas_call | solution.py:40
  29.9 1.5 copy-done.2
  31.4 1.5 copy-done.4
  32.9 1.5 copy-done.6
  37.9 6.8 %collective-permute-start.8 = (f32[448,128]{1,0:T(8,128)S(1)}, f32[448,128]{1,0:T(8,128)S(1)}, u32[]{:S(2)}, u32[]{:S(2)}) collective-permute-start(f32[448,128]{1,0:T(8,128)S(1)} %get-tuple-element.48.mine_ref), channel_id=1, source_target_pairs={{0,16},{8,24},{16,0},{24,8},{32,48},{40,56},{48,32},{56,40},{64,80... | collective-permute-start | bytes 688136 | tf_op jit(solution)/shard_map/ppermute | solution.py:202
  45.5 4.8 %rotate.3 = f32[768,896]{1,0:T(8,128)S(1)} custom-call(s32[8]{0:T(128)S(1)} %copy-done.11, f32[768,3584]{1,0:T(8,128)} %refs_0_.3), custom_call_target="tpu_custom_call" | custom-call | flops 1 | bytes 5505024 | tf_op jit(solution)/shard_map/rotate/pallas_call | solution.py:40
  50.4 4.7 %gather_fusion = f32[512]{0:T(512)} fusion(f32[8192]{0:T(1024)} %param.10, s32[1024]{0:T(1024)} %pad_clamp_fusion.1), kind=kCustom, calls=%fused_computation | custom fusion | bytes 6144 | tf_op jit(solution)/shard_map/gather | solution.py:182
  55.2 4.4 %gather_fusion.1 = f32[512]{0:T(512)} fusion(f32[28672]{0:T(1024)S(1)} %copy-done, s32[1024]{0:T(1024)} %pad_clamp_fusion), kind=kCustom, calls=%fused_computation.1 | custom fusion | bytes 6144 | tf_op jit(solution)/shard_map/gather | solution.py:182
  62.8 2.2 %collective-permute-start.10 = (f32[896,128]{1,0:T(8,128)S(1)}, f32[896,128]{1,0:T(8,128)S(1)}, u32[]{:S(2)}, u32[]{:S(2)}) collective-permute-start(f32[896,128]{1,0:T(8,128)S(1)} %join.2), channel_id=1, source_target_pairs={{0,8},{8,0},{16,24},{24,16},{32,40},{40,32},{48,56},{56,48},{64,72... | collective-permute-start | bytes 1376264 | tf_op jit(solution)/shard_map/ppermute | solution.py:231
  66.9 1.4 fusion.15
  68.4 3.5 %collective-permute-done.9 = f32[896,128]{1,0:T(8,128)S(1)} collective-permute-done((f32[896,128]{1,0:T(8,128)S(1)}, f32[896,128]{1,0:T(8,128)S(1)}, u32[]{:S(2)}, u32[]{:S(2)}) %collective-permute-start.9) | collective-permute-done | bytes 458784 | tf_op jit(solution)/shard_map/ppermute | solution.py:230
  71.9 1.7 collective-permute-start.12
  75.0 1.7 %collective-permute-done.17 = f32[896,128]{1,0:T(8,128)S(1)} collective-permute-done((f32[896,128]{1,0:T(8,128)S(1)}, f32[896,128]{1,0:T(8,128)S(1)}, u32[]{:S(2)}, u32[]{:S(2)}) %collective-permute-start.17) | collective-permute-done | bytes 458784 | tf_op jit(solution)/shard_map/ppermute | solution.py:230
  77.1 1.4 fusion.17
  78.6 3.1 %collective-permute-done.11 = f32[896,128]{1,0:T(8,128)S(1)} collective-permute-done((f32[896,128]{1,0:T(8,128)S(1)}, f32[896,128]{1,0:T(8,128)S(1)}, u32[]{:S(2)}, u32[]{:S(2)}) %collective-permute-start.11) | collective-permute-done | bytes 458784 | tf_op jit(solution)/shard_map/ppermute | solution.py:230
  81.7 1.7 collective-permute-start.16
  83.4 3.4 %collective-permute-done.19 = f32[896,128]{1,0:T(8,128)S(1)} collective-permute-done((f32[896,128]{1,0:T(8,128)S(1)}, f32[896,128]{1,0:T(8,128)S(1)}, u32[]{:S(2)}, u32[]{:S(2)}) %collective-permute-start.19) | collective-permute-done | bytes 458784 | tf_op jit(solution)/shard_map/ppermute | solution.py:230
  87.0 1.5 collective-permute-start.21
  88.9 1.4 convolution_add_fusion.4
  91.7 4.9 %collective-permute-done.20 = f32[896,128]{1,0:T(8,128)S(1)} collective-permute-done((f32[896,128]{1,0:T(8,128)S(1)}, f32[896,128]{1,0:T(8,128)S(1)}, u32[]{:S(2)}, u32[]{:S(2)}) %collective-permute-start.20) | collective-permute-done | bytes 458784 | tf_op jit(solution)/shard_map/ppermute | solution.py:230
  96.8 1.4 convolution_add_fusion.3
  98.8 1.4 convolution_add_fusion.2
  100.3 1.4 convolution_add_fusion.1
  101.9 1.4 convolution_add_fusion
  103.3 2.0 %collective-permute-start.30 = (f32[96,512]{1,0:T(8,128)S(1)}, f32[96,512]{1,0:T(8,128)S(1)}, u32[]{:S(2)}, u32[]{:S(2)}) collective-permute-start(f32[96,512]{1,0:T(8,128)S(1)} %fusion.9), channel_id=1, source_target_pairs={{0,1},{1,0},{2,3},{3,2},{4,5},{5,4},{6,7},{7,6},{8,9},{9,8},{10,11... | collective-permute-start | bytes 589832 | tf_op jit(solution)/shard_map/ppermute | solution.py:246
  105.5 3.1 %collective-permute-start.29 = (f32[96,512]{1,0:T(8,128)S(1)}, f32[96,512]{1,0:T(8,128)S(1)}, u32[]{:S(2)}, u32[]{:S(2)}) collective-permute-start(f32[96,512]{1,0:T(8,128)S(1)} %get-tuple-element.78), channel_id=1, source_target_pairs={{0,6},{1,7},{2,0},{3,1},{4,2},{5,3},{6,4},{7,5},{8,14},{9,15},{10,... | collective-permute-start | bytes 589832 | tf_op jit(solution)/shard_map/ppermute | solution.py:246
  108.5 2.8 %collective-permute-start.27 = (f32[96,512]{1,0:T(8,128)S(1)}, f32[96,512]{1,0:T(8,128)S(1)}, u32[]{:S(2)}, u32[]{:S(2)}) collective-permute-start(f32[96,512]{1,0:T(8,128)S(1)} %get-tuple-element.76), channel_id=1, source_target_pairs={{0,7},{1,6},{2,1},{3,0},{4,3},{5,2},{6,5},{7,4},{8,15},{9,14},{10,... | collective-permute-start | bytes 589832 | tf_op jit(solution)/shard_map/ppermute | solution.py:246
  111.5 4.2 %collective-permute-start.24 = (f32[96,512]{1,0:T(8,128)S(1)}, f32[96,512]{1,0:T(8,128)S(1)}, u32[]{:S(2)}, u32[]{:S(2)}) collective-permute-start(f32[96,512]{1,0:T(8,128)S(1)} %get-tuple-element.74), channel_id=1, source_target_pairs={{0,5},{1,4},{2,7},{3,6},{4,1},{5,0},{6,3},{7,2},{8,13},{9,12},{10,... | collective-permute-start | bytes 589832 | tf_op jit(solution)/shard_map/ppermute | solution.py:246
  115.7 3.8 %collective-permute-start.25 = (f32[96,512]{1,0:T(8,128)S(1)}, f32[96,512]{1,0:T(8,128)S(1)}, u32[]{:S(2)}, u32[]{:S(2)}) collective-permute-start(f32[96,512]{1,0:T(8,128)S(1)} %get-tuple-element.73), channel_id=1, source_target_pairs={{0,4},{1,5},{2,6},{3,7},{4,0},{5,1},{6,2},{7,3},{8,12},{9,13},{10,... | collective-permute-start | bytes 589832 | tf_op jit(solution)/shard_map/ppermute | solution.py:246
  119.5 2.8 %collective-permute-done.26 = f32[96,512]{1,0:T(8,128)S(1)} collective-permute-done((f32[96,512]{1,0:T(8,128)S(1)}, f32[96,512]{1,0:T(8,128)S(1)}, u32[]{:S(2)}, u32[]{:S(2)}) %collective-permute-start.26) | collective-permute-done | bytes 196640 | tf_op jit(solution)/shard_map/ppermute | solution.py:246
  122.3 3.5 %collective-permute-done.24 = f32[96,512]{1,0:T(8,128)S(1)} collective-permute-done((f32[96,512]{1,0:T(8,128)S(1)}, f32[96,512]{1,0:T(8,128)S(1)}, u32[]{:S(2)}, u32[]{:S(2)}) %collective-permute-start.24) | collective-permute-done | bytes 196640 | tf_op jit(solution)/shard_map/ppermute | solution.py:246
  125.8 3.9 %collective-permute-done.25 = f32[96,512]{1,0:T(8,128)S(1)} collective-permute-done((f32[96,512]{1,0:T(8,128)S(1)}, f32[96,512]{1,0:T(8,128)S(1)}, u32[]{:S(2)}, u32[]{:S(2)}) %collective-permute-start.25) | collective-permute-done | bytes 196640 | tf_op jit(solution)/shard_map/ppermute | solution.py:246
  129.9 1.5 collective-permute-start.31
  131.4 2.5 %collective-permute-start.32 = (f32[96,512]{1,0:T(8,128)S(1)}, f32[96,512]{1,0:T(8,128)S(1)}, u32[]{:S(2)}, u32[]{:S(2)}) collective-permute-start(f32[96,512]{1,0:T(8,128)S(1)} %fusion.2), channel_id=1, source_target_pairs={{0,4},{1,5},{2,6},{3,7},{4,0},{5,1},{6,2},{7,3},{8,12},{9,13},{10,... | collective-permute-start | bytes 589832 | tf_op jit(solution)/shard_map/ppermute | solution.py:250
  133.9 3.7 %place.1 = f32[3584,512]{1,0:T(8,128)S(1)} custom-call(s32[8]{0:T(128)S(1)} %copy-done.12, f32[896,256]{1,0:T(8,128)} %copy-done.18, f32[896,256]{1,0:T(8,128)} %copy-done.20, f32[896,256]{1,0:T(8,128)} %copy-done.14, f32[896,256]{1,0:T(8,128)} %copy-done.15, f32[896,256]{1,0:T(8,128)} %copy-done.19, f32[896,256]{1,0:T(8,128)} %copy-done.13, ...), custom_call_target="tpu_custom_call" | custom-call | flops 1 | bytes 14680064 | tf_op jit(solution)/shard_map/place/pallas_call | solution.py:145
  139.0 2.9 %collective-permute-start.34 = (f32[96,512]{1,0:T(8,128)S(1)}, f32[96,512]{1,0:T(8,128)S(1)}, u32[]{:S(2)}, u32[]{:S(2)}) collective-permute-start(f32[96,512]{1,0:T(8,128)S(1)} %fusion.2), channel_id=1, source_target_pairs={{0,7},{1,6},{2,1},{3,0},{4,3},{5,2},{6,5},{7,4},{8,15},{9,14},{10,... | collective-permute-start | bytes 589832 | tf_op jit(solution)/shard_map/ppermute | solution.py:250
  141.9 3.2 %collective-permute-start.36 = (f32[96,512]{1,0:T(8,128)S(1)}, f32[96,512]{1,0:T(8,128)S(1)}, u32[]{:S(2)}, u32[]{:S(2)}) collective-permute-start(f32[96,512]{1,0:T(8,128)S(1)} %fusion.2), channel_id=1, source_target_pairs={{0,6},{1,7},{2,0},{3,1},{4,2},{5,3},{6,4},{7,5},{8,14},{9,15},{10,... | collective-permute-start | bytes 589832 | tf_op jit(solution)/shard_map/ppermute | solution.py:250
  145.3 3.5 %collective-permute-done.32 = f32[96,512]{1,0:T(8,128)S(1)} collective-permute-done((f32[96,512]{1,0:T(8,128)S(1)}, f32[96,512]{1,0:T(8,128)S(1)}, u32[]{:S(2)}, u32[]{:S(2)}) %collective-permute-start.32) | collective-permute-done | bytes 196640 | tf_op jit(solution)/shard_map/ppermute | solution.py:250
  150.0 2.9 %collective-permute-done.35 = f32[96,512]{1,0:T(8,128)S(1)} collective-permute-done((f32[96,512]{1,0:T(8,128)S(1)}, f32[96,512]{1,0:T(8,128)S(1)}, u32[]{:S(2)}, u32[]{:S(2)}) %collective-permute-start.35) | collective-permute-done | bytes 196640 | tf_op jit(solution)/shard_map/ppermute | solution.py:250
  153.0 1.5 collective-permute-done.37
  154.5 11.8 %fusion.18 = f32[768,3584]{1,0:T(8,128)} fusion(f32[768,512]{1,0:T(8,128)S(1)} %constant_dynamic-update-slice_fusion, f32[3584,512]{1,0:T(8,128)S(1)} %place.1), kind=kOutput, calls=%fused_computation.80 | convolution fusion | flops 8455716864 | bytes 19922944 | tf_op jit(solution)/shard_map/dot_general | solution.py:252
  (125 shorter events, 18.6 us)
Async XLA Ops:
  0.0 55.2 %copy-start = (f32[28672]{0:T(1024)S(1)}, f32[28672]{0:T(1024)}, u32[]{:S(2)}) copy-start(f32[28672]{0:T(1024)} %param.11) | copy-start | bytes 344068
  1.7 13.0 %collective-permute-start = (f32[448,128]{1,0:T(8,128)S(1)}, f32[448,128]{1,0:T(8,128)S(1)}, u32[]{:S(2)}, u32[]{:S(2)}) collective-permute-start(f32[448,128]{1,0:T(8,128)S(1)} %get-tuple-element.70), channel_id=1, source_target_pairs={{0,16},{8,24},{16,0},{24,8},{32,48},{40,56},{48,32},{56,40},{64,80... | collective-permute-start | bytes 688136 | tf_op jit(solution)/shard_map/ppermute | solution.py:193
  4.9 18.6 %collective-permute-start.1 = (f32[448,128]{1,0:T(8,128)S(1)}, f32[448,128]{1,0:T(8,128)S(1)}, u32[]{:S(2)}, u32[]{:S(2)}) collective-permute-start(f32[448,128]{1,0:T(8,128)S(1)} %get-tuple-element.69), channel_id=1, source_target_pairs={{0,32},{8,40},{16,48},{24,56},{32,64},{40,72},{48,80},{56,88},{64,... | collective-permute-start | bytes 688136 | tf_op jit(solution)/shard_map/ppermute | solution.py:193
  6.9 27.7 %collective-permute-start.2 = (f32[448,128]{1,0:T(8,128)S(1)}, f32[448,128]{1,0:T(8,128)S(1)}, u32[]{:S(2)}, u32[]{:S(2)}) collective-permute-start(f32[448,128]{1,0:T(8,128)S(1)} %get-tuple-element.68), channel_id=1, source_target_pairs={{0,48},{8,56},{16,32},{24,40},{32,80},{40,88},{48,64},{56,72},{64,... | collective-permute-start | bytes 688136 | tf_op jit(solution)/shard_map/ppermute | solution.py:193
  8.7 25.8 %collective-permute-start.3 = (f32[448,128]{1,0:T(8,128)S(1)}, f32[448,128]{1,0:T(8,128)S(1)}, u32[]{:S(2)}, u32[]{:S(2)}) collective-permute-start(f32[448,128]{1,0:T(8,128)S(1)} %get-tuple-element.67), channel_id=1, source_target_pairs={{0,64},{8,72},{16,80},{24,88},{32,96},{40,104},{48,112},{56,120},{... | collective-permute-start | bytes 688136 | tf_op jit(solution)/shard_map/ppermute | solution.py:193
  10.4 24.1 %collective-permute-start.4 = (f32[448,128]{1,0:T(8,128)S(1)}, f32[448,128]{1,0:T(8,128)S(1)}, u32[]{:S(2)}, u32[]{:S(2)}) collective-permute-start(f32[448,128]{1,0:T(8,128)S(1)} %get-tuple-element.66), channel_id=1, source_target_pairs={{0,80},{8,88},{16,64},{24,72},{32,112},{40,120},{48,96},{56,104},{... | collective-permute-start | bytes 688136 | tf_op jit(solution)/shard_map/ppermute | solution.py:193
  14.7 19.8 %collective-permute-start.5 = (f32[448,128]{1,0:T(8,128)S(1)}, f32[448,128]{1,0:T(8,128)S(1)}, u32[]{:S(2)}, u32[]{:S(2)}) collective-permute-start(f32[448,128]{1,0:T(8,128)S(1)} %get-tuple-element.72), channel_id=1, source_target_pairs={{0,96},{8,104},{16,112},{24,120},{32,0},{40,8},{48,16},{56,24},{64... | collective-permute-start | bytes 688136 | tf_op jit(solution)/shard_map/ppermute | solution.py:193
  23.5 11.0 %collective-permute-start.6 = (f32[448,128]{1,0:T(8,128)S(1)}, f32[448,128]{1,0:T(8,128)S(1)}, u32[]{:S(2)}, u32[]{:S(2)}) collective-permute-start(f32[448,128]{1,0:T(8,128)S(1)} %get-tuple-element.65), channel_id=1, source_target_pairs={{0,112},{8,120},{16,96},{24,104},{32,16},{40,24},{48,0},{56,8},{64... | collective-permute-start | bytes 688136 | tf_op jit(solution)/shard_map/ppermute | solution.py:193
  23.6 6.2 %copy-start.10 = (s32[8]{0:T(128)}, s32[8]{0:T(128)S(1)}, u32[]{:S(2)}) copy-start(s32[8]{0:T(128)S(1)} %pad_add_fusion.1.at_ref) | copy-start | bytes 100
  23.6 10.8 %copy-start.23 = (s32[4]{0:T(128)S(1)}, s32[4]{0:T(128)}, u32[]{:S(2)}) copy-start(s32[4]{0:T(128)} %param.9) | copy-start | bytes 52
  34.5 10.3 %copy-start.8 = (s32[7]{0:T(128)}, s32[7]{0:T(128)S(1)}, u32[]{:S(2)}) copy-start(s32[7]{0:T(128)S(1)} %pad_add_fusion.at_ref) | copy-start | bytes 88
  35.4 1.9 %collective-permute-start.7 = (f32[2,448,128]{2,1,0:T(8,128)S(1)}, f32[2,448,128]{2,1,0:T(8,128)S(1)}, u32[]{:S(2)}, u32[]{:S(2)}) collective-permute-start(f32[2,448,128]{2,1,0:T(8,128)S(1)} %get-tuple-element.47), channel_id=1, source_target_pairs={{0,8},{8,0},{16,24},{24,16},{32,40},{40,32},{48,56},{56,48},{64,72... | collective-permute-start | bytes 1376264 | tf_op jit(solution)/shard_map/ppermute | solution.py:199
  37.9 22.3 %collective-permute-start.8 = (f32[448,128]{1,0:T(8,128)S(1)}, f32[448,128]{1,0:T(8,128)S(1)}, u32[]{:S(2)}, u32[]{:S(2)}) collective-permute-start(f32[448,128]{1,0:T(8,128)S(1)} %get-tuple-element.48.mine_ref), channel_id=1, source_target_pairs={{0,16},{8,24},{16,0},{24,8},{32,48},{40,56},{48,32},{56,40},{64,80... | collective-permute-start | bytes 688136 | tf_op jit(solution)/shard_map/ppermute | solution.py:202
  44.8 20.2 %collective-permute-start.13 = (f32[448,128]{1,0:T(8,128)S(1)}, f32[448,128]{1,0:T(8,128)}, u32[]{:S(2)}, u32[]{:S(2)}) collective-permute-start(f32[448,128]{1,0:T(8,128)S(1)} %get-tuple-element.52.mine_ref), channel_id=1, source_target_pairs={{0,16},{8,24},{16,0},{24,8},{32,48},{40,56},{48,32},{56,40},{64,80... | collective-permute-start | bytes 688136 | tf_op jit(solution)/shard_map/ppermute | solution.py:202
  61.5 5.4 %copy-start.7 = (f32[768,896]{1,0:T(8,128)S(1)}, f32[768,896]{1,0:T(8,128)}, u32[]{:S(2)}) copy-start(f32[768,896]{1,0:T(8,128)} %copy-done.6) | copy-start | bytes 8257540
  61.5 10.4 %collective-permute-start.9 = (f32[896,128]{1,0:T(8,128)S(1)}, f32[896,128]{1,0:T(8,128)S(1)}, u32[]{:S(2)}, u32[]{:S(2)}) collective-permute-start(f32[896,128]{1,0:T(8,128)S(1)} %join.2), channel_id=1, source_target_pairs={{0,32},{8,104},{16,48},{24,120},{32,64},{40,8},{48,80},{56,24},{64... | collective-permute-start | bytes 1376264 | tf_op jit(solution)/shard_map/ppermute | solution.py:230
  62.8 9.1 %collective-permute-start.10 = (f32[896,128]{1,0:T(8,128)S(1)}, f32[896,128]{1,0:T(8,128)S(1)}, u32[]{:S(2)}, u32[]{:S(2)}) collective-permute-start(f32[896,128]{1,0:T(8,128)S(1)} %join.2), channel_id=1, source_target_pairs={{0,8},{8,0},{16,24},{24,16},{32,40},{40,32},{48,56},{56,48},{64,72... | collective-permute-start | bytes 1376264 | tf_op jit(solution)/shard_map/ppermute | solution.py:231
  66.0 7.6 %collective-permute-start.14 = (f32[896,128]{1,0:T(8,128)S(1)}, f32[896,128]{1,0:T(8,128)S(1)}, u32[]{:S(2)}, u32[]{:S(2)}) collective-permute-start(f32[896,128]{1,0:T(8,128)S(1)} %join.3), channel_id=1, source_target_pairs={{0,8},{8,0},{16,24},{24,16},{32,40},{40,32},{48,56},{56,48},{64,72... | collective-permute-start | bytes 1376264 | tf_op jit(solution)/shard_map/ppermute | solution.py:231
  66.1 10.7 %collective-permute-start.17 = (f32[896,128]{1,0:T(8,128)S(1)}, f32[896,128]{1,0:T(8,128)S(1)}, u32[]{:S(2)}, u32[]{:S(2)}) collective-permute-start(f32[896,128]{1,0:T(8,128)S(1)} %join.3), channel_id=1, source_target_pairs={{0,32},{8,104},{16,48},{24,120},{32,64},{40,8},{48,80},{56,24},{64... | collective-permute-start | bytes 1376264 | tf_op jit(solution)/shard_map/ppermute | solution.py:230
  71.9 9.8 %collective-permute-start.11 = (f32[896,128]{1,0:T(8,128)S(1)}, f32[896,128]{1,0:T(8,128)S(1)}, u32[]{:S(2)}, u32[]{:S(2)}) collective-permute-start(f32[896,128]{1,0:T(8,128)S(1)} %collective-permute-done.9), channel_id=1, source_target_pairs={{0,32},{8,104},{16,48},{24,120},{32,64},{40,8},{48,80},{56,24},{64... | collective-permute-start | bytes 1376264 | tf_op jit(solution)/shard_map/ppermute | solution.py:230
  71.9 9.8 %collective-permute-start.12 = (f32[896,128]{1,0:T(8,128)S(1)}, f32[896,128]{1,0:T(8,128)S(1)}, u32[]{:S(2)}, u32[]{:S(2)}) collective-permute-start(f32[896,128]{1,0:T(8,128)S(1)} %collective-permute-done.9), channel_id=1, source_target_pairs={{0,8},{8,0},{16,24},{24,16},{32,40},{40,32},{48,56},{56,48},{64,72... | collective-permute-start | bytes 1376264 | tf_op jit(solution)/shard_map/ppermute | solution.py:231
  73.6 3.5 %copy-start.3 = (f32[768,896]{1,0:T(8,128)S(1)}, f32[768,896]{1,0:T(8,128)}, u32[]{:S(2)}) copy-start(f32[768,896]{1,0:T(8,128)} %copy-done.2) | copy-start | bytes 8257540
  76.8 6.6 %collective-permute-start.18 = (f32[896,128]{1,0:T(8,128)S(1)}, f32[896,128]{1,0:T(8,128)S(1)}, u32[]{:S(2)}, u32[]{:S(2)}) collective-permute-start(f32[896,128]{1,0:T(8,128)S(1)} %collective-permute-done.17), channel_id=1, source_target_pairs={{0,8},{8,0},{16,24},{24,16},{32,40},{40,32},{48,56},{56,48},{64,72... | collective-permute-start | bytes 1376264 | tf_op jit(solution)/shard_map/ppermute | solution.py:231
  76.8 9.9 %collective-permute-start.19 = (f32[896,128]{1,0:T(8,128)S(1)}, f32[896,128]{1,0:T(8,128)S(1)}, u32[]{:S(2)}, u32[]{:S(2)}) collective-permute-start(f32[896,128]{1,0:T(8,128)S(1)} %collective-permute-done.17), channel_id=1, source_target_pairs={{0,32},{8,104},{16,48},{24,120},{32,64},{40,8},{48,80},{56,24},{64... | collective-permute-start | bytes 1376264 | tf_op jit(solution)/shard_map/ppermute | solution.py:230
  81.7 10.0 %collective-permute-start.15 = (f32[896,128]{1,0:T(8,128)S(1)}, f32[896,128]{1,0:T(8,128)S(1)}, u32[]{:S(2)}, u32[]{:S(2)}) collective-permute-start(f32[896,128]{1,0:T(8,128)S(1)} %collective-permute-done.11), channel_id=1, source_target_pairs={{0,32},{8,104},{16,48},{24,120},{32,64},{40,8},{48,80},{56,24},{64... | collective-permute-start | bytes 1376264 | tf_op jit(solution)/shard_map/ppermute | solution.py:230
  81.7 10.0 %collective-permute-start.16 = (f32[896,128]{1,0:T(8,128)S(1)}, f32[896,128]{1,0:T(8,128)S(1)}, u32[]{:S(2)}, u32[]{:S(2)}) collective-permute-start(f32[896,128]{1,0:T(8,128)S(1)} %collective-permute-done.11), channel_id=1, source_target_pairs={{0,8},{8,0},{16,24},{24,16},{32,40},{40,32},{48,56},{56,48},{64,72... | collective-permute-start | bytes 1376264 | tf_op jit(solution)/shard_map/ppermute | solution.py:231
  83.4 5.1 %copy-start.13 = (f32[896,256]{1,0:T(8,128)}, f32[896,256]{1,0:T(8,128)S(1)}, u32[]{:S(2)}) copy-start(f32[896,256]{1,0:T(8,128)S(1)} %pad_maximum_fusion.3.refs_5_) | copy-start | bytes 2752516
  86.8 9.8 %collective-permute-start.20 = (f32[896,128]{1,0:T(8,128)S(1)}, f32[896,128]{1,0:T(8,128)S(1)}, u32[]{:S(2)}, u32[]{:S(2)}) collective-permute-start(f32[896,128]{1,0:T(8,128)S(1)} %collective-permute-done.19), channel_id=1, source_target_pairs={{0,32},{8,104},{16,48},{24,120},{32,64},{40,8},{48,80},{56,24},{64... | collective-permute-start | bytes 1376264 | tf_op jit(solution)/shard_map/ppermute | solution.py:230
  86.9 9.9 %copy-start.14 = (f32[896,256]{1,0:T(8,128)}, f32[896,256]{1,0:T(8,128)S(1)}, u32[]{:S(2)}) copy-start(f32[896,256]{1,0:T(8,128)S(1)} %pad_maximum_fusion.4.refs_2_) | copy-start | bytes 2752516
  87.0 13.3 %collective-permute-start.21 = (f32[896,128]{1,0:T(8,128)S(1)}, f32[896,128]{1,0:T(8,128)S(1)}, u32[]{:S(2)}, u32[]{:S(2)}) collective-permute-start(f32[896,128]{1,0:T(8,128)S(1)} %collective-permute-done.19), channel_id=1, source_target_pairs={{0,8},{8,0},{16,24},{24,16},{32,40},{40,32},{48,56},{56,48},{64,72... | collective-permute-start | bytes 1376264 | tf_op jit(solution)/shard_map/ppermute | solution.py:231
  96.7 5.1 %collective-permute-start.22 = (f32[896,128]{1,0:T(8,128)S(1)}, f32[896,128]{1,0:T(8,128)S(1)}, u32[]{:S(2)}, u32[]{:S(2)}) collective-permute-start(f32[896,128]{1,0:T(8,128)S(1)} %collective-permute-done.15), channel_id=1, source_target_pairs={{0,8},{8,0},{16,24},{24,16},{32,40},{40,32},{48,56},{56,48},{64,72... | collective-permute-start | bytes 1376264 | tf_op jit(solution)/shard_map/ppermute | solution.py:231
  98.2 3.5 %collective-permute-start.23 = (f32[896,128]{1,0:T(8,128)S(1)}, f32[896,128]{1,0:T(8,128)S(1)}, u32[]{:S(2)}, u32[]{:S(2)}) collective-permute-start(f32[896,128]{1,0:T(8,128)S(1)} %collective-permute-done.20), channel_id=1, source_target_pairs={{0,8},{8,0},{16,24},{24,16},{32,40},{40,32},{48,56},{56,48},{64,72... | collective-permute-start | bytes 1376264 | tf_op jit(solution)/shard_map/ppermute | solution.py:231
  103.3 8.1 %collective-permute-start.30 = (f32[96,512]{1,0:T(8,128)S(1)}, f32[96,512]{1,0:T(8,128)S(1)}, u32[]{:S(2)}, u32[]{:S(2)}) collective-permute-start(f32[96,512]{1,0:T(8,128)S(1)} %fusion.9), channel_id=1, source_target_pairs={{0,1},{1,0},{2,3},{3,2},{4,5},{5,4},{6,7},{7,6},{8,9},{9,8},{10,11... | collective-permute-start | bytes 589832 | tf_op jit(solution)/shard_map/ppermute | solution.py:246
  105.5 10.2 %collective-permute-start.29 = (f32[96,512]{1,0:T(8,128)S(1)}, f32[96,512]{1,0:T(8,128)S(1)}, u32[]{:S(2)}, u32[]{:S(2)}) collective-permute-start(f32[96,512]{1,0:T(8,128)S(1)} %get-tuple-element.78), channel_id=1, source_target_pairs={{0,6},{1,7},{2,0},{3,1},{4,2},{5,3},{6,4},{7,5},{8,14},{9,15},{10,... | collective-permute-start | bytes 589832 | tf_op jit(solution)/shard_map/ppermute | solution.py:246
  108.5 11.0 %collective-permute-start.28 = (f32[96,512]{1,0:T(8,128)S(1)}, f32[96,512]{1,0:T(8,128)S(1)}, u32[]{:S(2)}, u32[]{:S(2)}) collective-permute-start(f32[96,512]{1,0:T(8,128)S(1)} %get-tuple-element.77), channel_id=1, source_target_pairs={{0,2},{1,3},{2,4},{3,5},{4,6},{5,7},{6,0},{7,1},{8,10},{9,11},{10,... | collective-permute-start | bytes 589832 | tf_op jit(solution)/shard_map/ppermute | solution.py:246
  108.5 11.0 %collective-permute-start.27 = (f32[96,512]{1,0:T(8,128)S(1)}, f32[96,512]{1,0:T(8,128)S(1)}, u32[]{:S(2)}, u32[]{:S(2)}) collective-permute-start(f32[96,512]{1,0:T(8,128)S(1)} %get-tuple-element.76), channel_id=1, source_target_pairs={{0,7},{1,6},{2,1},{3,0},{4,3},{5,2},{6,5},{7,4},{8,15},{9,14},{10,... | collective-permute-start | bytes 589832 | tf_op jit(solution)/shard_map/ppermute | solution.py:246
  111.3 10.9 %collective-permute-start.26 = (f32[96,512]{1,0:T(8,128)S(1)}, f32[96,512]{1,0:T(8,128)S(1)}, u32[]{:S(2)}, u32[]{:S(2)}) collective-permute-start(f32[96,512]{1,0:T(8,128)S(1)} %get-tuple-element.75), channel_id=1, source_target_pairs={{0,3},{1,2},{2,5},{3,4},{4,7},{5,6},{6,1},{7,0},{8,11},{9,10},{10,... | collective-permute-start | bytes 589832 | tf_op jit(solution)/shard_map/ppermute | solution.py:246
  111.5 14.3 %collective-permute-start.24 = (f32[96,512]{1,0:T(8,128)S(1)}, f32[96,512]{1,0:T(8,128)S(1)}, u32[]{:S(2)}, u32[]{:S(2)}) collective-permute-start(f32[96,512]{1,0:T(8,128)S(1)} %get-tuple-element.74), channel_id=1, source_target_pairs={{0,5},{1,4},{2,7},{3,6},{4,1},{5,0},{6,3},{7,2},{8,13},{9,12},{10,... | collective-permute-start | bytes 589832 | tf_op jit(solution)/shard_map/ppermute | solution.py:246
  115.7 14.0 %collective-permute-start.25 = (f32[96,512]{1,0:T(8,128)S(1)}, f32[96,512]{1,0:T(8,128)S(1)}, u32[]{:S(2)}, u32[]{:S(2)}) collective-permute-start(f32[96,512]{1,0:T(8,128)S(1)} %get-tuple-element.73), channel_id=1, source_target_pairs={{0,4},{1,5},{2,6},{3,7},{4,0},{5,1},{6,2},{7,3},{8,12},{9,13},{10,... | collective-permute-start | bytes 589832 | tf_op jit(solution)/shard_map/ppermute | solution.py:246
  119.5 14.4 %copy-start.12 = (s32[8]{0:T(128)S(1)}, s32[8]{0:T(128)}, u32[]{:S(2)}) copy-start(s32[8]{0:T(128)} %copy-done.10) | copy-start | bytes 100
  129.9 12.0 %collective-permute-start.31 = (f32[96,512]{1,0:T(8,128)S(1)}, f32[96,512]{1,0:T(8,128)S(1)}, u32[]{:S(2)}, u32[]{:S(2)}) collective-permute-start(f32[96,512]{1,0:T(8,128)S(1)} %fusion.2), channel_id=1, source_target_pairs={{0,5},{1,4},{2,7},{3,6},{4,1},{5,0},{6,3},{7,2},{8,13},{9,12},{10,... | collective-permute-start | bytes 589832 | tf_op jit(solution)/shard_map/ppermute | solution.py:250
  131.4 17.4 %collective-permute-start.32 = (f32[96,512]{1,0:T(8,128)S(1)}, f32[96,512]{1,0:T(8,128)S(1)}, u32[]{:S(2)}, u32[]{:S(2)}) collective-permute-start(f32[96,512]{1,0:T(8,128)S(1)} %fusion.2), channel_id=1, source_target_pairs={{0,4},{1,5},{2,6},{3,7},{4,0},{5,1},{6,2},{7,3},{8,12},{9,13},{10,... | collective-permute-start | bytes 589832 | tf_op jit(solution)/shard_map/ppermute | solution.py:250
  137.7 11.7 %collective-permute-start.33 = (f32[96,512]{1,0:T(8,128)S(1)}, f32[96,512]{1,0:T(8,128)S(1)}, u32[]{:S(2)}, u32[]{:S(2)}) collective-permute-start(f32[96,512]{1,0:T(8,128)S(1)} %fusion.2), channel_id=1, source_target_pairs={{0,3},{1,2},{2,5},{3,4},{4,7},{5,6},{6,1},{7,0},{8,11},{9,10},{10,... | collective-permute-start | bytes 589832 | tf_op jit(solution)/shard_map/ppermute | solution.py:250
  139.0 11.0 %collective-permute-start.34 = (f32[96,512]{1,0:T(8,128)S(1)}, f32[96,512]{1,0:T(8,128)S(1)}, u32[]{:S(2)}, u32[]{:S(2)}) collective-permute-start(f32[96,512]{1,0:T(8,128)S(1)} %fusion.2), channel_id=1, source_target_pairs={{0,7},{1,6},{2,1},{3,0},{4,3},{5,2},{6,5},{7,4},{8,15},{9,14},{10,... | collective-permute-start | bytes 589832 | tf_op jit(solution)/shard_map/ppermute | solution.py:250
  141.9 11.1 %collective-permute-start.35 = (f32[96,512]{1,0:T(8,128)S(1)}, f32[96,512]{1,0:T(8,128)S(1)}, u32[]{:S(2)}, u32[]{:S(2)}) collective-permute-start(f32[96,512]{1,0:T(8,128)S(1)} %fusion.2), channel_id=1, source_target_pairs={{0,2},{1,3},{2,4},{3,5},{4,6},{5,7},{6,0},{7,1},{8,10},{9,11},{10,... | collective-permute-start | bytes 589832 | tf_op jit(solution)/shard_map/ppermute | solution.py:250
  141.9 11.1 %collective-permute-start.36 = (f32[96,512]{1,0:T(8,128)S(1)}, f32[96,512]{1,0:T(8,128)S(1)}, u32[]{:S(2)}, u32[]{:S(2)}) collective-permute-start(f32[96,512]{1,0:T(8,128)S(1)} %fusion.2), channel_id=1, source_target_pairs={{0,6},{1,7},{2,0},{3,1},{4,2},{5,3},{6,4},{7,5},{8,14},{9,15},{10,... | collective-permute-start | bytes 589832 | tf_op jit(solution)/shard_map/ppermute | solution.py:250
  148.8 5.7 %collective-permute-start.37 = (f32[96,512]{1,0:T(8,128)S(1)}, f32[96,512]{1,0:T(8,128)S(1)}, u32[]{:S(2)}, u32[]{:S(2)}) collective-permute-start(f32[96,512]{1,0:T(8,128)S(1)} %fusion.2), channel_id=1, source_target_pairs={{0,1},{1,0},{2,3},{3,2},{4,5},{5,4},{6,7},{7,6},{8,9},{9,8},{10,11... | collective-permute-start | bytes 589832 | tf_op jit(solution)/shard_map/ppermute | solution.py:250
  154.5 11.8 %copy-start.1 = (f32[28672]{0:T(1024)S(1)}, f32[28672]{0:T(1024)}, u32[]{:S(2)}) copy-start(f32[28672]{0:T(1024)} %param.11) | copy-start | bytes 344068
  (14 other events, 19.7 us)
